TPU v7x, 128 devices: a whole 4x4x4 slice. The times are simulated.
128 devices in a mesh: row: 4 (over x), col: 32 (over z, y, core).
Axes of the slice: x: 4, y: 4, z: 4, core: 2. Of those that a mesh axis runs over, the one named last changes fastest.
Arguments:
- a_tiles: bfloat16 [12288, 3200], P(('row', 'col')), may hold values from -4 to 4
- a_owner: int32 [12288], P(('row', 'col')), may hold values from 0 to 127, as said below
- a_offset: int32 [12288, 2], P(('row', 'col')), may hold values from 0 to 560, as said below
- b_tiles: bfloat16 [12288, 3200], P(('row', 'col')), may hold values from -6 to 6
- b_owner: int32 [12288], P(('row', 'col')), may hold values from 0 to 127, as said below
- b_offset: int32 [12288, 2], P(('row', 'col')), may hold values from 0 to 560, as said below
- patch_valid: int32 [48, 512], P('row', 'col'), may hold values 0 or 1
Outputs:
- flow_field: float32 [2, 48, 512], P(None, 'row', 'col')
- mesh_field: float32 [2, 48, 512], P(None, 'row', 'col')
Inputs may be any that keep to these rules, and one draw needn't show every extreme that they name: `a_owner`: each region owner receives exactly 96 first-section tiles, one for every tile position of its region; a device sends either no tile or exactly 1 tiles to one owner. `a_offset`: row offsets are multiples of 40 below 480, column offsets multiples of 80 below 640; each owner's tiles cover its region exactly once. `b_owner`: each region owner receives exactly 96 next-section tiles, one for every tile position of its region; a device sends either no tile or exactly 1 tiles to one owner. `b_offset`: row offsets are multiples of 40 below 480, column offsets multiples of 80 below 640; each owner's tiles cover its region exactly once.
All inputs are finite; a program needn't handle non-finite values. No bound on the sum of `patch_valid` on one device may be relied on, other than what follows from the above.
Results may differ from a plain program's by a relative error of at most 0.004.
Values may be sent and summed in bfloat16 or wider, within the bound.
No kernel may reach another device: no remote copies, remote signals or barrier semaphores. Data moves between devices by JAX's collectives and lax.ppermute only.
A program may use at most 64 MiB of HBM per device.

v0:
```python
import math

import jax
import jax.numpy as jnp
from jax import lax
from jax.sharding import PartitionSpec as P

PATCH = 160
STRIDE = 40
TY = 12
TX = 8
SWEEPS = 3
MARGIN = 60


stiffness = 1.0
tiny = 1e-06


def extended_2(block, sides, width):
    for axis, dim in sides:
        count = lax.axis_size(axis)
        forward = [(i, i + 1) for i in range(count - 1)]
        backward = [(target, source) for source, target in forward]
        low = lax.ppermute(
            lax.slice_in_dim(block, block.shape[dim] - width, None, axis=dim), axis, forward
        )
        high = lax.ppermute(lax.slice_in_dim(block, 0, width, axis=dim), axis, backward)
        block = jnp.concatenate([low, block, high], axis=dim)
    return block


def dft_tables():
    freq_index = jnp.arange(PATCH, dtype=jnp.int32)
    phase = (freq_index[:, None] * freq_index[None, :] % PATCH).astype(jnp.float32) * (
        2.0 * math.pi / PATCH
    )
    return (jnp.cos(phase).astype(jnp.bfloat16), jnp.sin(phase).astype(jnp.bfloat16))


def forward_rest(first_segment, cosine_table, sine_table):
    halves = first_segment.reshape(first_segment.shape[0], PATCH, 2, PATCH)
    left_real = jnp.stack([cosine_table, -sine_table])
    left_imag = jnp.stack([-sine_table, -cosine_table])
    spec_real = jnp.einsum("hky,nyhj->nkj", left_real, halves, preferred_element_type=jnp.float32)
    spec_imag = jnp.einsum("hky,nyhj->nkj", left_imag, halves, preferred_element_type=jnp.float32)
    return (spec_real, spec_imag)


def inverse(cross_real, cross_imag, cosine_table, sine_table):
    stacked = jnp.stack([cross_real, cross_imag], axis=2)
    right_u = jnp.stack([cosine_table, -sine_table])
    right_v = jnp.stack([sine_table, cosine_table])
    inverse_u = jnp.einsum(
        "nyhx,hxk->nyk", stacked, right_u, preferred_element_type=jnp.float32
    ).astype(jnp.bfloat16)
    inverse_v = jnp.einsum(
        "nyhx,hxk->nyk", stacked, right_v, preferred_element_type=jnp.float32
    ).astype(jnp.bfloat16)
    stacked_uv = jnp.stack([inverse_u, inverse_v], axis=2)
    left_real = jnp.stack([cosine_table, -sine_table])
    return jnp.einsum("hky,nyhj->nkj", left_real, stacked_uv, preferred_element_type=jnp.float32)


def correlate(first_a, first_b, norm_a, norm_b, cosine_table, sine_table):
    real_a, imag_a = forward_rest(first_a, cosine_table, sine_table)
    real_b, imag_b = forward_rest(first_b, cosine_table, sine_table)
    inv_norms = (1.0 / (norm_a * norm_b))[:, None, None]
    cross_real = ((real_a * real_b + imag_a * imag_b) * inv_norms).astype(jnp.bfloat16)
    cross_imag = ((real_a * imag_b - imag_a * real_b) * inv_norms).astype(jnp.bfloat16)
    correlation = inverse(cross_real, cross_imag, cosine_table, sine_table) / (PATCH * PATCH)
    weight = correlation * correlation
    weight_sum = jnp.sum(weight, axis=(1, 2))
    freq_index = jnp.arange(PATCH, dtype=jnp.int32)
    shift_units = jnp.where(freq_index < PATCH // 2, freq_index, freq_index - PATCH).astype(
        jnp.float32
    ) * (16.0 / PATCH)
    flow_y = jnp.sum(weight * shift_units[None, :, None], axis=(1, 2)) / (1.0 + weight_sum)
    flow_x = jnp.sum(weight * shift_units[None, None, :], axis=(1, 2)) / (1.0 + weight_sum)
    return (flow_y, flow_x, weight_sum / (1.0 + weight_sum))


def outgoing(tiles, tile_owner, tile_offset, slot_count, capacity, tile_h, tile_w):
    tile_count = tiles.shape[0]
    tile_index = jnp.arange(tile_count, dtype=jnp.int32)
    matches = (tile_owner[:, None] == tile_owner[None, :]) & (
        tile_index[:, None] > tile_index[None, :]
    )
    earlier_count = jnp.sum(matches.astype(jnp.int32), axis=1)
    target = tile_owner * capacity + earlier_count
    select = (jnp.arange(slot_count, dtype=jnp.int32)[:, None] == target[None, :]).astype(
        jnp.bfloat16
    )
    position = tile_offset[:, 0] // tile_h * TX + tile_offset[:, 1] // tile_w + 1
    sent_tiles = jnp.dot(select, tiles, preferred_element_type=jnp.float32).astype(jnp.bfloat16)
    slot_code = jnp.dot(
        select, position.astype(jnp.bfloat16)[:, None], preferred_element_type=jnp.float32
    ).astype(jnp.bfloat16)
    return (sent_tiles, slot_code)


def incoming(received, slot_code, tile_count, tile_h, tile_w):
    wanted = jnp.arange(1, tile_count + 1, dtype=jnp.int32).astype(jnp.float32)
    select = (slot_code[:, 0].astype(jnp.float32)[None, :] == wanted[:, None]).astype(jnp.bfloat16)
    blocks = jnp.dot(select, received, preferred_element_type=jnp.float32).astype(jnp.bfloat16)
    return (
        blocks.reshape(TY, TX, tile_h, tile_w)
        .transpose(0, 2, 1, 3)
        .reshape(TY * tile_h, TX * tile_w)
    )


def route(send_a, code_a, send_b, code_b, row_count, col_count, capacity):
    devices = row_count * col_count
    tile_size = send_a.shape[1]
    code_width = code_a.shape[1]
    recv_a, got_a, recv_b, got_b = (
        lax.all_to_all(
            send_a.reshape(devices, capacity, tile_size),
            ("row", "col"),
            split_axis=0,
            concat_axis=0,
            tiled=True,
        ),
        lax.all_to_all(
            code_a.reshape(devices, capacity, code_width),
            ("row", "col"),
            split_axis=0,
            concat_axis=0,
            tiled=True,
        ),
        lax.all_to_all(
            send_b.reshape(devices, capacity, tile_size),
            ("row", "col"),
            split_axis=0,
            concat_axis=0,
            tiled=True,
        ),
        lax.all_to_all(
            code_b.reshape(devices, capacity, code_width),
            ("row", "col"),
            split_axis=0,
            concat_axis=0,
            tiled=True,
        ),
    )
    slot_count = devices * capacity
    return (
        recv_a.reshape(slot_count, tile_size),
        got_a.reshape(slot_count, code_width),
        recv_b.reshape(slot_count, tile_size),
        got_b.reshape(slot_count, code_width),
    )


def per_device(a_tiles, a_owner, a_offset, b_tiles, b_owner, b_offset, patch_valid):
    grid_rows, grid_cols = patch_valid.shape
    tile_h = grid_rows * STRIDE // TY
    tile_w = grid_cols * STRIDE // TX
    tile_count = a_tiles.shape[0]
    row_count = lax.axis_size("row")
    col_count = lax.axis_size("col")
    devices = row_count * col_count
    capacity = 4 * tile_count // (3 * devices)
    slot_count = devices * capacity
    send_a, code_a = outgoing(a_tiles, a_owner, a_offset, slot_count, capacity, tile_h, tile_w)
    send_b, code_b = outgoing(b_tiles, b_owner, b_offset, slot_count, capacity, tile_h, tile_w)
    recv_a, got_a, recv_b, got_b = route(
        send_a, code_a, send_b, code_b, row_count, col_count, capacity
    )
    canvas_a = incoming(recv_a, got_a, tile_count, tile_h, tile_w)
    canvas_b = incoming(recv_b, got_b, tile_count, tile_h, tile_w)
    images = jnp.stack([canvas_a, canvas_b])
    padded = extended_2(images, (("row", 1), ("col", 2)), MARGIN)
    cosine_table, sine_table = dft_tables()
    column_table = jnp.concatenate([cosine_table, sine_table], axis=1).reshape(4, STRIDE, 2 * PATCH)
    cell_count = grid_cols + 3

    def one_row(grid_row):
        band_strip = lax.dynamic_slice(
            padded, (grid_row * 0, grid_row * STRIDE, grid_row * 0), (2, PATCH, cell_count * STRIDE)
        )
        cells = band_strip.reshape(2, PATCH, cell_count, STRIDE)
        first_total = jnp.zeros((2, grid_cols, PATCH, 2 * PATCH), jnp.float32)
        square_total = jnp.zeros((2, grid_cols), jnp.float32)
        for column_step in range(4):
            part_cells = cells[:, :, column_step : column_step + grid_cols, :]
            first_total = first_total + jnp.einsum(
                "ayjs,sk->ajyk",
                part_cells,
                column_table[column_step],
                preferred_element_type=jnp.float32,
            )
            values = part_cells.astype(jnp.float32)
            square_total = square_total + jnp.sum(values * values, axis=(1, 3))
        first_segment = first_total.astype(jnp.bfloat16)
        norms = PATCH * jnp.sqrt(square_total / (PATCH * PATCH) + tiny)
        return correlate(
            first_segment[0], first_segment[1], norms[0], norms[1], cosine_table, sine_table
        )

    flow_y, flow_x, confidence = lax.map(one_row, jnp.arange(grid_rows, dtype=jnp.int32))
    flow_field = jnp.stack([flow_y, flow_x])
    valid_float = patch_valid.astype(jnp.float32)
    strength = valid_float * confidence
    data_pull = strength[None] * flow_field
    initial = valid_float[None] * flow_field
    mesh_field = initial
    for sweep_index in range(SWEEPS):
        extended = extended_2(mesh_field, (("row", 1), ("col", 2)), 1)
        beside_all = (
            extended[:, :-2, 1:-1]
            + extended[:, 2:, 1:-1]
            + extended[:, 1:-1, :-2]
            + extended[:, 1:-1, 2:]
        )
        mesh_field = (data_pull + stiffness * beside_all) / (strength[None] + 4.0 * stiffness)
    return (flow_field, mesh_field)


def solution(mesh):
    in_specs = (
        P(("row", "col"), None),
        P(("row", "col")),
        P(("row", "col"), None),
        P(("row", "col"), None),
        P(("row", "col")),
        P(("row", "col"), None),
        P("row", "col"),
    )
    out_specs = (P(None, "row", "col"), P(None, "row", "col"))
    return jax.shard_map(
        per_device, mesh=mesh, in_specs=in_specs, out_specs=out_specs, check_vma=False
    )
```

profile of v0, /device:TPU:27, one launch (start us, length us, event | category | flops | bytes accessed | tf_op | source)
XLA Modules:
  0.0 831.9 jit_solution(16298543046438109463)
XLA Ops:
  3.9 10.5 %all-to-all-start.2 = ((bf16[128,1,1]{2,1,0:T(2,128)(2,1)}), bf16[128,1,1]{2,1,0:T(2,128)(2,1)S(1)}, u32[]{:S(2)}, u32[]{:S(2)}) async-start(bf16[128,1,1]{2,1,0:T(2,128)(2,1)} %copy.103), calls=%async_computation.2 | async-start | bytes 131072 | tf_op jit(solution)/shard_map/all_to_all | solution.py:139
  17.7 3.9 all-to-all-done.2
  21.6 7.0 all-to-all-start
  35.7 7.0 all-to-all-start.3
  46.2 11.0 %all-to-all-done.3 = bf16[128,2,1600]{2,1,0:T(2,128)(2,1)S(1)} async-done(((bf16[128,2,1600]{2,1,0:T(2,128)(2,1)}), bf16[128,2,1600]{2,1,0:T(2,128)(2,1)S(1)}, u32[]{:S(2)}, u32[]{:S(2)}) %all-to-all-start.3) | async-done | bytes 819232 | tf_op jit(solution)/shard_map/all_to_all | solution.py:132
  57.2 8.3 all-to-all-start.1
  71.9 7.7 all-to-all-done.1
  79.5 5.5 reshape.267
  96.5 5.5 collective-permute-start.2
  105.8 6.6 collective-permute-done.3
  115.1 663.7 %while.16 = (s32[]{:T(128)}, f32[12,16]{1,0:T(8,128)S(1)}, f32[12,16]{1,0:T(8,128)S(1)}, f32[12,16]{1,0:T(8,128)}, s32[12]{0:T(128)S(1)}, /*index=5*/bf16[2,600,...) while((s32[]{:T(128)}, f32[12,16]{1,0:T(8,128)S(1)}, ...), condition=%wide.region_10.11_spmd, body=%wide.region_2.10_spmd.sunk | while | flops 2378548224 | bytes 130922496 | solution.py:202
  134.1 4.2 fusion.207
  138.3 6.4 fusion.208
  144.7 4.4 fusion.209
  149.1 3.7 copy.157
  157.6 3.7 copy.158
  189.3 4.2 fusion.207
  193.6 6.4 fusion.208
  200.0 4.4 fusion.209
  204.4 3.7 copy.157
  212.9 3.7 copy.158
  244.6 4.2 fusion.207
  248.9 6.4 fusion.208
  255.3 4.4 fusion.209
  259.7 3.7 copy.157
  268.2 3.7 copy.158
  299.9 4.2 fusion.207
  304.1 6.4 fusion.208
  310.6 4.4 fusion.209
  315.0 3.7 copy.157
  323.5 3.7 copy.158
  355.2 4.2 fusion.207
  359.4 6.4 fusion.208
  365.9 4.4 fusion.209
  370.3 3.7 copy.157
  378.8 3.7 copy.158
  410.5 4.2 fusion.207
  414.7 6.4 fusion.208
  421.2 4.4 fusion.209
  425.6 3.7 copy.157
  434.1 3.7 copy.158
  465.8 4.2 fusion.207
  470.0 6.4 fusion.208
  476.4 4.4 fusion.209
  521.1 4.2 fusion.207
  525.3 6.4 fusion.208
  531.7 4.4 fusion.209
  544.7 3.7 copy.158
  576.4 4.2 fusion.207
  580.6 6.4 fusion.208
  587.0 4.4 fusion.209
  631.7 4.2 fusion.207
  635.9 6.4 fusion.208
  642.3 4.4 fusion.209
  687.0 4.2 fusion.207
  691.2 6.4 fusion.208
  697.6 4.4 fusion.209
  742.3 4.2 fusion.207
  746.5 6.4 fusion.208
  752.9 4.4 fusion.209
  757.3 3.7 copy.157
  792.7 4.5 collective-permute-done.7
  808.7 5.2 collective-permute-done.11
  825.4 5.2 collective-permute-done.15
  (615 shorter events, 500.3 us)
Async XLA Ops:
  0.6 28.0 %copy-start = (bf16[96,3200]{1,0:T(8,128)(2,1)S(1)}, bf16[96,3200]{1,0:T(8,128)(2,1)}, u32[]{:S(2)}) copy-start(bf16[96,3200]{1,0:T(8,128)(2,1)} %param.12) | copy-start | bytes 1843204
  3.9 17.7 %all-to-all-start.2 = ((bf16[128,1,1]{2,1,0:T(2,128)(2,1)}), bf16[128,1,1]{2,1,0:T(2,128)(2,1)S(1)}, u32[]{:S(2)}, u32[]{:S(2)}) async-start(bf16[128,1,1]{2,1,0:T(2,128)(2,1)} %copy.103), calls=%async_computation.2 | async-start | bytes 131072 | tf_op jit(solution)/shard_map/all_to_all | solution.py:139
  21.6 14.2 %all-to-all-start = ((bf16[128,1,1]{2,1,0:T(2,128)(2,1)}), bf16[128,1,1]{2,1,0:T(2,128)(2,1)S(1)}, u32[]{:S(2)}, u32[]{:S(2)}) async-start(bf16[128,1,1]{2,1,0:T(2,128)(2,1)} %copy.100), calls=%async_computation | async-start | bytes 131072 | tf_op jit(solution)/shard_map/all_to_all | solution.py:125
  29.0 13.8 %copy-start.10 = (bf16[96,3200]{1,0:T(8,128)(2,1)S(1)}, bf16[96,3200]{1,0:T(8,128)(2,1)}, u32[]{:S(2)}) copy-start(bf16[96,3200]{1,0:T(8,128)(2,1)} %param.9) | copy-start | bytes 1843204
  35.7 21.4 %all-to-all-start.3 = ((bf16[128,2,1600]{2,1,0:T(2,128)(2,1)}), bf16[128,2,1600]{2,1,0:T(2,128)(2,1)S(1)}, u32[]{:S(2)}, u32[]{:S(2)}) async-start(bf16[128,2,1600]{2,1,0:T(2,128)(2,1)} %reshape.268), calls=%async_computation.3 | async-start | bytes 1703936 | tf_op jit(solution)/shard_map/all_to_all | solution.py:132
  57.2 22.4 %all-to-all-start.1 = ((bf16[128,2,1600]{2,1,0:T(2,128)(2,1)}), bf16[128,2,1600]{2,1,0:T(2,128)(2,1)}, u32[]{:S(2)}, u32[]{:S(2)}) async-start(bf16[128,2,1600]{2,1,0:T(2,128)(2,1)} %reshape.266), calls=%async_computation.1 | async-start | bytes 1703936 | tf_op jit(solution)/shard_map/all_to_all | solution.py:118
  87.5 16.6 %copy-start.13 = (s32[12,16]{1,0:T(8,128)S(1)}, s32[12,16]{1,0:T(8,128)}, u32[]{:S(2)}) copy-start(s32[12,16]{1,0:T(8,128)} %param.15) | copy-start | bytes 2308
  87.6 8.7 %copy-start.9 = (bf16[2,480,640]{2,1,0:T(8,128)(2,1)}, bf16[2,480,640]{2,1,0:T(8,128)(2,1)S(1)}, u32[]{:S(2)}) copy-start(bf16[2,480,640]{2,1,0:T(8,128)(2,1)S(1)} %constant_dynamic-update-slice_fusion) | copy-start | bytes 3686404
  87.7 6.9 collective-permute-start
  89.6 6.7 collective-permute-start.1
  96.5 9.3 %collective-permute-start.2 = (bf16[2,600,60]{2,1,0:T(8,128)(2,1)S(1)}, bf16[2,600,60]{2,1,0:T(8,128)(2,1)S(1)}, u32[]{:S(2)}, u32[]{:S(2)}) collective-permute-start(bf16[2,600,60]{2,1,0:T(8,128)(2,1)S(1)} %get-tuple-element.221), channel_id=1, source_target_pairs={{0,1},{1,2},{2,3},{3,4},{4,5},{5,6},{6,7},{7,8},{8,9},{9,10},{10,1... | collective-permute-start | bytes 432008 | tf_op jit(solution)/shard_map/ppermute | solution.py:25
  102.0 10.4 %collective-permute-start.3 = (bf16[2,600,60]{2,1,0:T(8,128)(2,1)S(1)}, bf16[2,600,60]{2,1,0:T(8,128)(2,1)}, u32[]{:S(2)}, u32[]{:S(2)}) collective-permute-start(bf16[2,600,60]{2,1,0:T(8,128)(2,1)S(1)} %get-tuple-element.222), channel_id=1, source_target_pairs={{1,0},{2,1},{3,2},{4,3},{5,4},{6,5},{7,6},{8,7},{9,8},{10,9},{11,1... | collective-permute-start | bytes 432008 | tf_op jit(solution)/shard_map/ppermute | solution.py:28
  115.1 663.8 %copy-start.12 = (f32[12,16]{1,0:T(8,128)S(1)}, f32[12,16]{1,0:T(8,128)}, u32[]{:S(2)}) copy-start(f32[12,16]{1,0:T(8,128)} %convert_element_type.243) | copy-start | bytes 2308
  115.1 676.9 %copy-start.14 = (s32[12,16]{1,0:T(8,128)S(1)}, s32[12,16]{1,0:T(8,128)}, u32[]{:S(2)}) copy-start(s32[12,16]{1,0:T(8,128)} %param.15) | copy-start | bytes 2308
  134.1 4.2 copy-start.3
  152.8 2.4 copy-start.6
  161.3 2.5 copy-start.5
  167.5 3.1 copy-start.8
  189.3 4.2 copy-start.3
  216.6 2.5 copy-start.5
  222.8 3.1 copy-start.8
  244.6 4.2 copy-start.3
  271.9 2.5 copy-start.5
  278.1 3.1 copy-start.8
  299.9 4.2 copy-start.3
  327.2 2.5 copy-start.5
  333.4 3.1 copy-start.8
  355.2 4.2 copy-start.3
  382.5 2.5 copy-start.5
  388.7 3.1 copy-start.8
  410.5 4.2 copy-start.3
  437.8 2.5 copy-start.5
  444.0 3.1 copy-start.8
  465.8 4.2 copy-start.3
  493.1 2.5 copy-start.5
  499.3 3.1 copy-start.8
  521.1 4.2 copy-start.3
  548.4 2.5 copy-start.5
  554.6 3.1 copy-start.8
  576.4 4.2 copy-start.3
  603.7 2.5 copy-start.5
  609.9 3.1 copy-start.8
  631.7 4.2 copy-start.3
  659.0 2.5 copy-start.5
  665.2 3.1 copy-start.8
  687.0 4.2 copy-start.3
  714.3 2.5 copy-start.5
  720.5 3.1 copy-start.8
  742.3 4.2 copy-start.3
  769.6 2.5 copy-start.5
  775.7 3.1 copy-start.8
  778.8 53.1 %copy-start.1 = (bf16[96,3200]{1,0:T(8,128)(2,1)S(1)}, bf16[96,3200]{1,0:T(8,128)(2,1)}, u32[]{:S(2)}) copy-start(bf16[96,3200]{1,0:T(8,128)(2,1)} %param.12) | copy-start | bytes 1843204
  778.9 5.6 collective-permute-start.4
  782.6 4.3 collective-permute-start.5
  787.0 5.7 collective-permute-start.6
  790.1 7.2 collective-permute-start.7
  797.3 5.3 collective-permute-start.8
  799.3 4.3 collective-permute-start.9
  803.7 5.0 collective-permute-start.10
  806.7 7.2 collective-permute-start.11
  814.0 5.3 collective-permute-start.12
  815.9 4.3 collective-permute-start.13
  820.4 5.0 collective-permute-start.14
  823.4 7.2 collective-permute-start.15
  (59 other events, 93.1 us)
where the time goes:
time: 838 us; the launch traced here: 832 us
  local copies, waits for them, and re-layouts  334 us (40%)
  matrix products  290 us (35%)
  starting transfers between devices  76.7 us (9%)
  other arithmetic  66.6 us (8%)
  waiting for transfers between devices  53.7 us (6%)
  loops' own time  9.88 us (1%)
    dot_general x48, matrix products, one_row(): jnp.einsum('ayjs,sk->ajyk', part_cells, column_table[column_step], prefer...  155 us
    while x240, local copies, waits for them, and re-layouts  129 us
    squeeze x24, local copies, waits for them, and re-layouts, forward_rest(): halves = first_segment.reshape(first_segment.shape[0], PATCH, 2, PATCH)  88.9 us
    slice x12, local copies, waits for them, and re-layouts, one_row(): first_segment[0]  53.2 us
    reduce_sum x24, other arithmetic, one_row(): square_total = square_total + jnp.sum(values * values, axis=(1, 3))  51 us
    dot_general x24, matrix products, forward_rest(): jnp.einsum('hky,nyhj->nkj', left_real, halves, preferred_element_type=jnp...  45.6 us
    dot_general x24, matrix products, forward_rest(): jnp.einsum('hky,nyhj->nkj', left_imag, halves, preferred_element_type=jnp...  38.7 us
    ppermute x8, waiting for transfers between devices, extended_2(): lax.ppermute(lax.slice_in_dim(block, 0, width, axis=dim), axis, backward)  27.5 us
  transfers between devices with their start and end apart: 20, of which 14 were waited for; matrix products, arithmetic and copies ran while one was open for 2% of the time, Pallas kernels for 0%

commit v1 on v0

v1 whole, which is shorter than its diff:
```python
import math

import jax
import jax.numpy as jnp
import numpy as np
from jax import lax
from jax.experimental import pallas as pl
from jax.experimental.pallas import tpu as pltpu
from jax.sharding import PartitionSpec as P

PATCH = 160
STRIDE = 40
TY = 12
TX = 8
SWEEPS = 3
MARGIN = 60
HALF = PATCH // 2
FREQ = HALF + 1
WIN = 3
GROUPS = 6
BLOCKS = 11
ROWS = 16 * BLOCKS
IMG_H = 640
IMG_W = 896
FIRST_H = 608

stiffness = 1.0
tiny = 1e-06


def trig():
    k = np.arange(FREQ)
    n = np.arange(PATCH)
    phase = (k[:, None] * n[None, :] % PATCH).astype(np.float64) * (2.0 * math.pi / PATCH)
    cosine, sine = np.cos(phase), np.sin(phase)
    sine[0] = 0.0
    sine[HALF] = 0.0
    return cosine, sine


def tables():
    cosine, sine = trig()
    first = np.zeros((256, 512))
    for w in range(WIN):
        rows = slice(STRIDE * w, STRIDE * w + PATCH)
        first[rows, FREQ * w : FREQ * (w + 1)] = cosine.T
        first[rows, 256 + FREQ * w : 256 + FREQ * (w + 1)] = sine.T
    cos_pad = np.zeros((8 * BLOCKS, PATCH))
    sin_pad = np.zeros((8 * BLOCKS, PATCH))
    cos_pad[:FREQ] = cosine
    sin_pad[:FREQ] = sine
    mixed = np.stack([cos_pad.reshape(BLOCKS, 8, PATCH), sin_pad.reshape(BLOCKS, 8, PATCH)], 1)
    mixed = mixed.reshape(ROWS, PATCH)
    second = np.zeros((2, ROWS, ROWS))
    second[0, :, :PATCH] = mixed
    second[1, :, 8 : 8 + PATCH] = mixed
    half = np.ones((FREQ, 1))
    half[0] = half[HALF] = 0.5
    even = (cosine * half)[:, :HALF].copy()
    even[:, 0] = (cosine * half)[:, HALF]
    odd = sine[:, :HALF].copy()
    rows_inv = np.zeros((PATCH, BLOCKS, 2, 8))
    even_pad = np.zeros((8 * BLOCKS, HALF))
    odd_pad = np.zeros((8 * BLOCKS, HALF))
    even_pad[:FREQ] = even
    odd_pad[:FREQ] = odd
    rows_inv[:HALF, :, 0] = even_pad.T.reshape(HALF, BLOCKS, 8)
    rows_inv[HALF:, :, 1] = odd_pad.T.reshape(HALF, BLOCKS, 8)
    rows_inv[HALF, :, 0] = even_pad.T.reshape(HALF, BLOCKS, 8)[0]
    rows_inv = rows_inv.reshape(PATCH, ROWS)
    cols_even = np.zeros((256, 256))
    cols_odd = np.zeros((256, 256))
    for w in range(WIN):
        cols_even[FREQ * w : FREQ * (w + 1), HALF * w : HALF * (w + 1)] = even
        cols_odd[FREQ * w : FREQ * (w + 1), HALF * w : HALF * (w + 1)] = odd
    select = np.zeros((1280, 128))
    for w in range(WIN):
        lanes = np.arange(FREQ) + FREQ * w
        select[lanes, w] = half[:, 0]
        select[256 + lanes, w] = 1.0
        select[512 + HALF * w + np.arange(HALF), 32 + w] = 1.0
        select[768 + lanes, 64 + w] = half[:, 0]
        select[1024 + lanes, 64 + w] = 1.0
    window = np.zeros((IMG_W, 128))
    for j in range(16):
        for kind in range(3):
            window[STRIDE * j : STRIDE * j + PATCH, 32 * kind + j] = 1.0
    as_bf16 = lambda x: jnp.asarray(x.astype(jnp.bfloat16))
    return tuple(as_bf16(x) for x in (first, second, rows_inv, cols_even, cols_odd, select, window))


def dot(a, b):
    return lax.dot_general(a, b, (((1,), (0,)), ((), ())), preferred_element_type=jnp.float32)


def dot_exact(a, b):
    return lax.dot_general(
        a,
        b,
        (((1,), (0,)), ((), ())),
        preferred_element_type=jnp.float32,
        precision=lax.Precision.HIGHEST,
    )


def window_norms(img_ref, cells_ref, window):
    for c in range(8):
        values = img_ref[80 * c : 80 * c + 80, :].astype(jnp.float32)
        squares = (values * values).reshape(2, 5, 8, IMG_W).sum(axis=1)
        sums = squares.sum(axis=1)
        cells_ref[2 * c : 2 * c + 2, :] = sums
    cells = cells_ref[...]
    row = lax.broadcasted_iota(jnp.int32, (16, 16), 0)
    col = lax.broadcasted_iota(jnp.int32, (16, 16), 1)
    band = ((col >= row) & (col < row + 4)).astype(jnp.float32)
    total = dot_exact(dot_exact(band, cells), window)
    return total / (PATCH * PATCH) + tiny


def correlate_kernel(
    img_a, img_b, first, second, rows_inv, cols_even, cols_odd, select, window, out, fa, fb, cells, raw
):
    window_f32 = window[...].astype(jnp.float32)
    mean_a = window_norms(img_a, cells, window_f32)
    mean_b = window_norms(img_b, cells, window_f32)
    for g in range(GROUPS):
        lo = WIN * STRIDE * g
        for img, dst in ((img_a, fa), (img_b, fb)):
            dst[g] = dot(img[:FIRST_H, lo : lo + 256], first[...]).astype(jnp.bfloat16)

    sub = lax.broadcasted_iota(jnp.int32, (8, 256), 0)
    lane = lax.broadcasted_iota(jnp.int32, (8, 256), 1)
    top_half = jnp.where(sub == 0, 0.5, 1.0)
    top_half2 = jnp.concatenate([top_half, top_half], axis=1)
    slot_zero = lane % HALF == 0
    shift_x = jnp.where(slot_zero, -8.0, 0.4 * (lane % HALF).astype(jnp.float32))[:1]
    sub_f = jnp.concatenate([sub, sub], axis=1).astype(jnp.float32)

    def weighted_rows(x):
        total = x[1, 0] + x[1, 1]
        for t in range(2, BLOCKS - 1):
            total = total + (x[t, 0] + x[t, 1])
        return total + x[0, 1] + (x[0, 0] * (top_half2 if x.shape[-1] == 512 else top_half) + 0.5 * x[BLOCKS - 1, 0])

    def one(g, q, parity):
        start = pl.multiple_of(80 * q + 32 * parity, 16)
        spec = []
        for src in (fa, fb):
            s = dot(second[parity], src[g, pl.ds(start, ROWS), :]).reshape(BLOCKS, 2, 8, 512)
            cc, cs = s[:, 0, :, :256], s[:, 0, :, 256:]
            sc, ss = s[:, 1, :, :256], s[:, 1, :, 256:]
            spec.append((cc - ss, sc + cs, cc + ss, sc - cs))
        (a1, a2, a3, a4), (b1, b2, b3, b4) = spec
        plus_r = a1 * b1 + a2 * b2
        plus_i = a1 * b2 - a2 * b1
        minus_r = a3 * b3 + a4 * b4
        minus_i = a3 * b4 - a4 * b3
        dcc = plus_r + minus_r
        dss = minus_r - plus_r
        dsc = plus_i + minus_i
        dcs = plus_i - minus_i
        d = jnp.stack(
            [jnp.concatenate([dcc, dcs], axis=2), jnp.concatenate([dsc, dss], axis=2)], axis=1
        )
        weight = weighted_rows(d * d)
        d16 = d.reshape(ROWS, 512).astype(jnp.bfloat16)
        inv = dot(rows_inv[...], d16)
        prod = (inv[:HALF] * inv[HALF:]).reshape(10, 8, 512)
        run = prod[9]
        ramp = prod[9]
        for t in range(8, 0, -1):
            run = run + prod[t]
            ramp = ramp + run
        run = run + prod[0]
        flow_y = 3.2 * ramp + 0.4 * sub_f * run
        flow_y = jnp.where(sub_f == 0.0, flow_y - 8.0 * prod[0], flow_y)
        even = dot(d16[:, :256], cols_even[...]).reshape(BLOCKS, 2, 8, 256)
        odd = dot(d16[:, 256:], cols_odd[...]).reshape(BLOCKS, 2, 8, 256)
        flow_x = weighted_rows(even * jnp.where(slot_zero[None, None], even, odd))
        i = 2 * q + parity
        raw[g, pl.ds(i, 1), 0:512] = jnp.sum(flow_y, axis=0, keepdims=True)
        raw[g, pl.ds(i, 1), 512:768] = jnp.sum(flow_x, axis=0, keepdims=True) * shift_x
        raw[g, pl.ds(i, 1), 768:1280] = jnp.sum(weight, axis=0, keepdims=True)

    raw[:, 12:16, :] = jnp.zeros((GROUPS, 4, 1280), jnp.float32)

    def step(n, carry):
        g = n // 6
        q = n % 6
        one(g, q, 0)
        one(g, q, 1)
        return carry

    lax.fori_loop(0, GROUPS * 6, step, 0)
    sums = dot_exact(raw[...].reshape(GROUPS * 16, 1280), select[...].astype(jnp.float32))
    sums = sums.reshape(GROUPS, 16, 128)
    lane128 = lax.broadcasted_iota(jnp.int32, (16, 128), 1) % 32
    total = sums[0]
    for g in range(1, GROUPS):
        piece = sums[g] if g < 5 else jnp.where(lane128 == 0, sums[g], 0.0)
        total = total + pltpu.roll(piece, WIN * g, axis=1)
    scale = (1.0 / (PATCH * PATCH)) / (mean_a * mean_b)
    unit = (2.0 / (PATCH * PATCH)) ** 2 * HALF / (PATCH * PATCH)
    total = total * (scale * unit)
    lane_all = lax.broadcasted_iota(jnp.int32, (16, 128), 1)
    weight = jnp.where(lane_all >= 64, total * HALF, 0.0)
    down = 1.0 + weight + pltpu.roll(weight, 96, axis=1) + pltpu.roll(weight, 64, axis=1)
    out[...] = jnp.where(lane_all >= 64, weight, total) / down


def correlate(img_a, img_b):
    return pl.pallas_call(
        correlate_kernel,
        out_shape=jax.ShapeDtypeStruct((16, 128), jnp.float32),
        scratch_shapes=[
            pltpu.VMEM((GROUPS, FIRST_H, 512), jnp.bfloat16),
            pltpu.VMEM((GROUPS, FIRST_H, 512), jnp.bfloat16),
            pltpu.VMEM((16, IMG_W), jnp.float32),
            pltpu.VMEM((GROUPS, 16, 1280), jnp.float32),
        ],
    )(img_a, img_b, *tables())


def extended_2(block, sides, width):
    for axis, dim in sides:
        count = lax.axis_size(axis)
        forward = [(i, i + 1) for i in range(count - 1)]
        backward = [(target, source) for source, target in forward]
        low = lax.ppermute(
            lax.slice_in_dim(block, block.shape[dim] - width, None, axis=dim), axis, forward
        )
        high = lax.ppermute(lax.slice_in_dim(block, 0, width, axis=dim), axis, backward)
        block = jnp.concatenate([low, block, high], axis=dim)
    return block


def outgoing(tiles, tile_owner, tile_offset, slot_count, tile_h, tile_w):
    select = (jnp.arange(slot_count, dtype=jnp.int32)[:, None] == tile_owner[None, :]).astype(
        jnp.bfloat16
    )
    position = tile_offset[:, 0] // tile_h * TX + tile_offset[:, 1] // tile_w + 1
    sent_tiles = jnp.dot(select, tiles, preferred_element_type=jnp.float32).astype(jnp.bfloat16)
    slot_code = jnp.dot(
        select, position.astype(jnp.bfloat16)[:, None], preferred_element_type=jnp.float32
    ).astype(jnp.bfloat16)
    return (sent_tiles, slot_code)


def incoming(received, slot_code, tile_count, tile_h, tile_w):
    wanted = jnp.arange(1, tile_count + 1, dtype=jnp.int32).astype(jnp.float32)
    select = (slot_code.astype(jnp.float32)[None, :] == wanted[:, None]).astype(jnp.bfloat16)
    blocks = jnp.dot(select, received, preferred_element_type=jnp.float32).astype(jnp.bfloat16)
    return (
        blocks.reshape(TY, TX, tile_h, tile_w)
        .transpose(0, 2, 1, 3)
        .reshape(TY * tile_h, TX * tile_w)
    )


def per_device(a_tiles, a_owner, a_offset, b_tiles, b_owner, b_offset, patch_valid):
    grid_rows, grid_cols = patch_valid.shape
    tile_h = grid_rows * STRIDE // TY
    tile_w = grid_cols * STRIDE // TX
    tile_count, tile_size = a_tiles.shape
    devices = lax.axis_size("row") * lax.axis_size("col")
    send_a, code_a = outgoing(a_tiles, a_owner, a_offset, devices, tile_h, tile_w)
    send_b, code_b = outgoing(b_tiles, b_owner, b_offset, devices, tile_h, tile_w)
    code = jnp.pad(jnp.concatenate([code_a, code_b], axis=1), ((0, 0), (0, 126)))
    packed = jnp.concatenate([send_a, send_b, code], axis=1).reshape(devices, 51, 128)
    got = lax.all_to_all(packed, ("row", "col"), split_axis=0, concat_axis=0, tiled=True)
    got_a = got[:, :25].reshape(devices, tile_size)
    got_b = got[:, 25:50].reshape(devices, tile_size)
    canvas_a = incoming(got_a, got[:, 50, 0], tile_count, tile_h, tile_w)
    canvas_b = incoming(got_b, got[:, 50, 1], tile_count, tile_h, tile_w)
    images = jnp.stack([canvas_a, canvas_b])
    padded = extended_2(images, (("row", 1), ("col", 2)), MARGIN)
    padded = jnp.pad(
        padded, ((0, 0), (0, IMG_H - padded.shape[1]), (0, IMG_W - padded.shape[2]))
    )
    result = correlate(padded[0], padded[1])
    flow_field = jnp.stack([result[:grid_rows, :grid_cols], result[:grid_rows, 32 : 32 + grid_cols]])
    confidence = result[:grid_rows, 64 : 64 + grid_cols]
    valid_float = patch_valid.astype(jnp.float32)
    strength = valid_float * confidence
    start = valid_float[None] * flow_field
    fields = jnp.concatenate([start, (strength + 4.0 * stiffness)[None]])
    fields = extended_2(fields, (("row", 1), ("col", 2)), SWEEPS)
    mesh = fields[:2]
    down = fields[2]
    inside = down > 0.0
    rest = jnp.where(inside, 1.0 / jnp.where(inside, down, 1.0), 0.0)
    pull = mesh * jnp.where(inside, down - 4.0 * stiffness, 0.0)
    for sweep_index in range(SWEEPS):
        around = mesh[:, :-2, 1:-1] + mesh[:, 2:, 1:-1] + mesh[:, 1:-1, :-2] + mesh[:, 1:-1, 2:]
        rest = rest[1:-1, 1:-1]
        pull = pull[:, 1:-1, 1:-1]
        mesh = (pull + stiffness * around) * rest
    return (flow_field, mesh)


def solution(mesh):
    in_specs = (
        P(("row", "col"), None),
        P(("row", "col")),
        P(("row", "col"), None),
        P(("row", "col"), None),
        P(("row", "col")),
        P(("row", "col"), None),
        P("row", "col"),
    )
    out_specs = (P(None, "row", "col"), P(None, "row", "col"))
    return jax.shard_map(
        per_device, mesh=mesh, in_specs=in_specs, out_specs=out_specs, check_vma=False
    )
```

time: 838 us -> 152 us (0.18)
  local copies, waits for them, and re-layouts: 334 us -> 21.8 us
  matrix products: 290 us -> 7.17 us
  other arithmetic: 66.6 us -> 4.98 us
  starting transfers between devices: 76.7 us -> 35 us
  Pallas kernels: 0 us -> 38.4 us
  waiting for transfers between devices: 53.7 us -> 42.6 us
  loops' own time: 9.88 us -> 0 us
    dot_general x132 -> x0, matrix products: 287 us -> none  [the longest x48 155 us: one_row(): jnp.einsum('ayjs,sk->ajyk', part_cells, column_table[column_step], prefer...]
    while x240 -> x0, local copies, waits for them, and re-layouts: 129 us -> none
    squeeze x24 -> x1, local copies, waits for them, and re-layouts: 88.9 us -> 1.57 us  [per_device(): result = correlate(padded[0], padded[1])]
    slice x24 -> x4, local copies, waits for them, and re-layouts: 69.1 us -> 1.72 us  [the longest x1 1.51 us: per_device(): got_b = got[:, 25:50].reshape(devices, tile_size)]
    reduce_sum x26 -> x0, other arithmetic: 52.8 us -> none  [the longest x24 51 us: one_row(): square_total = square_total + jnp.sum(values * values, axis=(1, 3))]
    pallas_call x0 -> x1, Pallas kernels: none -> 38.4 us  [correlate(): pl.pallas_call(correlate_kernel, out_shape=jax.ShapeDtypeStruct((16, 128)...]
    all_to_all x4 -> x1, starting transfers between devices: 32.9 us -> 10.5 us  [per_device(): lax.all_to_all(packed, ('row', 'col'), split_axis=0, concat_axis=0, tiled...]
    dynamic_update_slice x36 -> x0, local copies, waits for them, and re-layouts: 16.5 us -> none  [per_device(): lax.map(one_row, jnp.arange(grid_rows, dtype=jnp.int32))]
  transfers between devices with their start and end apart: 20 -> 9, of which waited for: 14 -> 7; matrix products, arithmetic and copies ran while one was open for 2% -> 0% of each run, Pallas kernels for 0% -> 0%
where the time goes in v1:
time: 152 us; the launch traced here: 151 us
  waiting for transfers between devices  42.6 us (28%)
  Pallas kernels  38.4 us (25%)
  starting transfers between devices  35 us (23%)
  local copies, waits for them, and re-layouts  21.8 us (14%)
  matrix products  7.17 us (5%)
  other arithmetic  4.98 us (3%)
    pallas_call x1, Pallas kernels, correlate(): pl.pallas_call(correlate_kernel, out_shape=jax.ShapeDtypeStruct((16, 128)...  38.4 us
    all_to_all x1, waiting for transfers between devices, per_device(): lax.all_to_all(packed, ('row', 'col'), split_axis=0, concat_axis=0, tiled...  24.4 us
    ppermute x4, waiting for transfers between devices, extended_2(): lax.ppermute(lax.slice_in_dim(block, 0, width, axis=dim), axis, backward)  15.5 us
    ppermute x4, starting transfers between devices, extended_2(): lax.ppermute(lax.slice_in_dim(block, block.shape[dim] - width, None, axis...  15.2 us
    all_to_all x1, starting transfers between devices, per_device(): lax.all_to_all(packed, ('row', 'col'), split_axis=0, concat_axis=0, tiled...  10.5 us
    ppermute x4, starting transfers between devices, extended_2(): lax.ppermute(lax.slice_in_dim(block, 0, width, axis=dim), axis, backward)  9.27 us
    unnamed x9, local copies, waits for them, and re-layouts  5.04 us
    reshape x4, local copies, waits for them, and re-layouts, incoming(): blocks.reshape(TY, TX, tile_h, tile_w).transpose(0, 2, 1, 3)  4.56 us
  transfers between devices with their start and end apart: 9, of which 7 were waited for; matrix products, arithmetic and copies ran while one was open for 0% of the time, Pallas kernels for 0%

profile of v1, /device:TPU:27, one launch (start us, length us, event | category | flops | bytes accessed | tf_op | source)
XLA Modules:
  0.0 150.9 jit_solution(2695007695314095589)
XLA Ops:
  0.6 0.0 copy-start
  0.6 0.9 fusion.18
  1.6 0.9 fusion.20
  2.5 0.1 copy.37
  2.6 0.0 copy-done
  2.6 1.0 convolution_convert_fusion.1
  3.7 1.5 convolution_convert_fusion
  5.1 0.1 fusion.16
  5.2 2.2 %copy.38 = bf16[128,6528]{0,1:T(8,128)(2,1)} copy(bf16[128,6528]{1,0:T(8,128)(2,1)S(1)} %fusion.16) | data formatting | bytes 3342336 | tf_op jit(solution)/shard_map/concatenate | solution.py:269
  7.4 3.6 %copy.39 = bf16[128,51,128]{2,1,0:T(8,128)(2,1)} copy(bf16[128,51,128]{0,2,1:T(8,128)(2,1)} %bitcast.49) | data formatting | bytes 3342336 | tf_op jit(solution)/shard_map/reshape | solution.py:269
  11.1 10.5 %all-to-all-start = ((bf16[128,51,128]{2,1,0:T(8,128)(2,1)}), bf16[128,51,128]{2,1,0:T(8,128)(2,1)S(1)}, u32[]{:S(2)}, u32[]{:S(2)}) async-start(bf16[128,51,128]{2,1,0:T(8,128)(2,1)} %copy.39), calls=%async_computation | async-start | bytes 3670016 | tf_op jit(solution)/shard_map/all_to_all | solution.py:270
  21.6 24.4 %all-to-all-done = bf16[128,51,128]{2,1,0:T(8,128)(2,1)S(1)} async-done(((bf16[128,51,128]{2,1,0:T(8,128)(2,1)}), bf16[128,51,128]{2,1,0:T(8,128)(2,1)S(1)}, u32[]{:S(2)}, u32[]{:S(2)}) %all-to-all-start) | async-done | bytes 1671200 | tf_op jit(solution)/shard_map/all_to_all | solution.py:270
  46.0 1.5 fusion.82
  47.5 2.6 %copy.47 = bf16[128,25,128]{0,2,1:T(8,128)(2,1)} copy(bf16[128,25,128]{2,1,0:T(8,128)(2,1)} %get-tuple-element.14) | data formatting | bytes 1638400
  50.1 1.6 %fusion.21 = (f32[128]{0:T(128)S(1)}, f32[128]{0:T(128)S(1)}) fusion(bf16[128,51,128]{2,1,0:T(8,128)(2,1)S(1)} %all-to-all-done), kind=kLoop, calls=%fused_computation.38 | loop fusion | flops 256 | bytes 1536 | tf_op jit(solution)/shard_map/convert_element_type | solution.py:251
  51.7 1.6 %convolution_convert_fusion.2 = bf16[96,3200]{1,0:T(8,128)(2,1)S(1)} fusion(bf16[128,3200]{0,1:T(8,128)(2,1)} %bitcast.52, f32[128]{0:T(128)S(1)} %get-tuple-element.10, f32[96]{0:T(128)S(1)} %add_convert_fusion), kind=kOutput, calls=%fused_computation.2 | convolution fusion | flops 78962688 | bytes 1434496 | tf_op jit(solution)/shard_map/dot_general | solution.py:252
  53.3 1.1 reshape.60
  54.3 1.1 copy.50
  55.4 2.0 %stack_reshape.7 = bf16[1,480,640]{2,1,0:T(8,128)(2,1)S(1)} reshape(bf16[12,40,8,80]{3,2,1,0:T(8,128)(2,1)} %bitcast.50) | data formatting | bytes 1228800 | tf_op jit(solution)/shard_map/stack;reshape | solution.py:275
  57.4 1.2 copy.46
  58.6 1.3 convolution_convert_fusion.3
  59.9 2.2 %reshape.58 = bf16[12,8,40,80]{3,2,1,0:T(8,128)(2,1)S(1)} reshape(bf16[96,3200]{1,0:T(8,128)(2,1)} %convolution_convert_fusion.3) | data formatting | bytes 1228800 | tf_op jit(solution)/shard_map/reshape | solution.py:254
  62.1 0.2 copy.51
  62.3 0.8 stack_reshape.6
  63.0 0.1 constant_dynamic-update-slice_fusion.1
  63.1 0.0 copy-start.1
  63.1 0.1 constant_dynamic-update-slice_fusion
  63.3 2.0 %collective-permute-start = (bf16[2,60,640]{2,1,0:T(8,128)(2,1)S(1)}, bf16[2,60,640]{2,1,0:T(8,128)(2,1)S(1)}, u32[]{:S(2)}, u32[]{:S(2)}) collective-permute-start(bf16[2,60,640]{2,1,0:T(8,128)(2,1)S(1)} %get-tuple-element.18), channel_id=1, source_target_pairs={{0,32},{32,64},{64,96},{1,33},{33,65},{65,97},{2,34},{34,66},{66,9... | collective-permute-start | bytes 460808 | tf_op jit(solution)/shard_map/ppermute | solution.py:229
  65.2 3.3 %collective-permute-start.1 = (bf16[2,60,640]{2,1,0:T(8,128)(2,1)S(1)}, bf16[2,60,640]{2,1,0:T(8,128)(2,1)S(1)}, u32[]{:S(2)}, u32[]{:S(2)}) collective-permute-start(bf16[2,60,640]{2,1,0:T(8,128)(2,1)S(1)} %get-tuple-element.19), channel_id=1, source_target_pairs={{32,0},{64,32},{96,64},{33,1},{65,33},{97,65},{34,2},{66,34},{98,6... | collective-permute-start | bytes 460808 | tf_op jit(solution)/shard_map/ppermute | solution.py:232
  68.6 1.1 collective-permute-done
  69.7 1.7 %collective-permute-done.1 = bf16[2,60,640]{2,1,0:T(8,128)(2,1)S(1)} collective-permute-done((bf16[2,60,640]{2,1,0:T(8,128)(2,1)S(1)}, bf16[2,60,640]{2,1,0:T(8,128)(2,1)S(1)}, u32[]{:S(2)}, u32[]{:S(2)}) %collective-permute-start.1) | collective-permute-done | bytes 153632 | tf_op jit(solution)/shard_map/ppermute | solution.py:232
  71.4 0.2 pad_maximum_fusion.2
  71.6 6.5 %collective-permute-start.2 = (bf16[2,600,60]{2,1,0:T(8,128)(2,1)S(1)}, bf16[2,600,60]{2,1,0:T(8,128)(2,1)S(1)}, u32[]{:S(2)}, u32[]{:S(2)}) collective-permute-start(bf16[2,600,60]{2,1,0:T(8,128)(2,1)S(1)} %get-tuple-element.16), channel_id=1, source_target_pairs={{0,1},{1,2},{2,3},{3,4},{4,5},{5,6},{6,7},{7,8},{8,9},{9,10},{10,1... | collective-permute-start | bytes 432008 | tf_op jit(solution)/shard_map/ppermute | solution.py:229
  78.1 2.1 %collective-permute-start.3 = (bf16[2,600,60]{2,1,0:T(8,128)(2,1)S(1)}, bf16[2,600,60]{2,1,0:T(8,128)(2,1)S(1)}, u32[]{:S(2)}, u32[]{:S(2)}) collective-permute-start(bf16[2,600,60]{2,1,0:T(8,128)(2,1)S(1)} %get-tuple-element.17), channel_id=1, source_target_pairs={{1,0},{2,1},{3,2},{4,3},{5,4},{6,5},{7,6},{8,7},{9,8},{10,9},{11,1... | collective-permute-start | bytes 432008 | tf_op jit(solution)/shard_map/ppermute | solution.py:232
  80.2 0.0 copy-done.1
  80.2 1.6 %collective-permute-done.2 = bf16[2,600,60]{2,1,0:T(8,128)(2,1)S(1)} collective-permute-done((bf16[2,600,60]{2,1,0:T(8,128)(2,1)S(1)}, bf16[2,600,60]{2,1,0:T(8,128)(2,1)S(1)}, u32[]{:S(2)}, u32[]{:S(2)}) %collective-permute-start.2) | collective-permute-done | bytes 144032 | tf_op jit(solution)/shard_map/ppermute | solution.py:229
  81.9 6.5 %collective-permute-done.3 = bf16[2,600,60]{2,1,0:T(8,128)(2,1)S(1)} collective-permute-done((bf16[2,600,60]{2,1,0:T(8,128)(2,1)S(1)}, bf16[2,600,60]{2,1,0:T(8,128)(2,1)S(1)}, u32[]{:S(2)}, u32[]{:S(2)}) %collective-permute-start.3) | collective-permute-done | bytes 144032 | tf_op jit(solution)/shard_map/ppermute | solution.py:232
  88.4 1.8 %fusion.9 = bf16[2,640,896]{2,1,0:T(8,128)(2,1)S(1)} fusion(bf16[2,600,60]{2,1,0:T(8,128)(2,1)S(1)} %collective-permute-done.3, bf16[2,600,60]{2,1,0:T(8,128)(2,1)S(1)} %collective-permute-done.2, bf16[2,60,640]{2,1,0:T(8,128)(2,1)S(1)} %collective-permute-done.1, bf16[2,480,640]{2,1,0:T(8,128)(2,1)S(1)} %constant_dynamic-update-slice_fusion, ...), kind=kLoop, calls=%fused_computation.16 | loop fusion | flops 26378240 | bytes 4117760 | tf_op jit(solution)/shard_map/concatenate | solution.py:233
  90.2 1.6 %slice_bitcast_fusion = (bf16[640,896]{1,0:T(8,128)(2,1)}, bf16[640,896]{1,0:T(8,128)(2,1)}) fusion(bf16[2,640,896]{2,1,0:T(8,128)(2,1)S(1)} %fusion.9), kind=kLoop, calls=%fused_computation.24 | loop fusion | bytes 4587520 | tf_op jit(solution)/shard_map/squeeze | solution.py:280
  91.7 38.4 %shard_map.149 = f32[16,128]{1,0:T(8,128)} custom-call(bf16[640,896]{1,0:T(8,128)(2,1)} %get-tuple-element.13.img_a, bf16[640,896]{1,0:T(8,128)(2,1)} %get-tuple-element.12.img_b, bf16[256,512]{1,0:T(8,128)(2,1)} %constant.54.clone.first, bf16[2,176,176]{2,1,0:T(8,128)(2,1)} %constant.55.clone.second, bf16[160,176]{1,0:T(8,128)(2,1)} %constant.56.clone.rows_inv, ...), custom_call_target="tpu_custom_call" | custom-call | tf_op jit(solution)/shard_map/pallas_call | solution.py:212
  130.2 0.9 fusion.41
  131.1 3.6 %collective-permute-start.4 = (f32[3,3,16]{2,1,0:T(4,128)S(1)}, f32[3,3,16]{2,1,0:T(4,128)S(1)}, u32[]{:S(2)}, u32[]{:S(2)}) collective-permute-start(f32[3,3,16]{2,1,0:T(4,128)S(1)} %get-tuple-element.22), channel_id=1, source_target_pairs={{0,32},{32,64},{64,96},{1,33},{33,65},{65,97},{2,34},{34,66},{66,9... | collective-permute-start | bytes 1736 | tf_op jit(solution)/shard_map/ppermute | solution.py:229
  134.7 1.9 %collective-permute-start.5 = (f32[3,3,16]{2,1,0:T(4,128)S(1)}, f32[3,3,16]{2,1,0:T(4,128)S(1)}, u32[]{:S(2)}, u32[]{:S(2)}) collective-permute-start(f32[3,3,16]{2,1,0:T(4,128)S(1)} %get-tuple-element.23), channel_id=1, source_target_pairs={{32,0},{64,32},{96,64},{33,1},{65,33},{97,65},{34,2},{66,34},{98,6... | collective-permute-start | bytes 1736 | tf_op jit(solution)/shard_map/ppermute | solution.py:232
  136.6 0.0 collective-permute-done.4
  136.6 2.4 %collective-permute-done.5 = f32[3,3,16]{2,1,0:T(4,128)S(1)} collective-permute-done((f32[3,3,16]{2,1,0:T(4,128)S(1)}, f32[3,3,16]{2,1,0:T(4,128)S(1)}, u32[]{:S(2)}, u32[]{:S(2)}) %collective-permute-start.5) | collective-permute-done | bytes 608 | tf_op jit(solution)/shard_map/ppermute | solution.py:232
  139.0 0.1 fusion.84
  139.1 3.2 %collective-permute-start.6 = (f32[3,18,3]{2,1,0:T(8,128)S(1)}, f32[3,18,3]{2,1,0:T(8,128)S(1)}, u32[]{:S(2)}, u32[]{:S(2)}) collective-permute-start(f32[3,18,3]{2,1,0:T(8,128)S(1)} %get-tuple-element.20), channel_id=1, source_target_pairs={{0,1},{1,2},{2,3},{3,4},{4,5},{5,6},{6,7},{7,8},{8,9},{9,10},{10,1... | collective-permute-start | bytes 1952 | tf_op jit(solution)/shard_map/ppermute | solution.py:229
  142.3 1.9 %collective-permute-start.7 = (f32[3,18,3]{2,1,0:T(8,128)S(1)}, f32[3,18,3]{2,1,0:T(8,128)S(1)}, u32[]{:S(2)}, u32[]{:S(2)}) collective-permute-start(f32[3,18,3]{2,1,0:T(8,128)S(1)} %get-tuple-element.21), channel_id=1, source_target_pairs={{1,0},{2,1},{3,2},{4,3},{5,4},{6,5},{7,6},{8,7},{9,8},{10,9},{11,1... | collective-permute-start | bytes 1952 | tf_op jit(solution)/shard_map/ppermute | solution.py:232
  144.2 0.6 copy.44
  144.8 0.0 collective-permute-done.6
  144.8 4.8 %collective-permute-done.7 = f32[3,18,3]{2,1,0:T(8,128)S(1)} collective-permute-done((f32[3,18,3]{2,1,0:T(8,128)S(1)}, f32[3,18,3]{2,1,0:T(8,128)S(1)}, u32[]{:S(2)}, u32[]{:S(2)}) %collective-permute-start.7) | collective-permute-done | bytes 680 | tf_op jit(solution)/shard_map/ppermute | solution.py:232
  149.7 0.1 pad_maximum_fusion.4
  149.8 0.1 slice.204
  149.9 0.1 slice.199
  150.0 0.1 slice.194
  150.0 0.1 fusion.38
  150.1 0.1 fusion.36
  150.2 0.1 fusion.34
  150.3 0.6 copy.45
  (10 shorter events, 0.1 us)
Async XLA Ops:
  0.6 2.0 %copy-start = (bf16[96,3200]{1,0:T(8,128)(2,1)S(1)}, bf16[96,3200]{1,0:T(8,128)(2,1)}, u32[]{:S(2)}) copy-start(bf16[96,3200]{1,0:T(8,128)(2,1)} %param.14) | copy-start | bytes 1843204
  11.1 34.9 %all-to-all-start = ((bf16[128,51,128]{2,1,0:T(8,128)(2,1)}), bf16[128,51,128]{2,1,0:T(8,128)(2,1)S(1)}, u32[]{:S(2)}, u32[]{:S(2)}) async-start(bf16[128,51,128]{2,1,0:T(8,128)(2,1)} %copy.39), calls=%async_computation | async-start | bytes 3670016 | tf_op jit(solution)/shard_map/all_to_all | solution.py:270
  63.1 17.1 %copy-start.1 = (s32[12,16]{1,0:T(8,128)S(1)}, s32[12,16]{1,0:T(8,128)}, u32[]{:S(2)}) copy-start(s32[12,16]{1,0:T(8,128)} %param.20) | copy-start | bytes 2308
  63.3 6.4 %collective-permute-start = (bf16[2,60,640]{2,1,0:T(8,128)(2,1)S(1)}, bf16[2,60,640]{2,1,0:T(8,128)(2,1)S(1)}, u32[]{:S(2)}, u32[]{:S(2)}) collective-permute-start(bf16[2,60,640]{2,1,0:T(8,128)(2,1)S(1)} %get-tuple-element.18), channel_id=1, source_target_pairs={{0,32},{32,64},{64,96},{1,33},{33,65},{65,97},{2,34},{34,66},{66,9... | collective-permute-start | bytes 460808 | tf_op jit(solution)/shard_map/ppermute | solution.py:229
  65.2 6.1 %collective-permute-start.1 = (bf16[2,60,640]{2,1,0:T(8,128)(2,1)S(1)}, bf16[2,60,640]{2,1,0:T(8,128)(2,1)S(1)}, u32[]{:S(2)}, u32[]{:S(2)}) collective-permute-start(bf16[2,60,640]{2,1,0:T(8,128)(2,1)S(1)} %get-tuple-element.19), channel_id=1, source_target_pairs={{32,0},{64,32},{96,64},{33,1},{65,33},{97,65},{34,2},{66,34},{98,6... | collective-permute-start | bytes 460808 | tf_op jit(solution)/shard_map/ppermute | solution.py:232
  71.6 10.3 %collective-permute-start.2 = (bf16[2,600,60]{2,1,0:T(8,128)(2,1)S(1)}, bf16[2,600,60]{2,1,0:T(8,128)(2,1)S(1)}, u32[]{:S(2)}, u32[]{:S(2)}) collective-permute-start(bf16[2,600,60]{2,1,0:T(8,128)(2,1)S(1)} %get-tuple-element.16), channel_id=1, source_target_pairs={{0,1},{1,2},{2,3},{3,4},{4,5},{5,6},{6,7},{7,8},{8,9},{9,10},{10,1... | collective-permute-start | bytes 432008 | tf_op jit(solution)/shard_map/ppermute | solution.py:229
  78.1 10.3 %collective-permute-start.3 = (bf16[2,600,60]{2,1,0:T(8,128)(2,1)S(1)}, bf16[2,600,60]{2,1,0:T(8,128)(2,1)S(1)}, u32[]{:S(2)}, u32[]{:S(2)}) collective-permute-start(bf16[2,600,60]{2,1,0:T(8,128)(2,1)S(1)} %get-tuple-element.17), channel_id=1, source_target_pairs={{1,0},{2,1},{3,2},{4,3},{5,4},{6,5},{7,6},{8,7},{9,8},{10,9},{11,1... | collective-permute-start | bytes 432008 | tf_op jit(solution)/shard_map/ppermute | solution.py:232
  131.1 5.5 %collective-permute-start.4 = (f32[3,3,16]{2,1,0:T(4,128)S(1)}, f32[3,3,16]{2,1,0:T(4,128)S(1)}, u32[]{:S(2)}, u32[]{:S(2)}) collective-permute-start(f32[3,3,16]{2,1,0:T(4,128)S(1)} %get-tuple-element.22), channel_id=1, source_target_pairs={{0,32},{32,64},{64,96},{1,33},{33,65},{65,97},{2,34},{34,66},{66,9... | collective-permute-start | bytes 1736 | tf_op jit(solution)/shard_map/ppermute | solution.py:229
  134.7 4.4 %collective-permute-start.5 = (f32[3,3,16]{2,1,0:T(4,128)S(1)}, f32[3,3,16]{2,1,0:T(4,128)S(1)}, u32[]{:S(2)}, u32[]{:S(2)}) collective-permute-start(f32[3,3,16]{2,1,0:T(4,128)S(1)} %get-tuple-element.23), channel_id=1, source_target_pairs={{32,0},{64,32},{96,64},{33,1},{65,33},{97,65},{34,2},{66,34},{98,6... | collective-permute-start | bytes 1736 | tf_op jit(solution)/shard_map/ppermute | solution.py:232
  139.1 5.7 %collective-permute-start.6 = (f32[3,18,3]{2,1,0:T(8,128)S(1)}, f32[3,18,3]{2,1,0:T(8,128)S(1)}, u32[]{:S(2)}, u32[]{:S(2)}) collective-permute-start(f32[3,18,3]{2,1,0:T(8,128)S(1)} %get-tuple-element.20), channel_id=1, source_target_pairs={{0,1},{1,2},{2,3},{3,4},{4,5},{5,6},{6,7},{7,8},{8,9},{9,10},{10,1... | collective-permute-start | bytes 1952 | tf_op jit(solution)/shard_map/ppermute | solution.py:229
  142.3 7.4 %collective-permute-start.7 = (f32[3,18,3]{2,1,0:T(8,128)S(1)}, f32[3,18,3]{2,1,0:T(8,128)S(1)}, u32[]{:S(2)}, u32[]{:S(2)}) collective-permute-start(f32[3,18,3]{2,1,0:T(8,128)S(1)} %get-tuple-element.21), channel_id=1, source_target_pairs={{1,0},{2,1},{3,2},{4,3},{5,4},{6,5},{7,6},{8,7},{9,8},{10,9},{11,1... | collective-permute-start | bytes 1952 | tf_op jit(solution)/shard_map/ppermute | solution.py:232

commit v2 on v1

--- a/solution.py
+++ b/solution.py
@@ -20,9 +20,16 @@
 GROUPS = 6
 BLOCKS = 11
 ROWS = 16 * BLOCKS
-IMG_H = 640
-IMG_W = 896
-FIRST_H = 608
+TILE_H = 40
+TILE_W = 80
+SPLIT = 128 - TILE_W
+LANES = 32
+SLOT_H = 56
+FRAME_H = 608
+FORM_H = 488
+EDGE_H = 64
+TOP = 56
+FIRST_H = FRAME_H
 
 stiffness = 1.0
 tiny = 1e-06
@@ -81,10 +88,10 @@
         select[512 + HALF * w + np.arange(HALF), 32 + w] = 1.0
         select[768 + lanes, 64 + w] = half[:, 0]
         select[1024 + lanes, 64 + w] = 1.0
-    window = np.zeros((IMG_W, 128))
-    for j in range(16):
+    window = np.zeros((256, 128))
+    for w in range(WIN):
         for kind in range(3):
-            window[STRIDE * j : STRIDE * j + PATCH, 32 * kind + j] = 1.0
+            window[STRIDE * w : STRIDE * w + PATCH, 32 * kind + w] = 1.0
     as_bf16 = lambda x: jnp.asarray(x.astype(jnp.bfloat16))
     return tuple(as_bf16(x) for x in (first, second, rows_inv, cols_even, cols_odd, select, window))
 
@@ -103,30 +110,83 @@
     )
 
 
-def window_norms(img_ref, cells_ref, window):
-    for c in range(8):
-        values = img_ref[80 * c : 80 * c + 80, :].astype(jnp.float32)
-        squares = (values * values).reshape(2, 5, 8, IMG_W).sum(axis=1)
-        sums = squares.sum(axis=1)
-        cells_ref[2 * c : 2 * c + 2, :] = sums
-    cells = cells_ref[...]
+def spread_groups(sums):
+    lane = lax.broadcasted_iota(jnp.int32, (16, 128), 1) % 32
+    total = sums[0]
+    for g in range(1, GROUPS):
+        piece = sums[g] if g < GROUPS - 1 else jnp.where(lane == 0, sums[g], 0.0)
+        total = total + pltpu.roll(piece, WIN * g, axis=1)
+    return total
+
+
+def window_means(grp, sec, cells, window):
     row = lax.broadcasted_iota(jnp.int32, (16, 16), 0)
     col = lax.broadcasted_iota(jnp.int32, (16, 16), 1)
     band = ((col >= row) & (col < row + 4)).astype(jnp.float32)
-    total = dot_exact(dot_exact(band, cells), window)
-    return total / (PATCH * PATCH) + tiny
+    for g in range(GROUPS):
+        for c in range(7):
+            values = grp[sec, g, 80 * c : 80 * c + 80, :].astype(jnp.float32)
+            squares = (values * values).reshape(2, 5, 8, 256).sum(axis=1)
+            cells[2 * c : 2 * c + 2, 256 * g : 256 * g + 256] = squares.sum(axis=1)
+        values = grp[sec, g, 560:608, :].astype(jnp.float32)[:40]
+        cells[14:15, 256 * g : 256 * g + 256] = (
+            (values * values).reshape(5, 8, 256).sum(axis=0).sum(axis=0, keepdims=True)
+        )
+    cells[15:16, :] = jnp.zeros((1, 256 * GROUPS), jnp.float32)
+    sums = dot_exact(band, cells[...])
+    stacked = jnp.concatenate([sums[:, 256 * g : 256 * g + 256] for g in range(GROUPS)], axis=0)
+    total = dot_exact(stacked, window).reshape(GROUPS, 16, 128)
+    return spread_groups(total) / (PATCH * PATCH) + tiny
+
+
+def pixel_places(sec, odd_group):
+    row = lax.broadcasted_iota(jnp.int32, (512, 256), 0)
+    col = lax.broadcasted_iota(jnp.int32, (512, 256), 1)
+    tile, lane = row // 128, row % 128
+    if sec == 0:
+        pixel = jnp.where(lane < TILE_W, lane, -1000)
+    else:
+        tail = jnp.where(lane < LANES, lane + SPLIT, -1000)
+        pixel = jnp.where(lane >= TILE_W, lane - TILE_W, tail)
+    offset = 20 + 40 * odd_group
+    return jnp.where((tile * TILE_W + pixel - offset == col) & (col < 240), 1.0, 0.0).astype(jnp.bfloat16)
+
+
+def gather_frame(form, top, bottom, left, right, frame):
+    for sec in range(2):
+        for c in range(10):
+            if 1 <= c <= 8:
+                t = c - 1
+                frame[sec, c, 0:TOP, :] = top[sec, t, 0:TOP, :]
+                frame[sec, c, TOP : TOP + FORM_H, :] = form[sec, t]
+                frame[sec, c, 544:600, :] = bottom[sec, t, 8:EDGE_H, :]
+                frame[sec, c, 600:608, :] = jnp.zeros((8, 128), jnp.bfloat16)
+                for dst, own, other in ((TOP, form[sec, t, 0:8, :], top[sec, t, TOP:EDGE_H, :]),
+                                        (536, form[sec, t, 480:488, :], bottom[sec, t, 0:8, :])):
+                    both = own.astype(jnp.float32) + other.astype(jnp.float32)
+                    frame[sec, c, dst : dst + 8, :] = both.astype(jnp.bfloat16)
+            else:
+                frame[sec, c] = (left if c == 0 else right)[sec]
 
 
 def correlate_kernel(
-    img_a, img_b, first, second, rows_inv, cols_even, cols_odd, select, window, out, fa, fb, cells, raw
+    form, top, bottom, left, right, first, second, rows_inv, cols_even, cols_odd, select, window,
+    out, frame, grp, fa, fb, cells, raw, cross,
 ):
+    gather_frame(form, top, bottom, left, right, frame)
+    for sec, dst in ((0, fa), (1, fb)):
+        for odd_group in range(2):
+            places = pixel_places(sec, odd_group)
+            for g in range(odd_group, GROUPS, 2):
+                c = 3 * (g // 2) + odd_group
+                count = min(4, 10 - c)
+                wide = jnp.concatenate([frame[sec, c + k] for k in range(count)], axis=1)
+                pixels = dot(wide, places[: 128 * count]).astype(jnp.bfloat16)
+                grp[sec, g] = pixels
+                dst[g] = dot(pixels, first[...]).astype(jnp.bfloat16)
     window_f32 = window[...].astype(jnp.float32)
-    mean_a = window_norms(img_a, cells, window_f32)
-    mean_b = window_norms(img_b, cells, window_f32)
-    for g in range(GROUPS):
-        lo = WIN * STRIDE * g
-        for img, dst in ((img_a, fa), (img_b, fb)):
-            dst[g] = dot(img[:FIRST_H, lo : lo + 256], first[...]).astype(jnp.bfloat16)
+    mean_a = window_means(grp, 0, cells, window_f32)
+    mean_b = window_means(grp, 1, cells, window_f32)
 
     sub = lax.broadcasted_iota(jnp.int32, (8, 256), 0)
     lane = lax.broadcasted_iota(jnp.int32, (8, 256), 1)
@@ -142,7 +202,7 @@
             total = total + (x[t, 0] + x[t, 1])
         return total + x[0, 1] + (x[0, 0] * (top_half2 if x.shape[-1] == 512 else top_half) + 0.5 * x[BLOCKS - 1, 0])
 
-    def one(g, q, parity):
+    def spectra(g, q, parity):
         start = pl.multiple_of(80 * q + 32 * parity, 16)
         spec = []
         for src in (fa, fb):
@@ -163,7 +223,11 @@
             [jnp.concatenate([dcc, dcs], axis=2), jnp.concatenate([dsc, dss], axis=2)], axis=1
         )
         weight = weighted_rows(d * d)
-        d16 = d.reshape(ROWS, 512).astype(jnp.bfloat16)
+        raw[g, pl.ds(2 * q + parity, 1), 768:1280] = jnp.sum(weight, axis=0, keepdims=True)
+        cross[parity] = d.reshape(ROWS, 512).astype(jnp.bfloat16)
+
+    def flows(g, q, parity):
+        d16 = cross[parity]
         inv = dot(rows_inv[...], d16)
         prod = (inv[:HALF] * inv[HALF:]).reshape(10, 8, 512)
         run = prod[9]
@@ -180,25 +244,23 @@
         i = 2 * q + parity
         raw[g, pl.ds(i, 1), 0:512] = jnp.sum(flow_y, axis=0, keepdims=True)
         raw[g, pl.ds(i, 1), 512:768] = jnp.sum(flow_x, axis=0, keepdims=True) * shift_x
-        raw[g, pl.ds(i, 1), 768:1280] = jnp.sum(weight, axis=0, keepdims=True)
 
     raw[:, 12:16, :] = jnp.zeros((GROUPS, 4, 1280), jnp.float32)
 
+    spectra(0, 0, 0)
+    spectra(0, 0, 1)
+
     def step(n, carry):
-        g = n // 6
-        q = n % 6
-        one(g, q, 0)
-        one(g, q, 1)
+        for parity in range(2):
+            flows((n - 1) // 6, (n - 1) % 6, parity)
+            spectra(n // 6, n % 6, parity)
         return carry
 
-    lax.fori_loop(0, GROUPS * 6, step, 0)
+    lax.fori_loop(1, GROUPS * 6, step, 0)
+    flows(GROUPS - 1, 5, 0)
+    flows(GROUPS - 1, 5, 1)
     sums = dot_exact(raw[...].reshape(GROUPS * 16, 1280), select[...].astype(jnp.float32))
-    sums = sums.reshape(GROUPS, 16, 128)
-    lane128 = lax.broadcasted_iota(jnp.int32, (16, 128), 1) % 32
-    total = sums[0]
-    for g in range(1, GROUPS):
-        piece = sums[g] if g < 5 else jnp.where(lane128 == 0, sums[g], 0.0)
-        total = total + pltpu.roll(piece, WIN * g, axis=1)
+    total = spread_groups(sums.reshape(GROUPS, 16, 128))
     scale = (1.0 / (PATCH * PATCH)) / (mean_a * mean_b)
     unit = (2.0 / (PATCH * PATCH)) ** 2 * HALF / (PATCH * PATCH)
     total = total * (scale * unit)
@@ -208,17 +270,148 @@
     out[...] = jnp.where(lane_all >= 64, weight, total) / down
 
 
-def correlate(img_a, img_b):
+def correlate(form, top, bottom, left, right):
     return pl.pallas_call(
         correlate_kernel,
         out_shape=jax.ShapeDtypeStruct((16, 128), jnp.float32),
         scratch_shapes=[
+            pltpu.VMEM((2, 10, FRAME_H, 128), jnp.bfloat16),
+            pltpu.VMEM((2, GROUPS, FRAME_H, 256), jnp.bfloat16),
             pltpu.VMEM((GROUPS, FIRST_H, 512), jnp.bfloat16),
             pltpu.VMEM((GROUPS, FIRST_H, 512), jnp.bfloat16),
-            pltpu.VMEM((16, IMG_W), jnp.float32),
+            pltpu.VMEM((16, 256 * GROUPS), jnp.float32),
             pltpu.VMEM((GROUPS, 16, 1280), jnp.float32),
+            pltpu.VMEM((2, ROWS, 512), jnp.bfloat16),
         ],
-    )(img_a, img_b, *tables())
+    )(form, top, bottom, left, right, *tables())
+
+
+def pack_kernel(a_tiles, b_tiles, a_owner, b_owner, a_offset, b_offset, out, rows):
+    count = a_tiles.shape[0]
+    owners = jnp.concatenate([a_owner[...], b_owner[...]], axis=1)
+    slot = lax.broadcasted_iota(jnp.int32, (128, 2 * count), 0)
+    select = jnp.where(slot == owners, 1.0, 0.0).astype(jnp.bfloat16)
+    zero = lambda width: jnp.zeros((count, width), jnp.bfloat16)
+
+    def position(offset):
+        row = offset[:, 0:1].astype(jnp.float32)
+        col = offset[:, 1:2].astype(jnp.float32)
+        code = row * (TX / TILE_H) + col * (1.0 / TILE_W) + 1.0
+        return jnp.floor(code + 0.5)
+
+    def piece(tiles, start, width):
+        return tiles[:, start : start + width]
+
+    lane = lax.broadcasted_iota(jnp.int32, (count, 128), 1)
+    code_a = jnp.where(lane == 64, position(a_offset), 0.0).astype(jnp.bfloat16)
+    code_b = jnp.where(lane == 96, position(b_offset), 0.0).astype(jnp.bfloat16)
+
+    def send_row(y):
+        if y < TILE_H:
+            a_part = jnp.concatenate([piece(a_tiles, TILE_W * y, TILE_W), zero(SPLIT)], axis=1)
+            b_part = jnp.concatenate([zero(TILE_W), piece(b_tiles, TILE_W * y, SPLIT)], axis=1)
+        elif y < TILE_H + 8:
+            u = y - TILE_H
+            a_part = zero(128)
+            b_part = jnp.concatenate(
+                [piece(b_tiles, TILE_W * (8 * k + u) + SPLIT, LANES) for k in range(4)], axis=1
+            )
+        else:
+            u = y - TILE_H - 8
+            a_part = code_a
+            b_part = jnp.concatenate(
+                [piece(b_tiles, TILE_W * (32 + u) + SPLIT, LANES), zero(96)], axis=1
+            )
+            b_part = b_part + code_b
+        return jnp.concatenate([a_part, b_part], axis=0)
+
+    for y in range(0, SLOT_H, 2):
+        both = jnp.concatenate([send_row(y), send_row(y + 1)], axis=1)
+        sent = dot(select, both)
+        rows[pl.ds(y, 128, stride=SLOT_H), :] = sent[:, :128]
+        rows[pl.ds(y + 1, 128, stride=SLOT_H), :] = sent[:, 128:]
+
+    def flush(n, carry):
+        start = pl.multiple_of(8 * SLOT_H * n, 8)
+        block = rows[pl.ds(start, 8 * SLOT_H), :].reshape(8, SLOT_H, 128)
+        out[pl.ds(8 * n, 8)] = block.astype(jnp.bfloat16)
+        return carry
+
+    lax.fori_loop(0, 16, flush, 0)
+
+
+def place_kernel(got, form, up, down, rows, plane_a, plane_b):
+    def widen(n, carry):
+        start = pl.multiple_of(8 * SLOT_H * n, 8)
+        block = got[pl.ds(8 * n, 8)].astype(jnp.float32)
+        rows[pl.ds(start, 8 * SLOT_H), :] = block.reshape(8 * SLOT_H, 128)
+        return carry
+
+    lax.fori_loop(0, 16, widen, 0)
+    codes = rows[pl.ds(TILE_H + 8, 128, stride=SLOT_H), :]
+    wanted = lax.broadcasted_iota(jnp.int32, (128, 128), 1).astype(jnp.float32) + 1.0
+    pick = lambda col: jnp.where(codes[:, col : col + 1] == wanted, 1.0, 0.0).T[:96]
+    select_a = pick(64)
+    select_b = pick(96)
+    select = jnp.concatenate([select_a, select_b], axis=0).astype(jnp.bfloat16)
+    select_b = select_b.astype(jnp.bfloat16)
+
+    def slot_row(y):
+        return rows[pl.ds(y, 128, stride=SLOT_H), :].astype(jnp.bfloat16)
+
+    for plane in (plane_a, plane_b):
+        for t in range(TX):
+            plane[FORM_H * t : FORM_H * t + 8, :] = jnp.zeros((8, 128), jnp.float32)
+            plane[FORM_H * t + 480 : FORM_H * t + 488, :] = jnp.zeros((8, 128), jnp.float32)
+    lane = lax.broadcasted_iota(jnp.int32, (96, 128), 1)
+    tail = lane < LANES
+
+    for u in range(0, 8, 2):
+        tails = jnp.concatenate([slot_row(TILE_H + u + v + w) for v in range(2) for w in (0, 8)], axis=1)
+        tails = dot(select_b, tails)
+        mains = {}
+        for k in range(5):
+            y = 8 * k + u
+            main = dot(select, jnp.concatenate([slot_row(y), slot_row(y + 1)], axis=1))
+            for v in range(2):
+                part_a = main[:96, 128 * v : 128 * v + 128]
+                part_b = main[96:, 128 * v : 128 * v + 128]
+                rest = tails[:, 256 * v : 256 * v + 128] if k < 4 else tails[:, 256 * v + 128 : 256 * v + 256]
+                if 0 < k < 4:
+                    rest = pltpu.roll(rest, 128 - LANES * k, axis=1)
+                part_b = jnp.where(tail, rest, part_b)
+                for ty in range(TY):
+                    where = pl.ds(TILE_H * ty + y + v + 4, TX, stride=FORM_H)
+                    plane_a[where, :] = part_a[TX * ty : TX * ty + TX]
+                    plane_b[where, :] = part_b[TX * ty : TX * ty + TX]
+
+    for sec, plane in ((0, plane_a), (1, plane_b)):
+        for t in range(TX):
+            block = plane[FORM_H * t : FORM_H * t + FORM_H, :].astype(jnp.bfloat16)
+            form[sec, t] = block
+            up[sec, t] = plane[FORM_H * t : FORM_H * t + EDGE_H, :].astype(jnp.bfloat16)
+            down[sec, t] = plane[FORM_H * t + 424 : FORM_H * t + 488, :].astype(jnp.bfloat16)
+
+
+def pack(a_tiles, b_tiles, a_owner, b_owner, a_offset, b_offset):
+    return pl.pallas_call(
+        pack_kernel,
+        out_shape=jax.ShapeDtypeStruct((128, SLOT_H, 128), jnp.bfloat16),
+        scratch_shapes=[pltpu.VMEM((128 * SLOT_H, 128), jnp.float32)],
+    )(a_tiles, b_tiles, a_owner[None], b_owner[None], a_offset, b_offset)
+
+
+def place(got):
+    edge = jax.ShapeDtypeStruct((2, TX, EDGE_H, 128), jnp.bfloat16)
+    return pl.pallas_call(
+        place_kernel,
+        out_shape=(jax.ShapeDtypeStruct((2, TX, FORM_H, 128), jnp.bfloat16), edge, edge),
+        scratch_shapes=[
+            pltpu.VMEM((128 * SLOT_H, 128), jnp.float32),
+            pltpu.VMEM((TX * FORM_H, 128), jnp.float32),
+            pltpu.VMEM((TX * FORM_H, 128), jnp.float32),
+        ],
+    )(got)
 
 
 def extended_2(block, sides, width):
@@ -234,50 +427,31 @@
     return block
 
 
-def outgoing(tiles, tile_owner, tile_offset, slot_count, tile_h, tile_w):
-    select = (jnp.arange(slot_count, dtype=jnp.int32)[:, None] == tile_owner[None, :]).astype(
-        jnp.bfloat16
-    )
-    position = tile_offset[:, 0] // tile_h * TX + tile_offset[:, 1] // tile_w + 1
-    sent_tiles = jnp.dot(select, tiles, preferred_element_type=jnp.float32).astype(jnp.bfloat16)
-    slot_code = jnp.dot(
-        select, position.astype(jnp.bfloat16)[:, None], preferred_element_type=jnp.float32
-    ).astype(jnp.bfloat16)
-    return (sent_tiles, slot_code)
-
-
-def incoming(received, slot_code, tile_count, tile_h, tile_w):
-    wanted = jnp.arange(1, tile_count + 1, dtype=jnp.int32).astype(jnp.float32)
-    select = (slot_code.astype(jnp.float32)[None, :] == wanted[:, None]).astype(jnp.bfloat16)
-    blocks = jnp.dot(select, received, preferred_element_type=jnp.float32).astype(jnp.bfloat16)
+def shifted(block, axis, step):
+    count = lax.axis_size(axis)
+    pairs = [(i, i + step) for i in range(count) if 0 <= i + step < count]
+    return lax.ppermute(block, axis, pairs)
+
+
+def column(form, top, bottom, t):
+    grow = lambda x, low, high: jnp.pad(x[:, t], ((0, 0), (low, high), (0, 0)))
     return (
-        blocks.reshape(TY, TX, tile_h, tile_w)
-        .transpose(0, 2, 1, 3)
-        .reshape(TY * tile_h, TX * tile_w)
+        grow(form, TOP, FRAME_H - TOP - FORM_H)
+        + grow(top, 0, FRAME_H - EDGE_H)
+        + grow(bottom, 536, FRAME_H - 536 - EDGE_H)
     )
 
 
 def per_device(a_tiles, a_owner, a_offset, b_tiles, b_owner, b_offset, patch_valid):
     grid_rows, grid_cols = patch_valid.shape
-    tile_h = grid_rows * STRIDE // TY
-    tile_w = grid_cols * STRIDE // TX
-    tile_count, tile_size = a_tiles.shape
-    devices = lax.axis_size("row") * lax.axis_size("col")
-    send_a, code_a = outgoing(a_tiles, a_owner, a_offset, devices, tile_h, tile_w)
-    send_b, code_b = outgoing(b_tiles, b_owner, b_offset, devices, tile_h, tile_w)
-    code = jnp.pad(jnp.concatenate([code_a, code_b], axis=1), ((0, 0), (0, 126)))
-    packed = jnp.concatenate([send_a, send_b, code], axis=1).reshape(devices, 51, 128)
+    packed = pack(a_tiles, b_tiles, a_owner, b_owner, a_offset, b_offset)
     got = lax.all_to_all(packed, ("row", "col"), split_axis=0, concat_axis=0, tiled=True)
-    got_a = got[:, :25].reshape(devices, tile_size)
-    got_b = got[:, 25:50].reshape(devices, tile_size)
-    canvas_a = incoming(got_a, got[:, 50, 0], tile_count, tile_h, tile_w)
-    canvas_b = incoming(got_b, got[:, 50, 1], tile_count, tile_h, tile_w)
-    images = jnp.stack([canvas_a, canvas_b])
-    padded = extended_2(images, (("row", 1), ("col", 2)), MARGIN)
-    padded = jnp.pad(
-        padded, ((0, 0), (0, IMG_H - padded.shape[1]), (0, IMG_W - padded.shape[2]))
-    )
-    result = correlate(padded[0], padded[1])
+    form, up, down = place(got)
+    top = shifted(down, "row", 1)
+    bottom = shifted(up, "row", -1)
+    left = shifted(column(form, top, bottom, TX - 1), "col", 1)
+    right = shifted(column(form, top, bottom, 0), "col", -1)
+    result = correlate(form, top, bottom, left, right)
     flow_field = jnp.stack([result[:grid_rows, :grid_cols], result[:grid_rows, 32 : 32 + grid_cols]])
     confidence = result[:grid_rows, 64 : 64 + grid_cols]
     valid_float = patch_valid.astype(jnp.float32)
@@ -286,10 +460,10 @@
     fields = jnp.concatenate([start, (strength + 4.0 * stiffness)[None]])
     fields = extended_2(fields, (("row", 1), ("col", 2)), SWEEPS)
     mesh = fields[:2]
-    down = fields[2]
-    inside = down > 0.0
-    rest = jnp.where(inside, 1.0 / jnp.where(inside, down, 1.0), 0.0)
-    pull = mesh * jnp.where(inside, down - 4.0 * stiffness, 0.0)
+    below = fields[2]
+    inside = below > 0.0
+    rest = jnp.where(inside, 1.0 / jnp.where(inside, below, 1.0), 0.0)
+    pull = mesh * jnp.where(inside, below - 4.0 * stiffness, 0.0)
     for sweep_index in range(SWEEPS):
         around = mesh[:, :-2, 1:-1] + mesh[:, 2:, 1:-1] + mesh[:, 1:-1, :-2] + mesh[:, 1:-1, 2:]
         rest = rest[1:-1, 1:-1]

time: 152 us -> 128 us (0.84)
  blocking collectives: 0 us -> 35 us
  waiting for transfers between devices: 42.6 us -> 13.6 us
  local copies, waits for them, and re-layouts: 21.8 us -> 9.54 us
  matrix products: 7.17 us -> 0 us
  starting transfers between devices: 35 us -> 28.7 us
  other arithmetic: 4.98 us -> 1.33 us
    all_to_all x0 -> x1, blocking collectives: none -> 35 us  [per_device(): lax.all_to_all(packed, ('row', 'col'), split_axis=0, concat_axis=0, tiled...]
    all_to_all x1 -> x0, waiting for transfers between devices: 24.4 us -> none  [per_device(): lax.all_to_all(packed, ('row', 'col'), split_axis=0, concat_axis=0, tiled...]
    ppermute x0 -> x4, starting transfers between devices: none -> 13.6 us  [shifted(): return lax.ppermute(block, axis, pairs)]
    all_to_all x1 -> x0, starting transfers between devices: 10.5 us -> none  [per_device(): lax.all_to_all(packed, ('row', 'col'), split_axis=0, concat_axis=0, tiled...]
    pallas_call x0 -> x2, Pallas kernels: none -> 9 us  [the longest x1 4.92 us: place(): pl.pallas_call(place_kernel, out_shape=(jax.ShapeDtypeStruct((2, TX, FORM...]
    pallas_call x1, Pallas kernels: 38.4 us -> 29.9 us  [correlate(): pl.pallas_call(correlate_kernel, out_shape=jax.ShapeDtypeStruct((16, 128)...]
    ppermute x4 -> x2, waiting for transfers between devices: 15.5 us -> 7.28 us  [extended_2(): lax.ppermute(lax.slice_in_dim(block, 0, width, axis=dim), axis, backward)]
    reshape x5 -> x0, local copies, waits for them, and re-layouts: 8.18 us -> none  [the longest x4 4.56 us: incoming(): blocks.reshape(TY, TX, tile_h, tile_w).transpose(0, 2, 1, 3)]
  transfers between devices with their start and end apart: 9 -> 8, of which waited for: 7 -> 6; matrix products, arithmetic and copies ran while one was open for 0% -> 3% of each run, Pallas kernels for 0% -> 0%
where the time goes in v2:
time: 128 us
  Pallas kernels  38.9 us (30%)
  blocking collectives  35 us (27%)
  starting transfers between devices  28.7 us (22%)
  waiting for transfers between devices  13.6 us (11%)
  local copies, waits for them, and re-layouts  9.54 us (7%)
  other arithmetic  1.33 us (1%)
    all_to_all x1, blocking collectives, per_device(): lax.all_to_all(packed, ('row', 'col'), split_axis=0, concat_axis=0, tiled...  35 us
    pallas_call x1, Pallas kernels, correlate(): pl.pallas_call(correlate_kernel, out_shape=jax.ShapeDtypeStruct((16, 128)...  29.9 us
    ppermute x4, starting transfers between devices, shifted(): return lax.ppermute(block, axis, pairs)  13.6 us
    ppermute x2, starting transfers between devices, extended_2(): lax.ppermute(lax.slice_in_dim(block, block.shape[dim] - width, None, axis...  11.3 us
    ppermute x2, waiting for transfers between devices, extended_2(): lax.ppermute(lax.slice_in_dim(block, 0, width, axis=dim), axis, backward)  7.28 us
    ppermute x4, waiting for transfers between devices, shifted(): return lax.ppermute(block, axis, pairs)  6.28 us
    pallas_call x1, Pallas kernels, place(): pl.pallas_call(place_kernel, out_shape=(jax.ShapeDtypeStruct((2, TX, FORM...  4.92 us
    unnamed x10, local copies, waits for them, and re-layouts  4.72 us
  transfers between devices with their start and end apart: 8, of which 6 were waited for; matrix products, arithmetic and copies ran while one was open for 3% of the time, Pallas kernels for 0%

profile of v2, /device:TPU:27, one launch (start us, length us, event | category | flops | bytes accessed | tf_op | source)
XLA Modules:
  0.0 127.9 jit_solution(9038817825944159909)
XLA Ops:
  0.6 1.4 %copy.16.a_offset = s32[96,2]{1,0:T(8,128)} copy(s32[96,2]{0,1:T(2,128)} %param.16) | data formatting | bytes 1536 | tf_op args[2]
  2.0 1.4 %copy.17.b_offset = s32[96,2]{1,0:T(8,128)} copy(s32[96,2]{0,1:T(2,128)} %param.19) | data formatting | bytes 1536 | tf_op args[5]
  3.4 4.1 %shard_map.149 = bf16[128,56,128]{2,1,0:T(8,128)(2,1)} custom-call(bf16[96,3200]{1,0:T(8,128)(2,1)} %a_tiles.1, bf16[96,3200]{1,0:T(8,128)(2,1)} %b_tiles.1, s32[1,96]{1,0:T(1,128)} %bitcast.24, s32[1,96]{1,0:T(1,128)} %bitcast.25, s32[96,2]{1,0:T(8,128)} %copy.16.a_offset, s32[96,2]{1,0:T(8,128)} %copy.17.b_offset), custom_call_target="tpu_custom_call" | custom-call | tf_op jit(solution)/shard_map/pallas_call | solution.py:397
  7.5 35.0 %all_to_all.5.got = bf16[128,56,128]{2,1,0:T(8,128)(2,1)} all-to-all(bf16[128,56,128]{2,1,0:T(8,128)(2,1)} %shard_map.149), channel_id=1, replica_groups=mesh['row'=4,'col'=32] {'row','col'}, dimensions={0} | all-to-all | bytes 3670016 | tf_op jit(solution)/shard_map/all_to_all | solution.py:448
  42.5 4.9 %shard_map.150 = (bf16[2,8,488,128]{3,2,1,0:T(8,128)(2,1)}, bf16[2,8,64,128]{3,2,1,0:T(8,128)(2,1)}, bf16[2,8,64,128]{3,2,1,0:T(8,128)(2,1)}) custom-call(bf16[128,56,128]{2,1,0:T(8,128)(2,1)} %all_to_all.5.got), custom_call_target="tpu_custom_call" | custom-call | tf_op jit(solution)/shard_map/pallas_call | solution.py:406
  47.5 0.0 copy-start.2
  47.5 1.0 copy.18
  48.4 2.0 %collective-permute-start = (bf16[2,8,64,128]{3,2,0,1:T(8,128)(2,1)S(1)}, bf16[2,8,64,128]{3,2,0,1:T(8,128)(2,1)S(1)}, u32[]{:S(2)}, u32[]{:S(2)}) collective-permute-start(bf16[2,8,64,128]{3,2,0,1:T(8,128)(2,1)S(1)} %copy.18), channel_id=1, source_target_pairs={{0,32},{32,64},{64,96},{1,33},{33,65},{65,97},{2,34},{34,66},{66,9... | collective-permute-start | bytes 786440 | tf_op jit(solution)/shard_map/ppermute | solution.py:433
  50.5 1.0 copy.19
  51.4 3.3 %collective-permute-start.1 = (bf16[2,8,64,128]{3,2,0,1:T(8,128)(2,1)S(1)}, bf16[2,8,64,128]{3,2,0,1:T(8,128)(2,1)S(1)}, u32[]{:S(2)}, u32[]{:S(2)}) collective-permute-start(bf16[2,8,64,128]{3,2,0,1:T(8,128)(2,1)S(1)} %copy.19), channel_id=1, source_target_pairs={{32,0},{64,32},{96,64},{33,1},{65,33},{97,65},{34,2},{66,34},{98,6... | collective-permute-start | bytes 786440 | tf_op jit(solution)/shard_map/ppermute | solution.py:433
  54.7 1.1 slice_bitcast_fusion
  55.8 1.1 collective-permute-done
  57.0 2.8 %collective-permute-done.1 = bf16[2,8,64,128]{3,2,0,1:T(8,128)(2,1)S(1)} collective-permute-done((bf16[2,8,64,128]{3,2,0,1:T(8,128)(2,1)S(1)}, bf16[2,8,64,128]{3,2,0,1:T(8,128)(2,1)S(1)}, u32[]{:S(2)}, u32[]{:S(2)}) %collective-permute-start.1) | collective-permute-done | bytes 262176 | tf_op jit(solution)/shard_map/ppermute | solution.py:433
  59.8 4.2 %collective-permute-start.3 = (bf16[2,608,128]{2,1,0:T(8,128)(2,1)S(1)}, bf16[2,608,128]{2,1,0:T(8,128)(2,1)S(1)}, u32[]{:S(2)}, u32[]{:S(2)}) collective-permute-start(bf16[2,608,128]{2,1,0:T(8,128)(2,1)S(1)} %pad_add_fusion), channel_id=1, source_target_pairs={{1,0},{2,1},{3,2},{4,3},{5,4},{6,5},{7,6},{8,7},{9,8},{10,9},{11,1... | collective-permute-start | bytes 933896 | tf_op jit(solution)/shard_map/ppermute | solution.py:433
  64.0 4.1 %collective-permute-start.2 = (bf16[2,608,128]{2,1,0:T(8,128)(2,1)S(1)}, bf16[2,608,128]{2,1,0:T(8,128)(2,1)S(1)}, u32[]{:S(2)}, u32[]{:S(2)}) collective-permute-start(bf16[2,608,128]{2,1,0:T(8,128)(2,1)S(1)} %pad_add_fusion.1), channel_id=1, source_target_pairs={{0,1},{1,2},{2,3},{3,4},{4,5},{5,6},{6,7},{7,8},{8,9},{9,10},{10,1... | collective-permute-start | bytes 933896 | tf_op jit(solution)/shard_map/ppermute | solution.py:433
  68.2 0.0 copy-done.2
  68.2 0.7 copy.22.top
  68.9 0.7 copy.23.bottom
  69.7 1.1 collective-permute-done.3.right
  70.8 0.0 copy-start
  70.8 1.2 collective-permute-done.2.left
  72.0 0.0 copy-done
  72.0 0.0 copy-start.1
  72.0 0.7 copy-done.1
  72.7 29.9 %shard_map.151 = f32[16,128]{1,0:T(8,128)} custom-call(bf16[2,8,488,128]{3,2,1,0:T(8,128)(2,1)} %get-tuple-element.5.form, bf16[2,8,64,128]{3,2,1,0:T(8,128)(2,1)} %copy.22.top, bf16[2,8,64,128]{3,2,1,0:T(8,128)(2,1)} %copy.23.bottom, bf16[2,608,128]{2,1,0:T(8,128)(2,1)} %copy-done.1, bf16[2,608,128]{2,1,0:T(8,128)(2,1)} %copy-done, ...), custom_call_target="tpu_custom_call" | custom-call | tf_op jit(solution)/shard_map/pallas_call | solution.py:274
  102.6 0.9 fusion.8
  103.5 3.4 %collective-permute-start.4 = (f32[3,3,16]{2,1,0:T(4,128)S(1)}, f32[3,3,16]{2,1,0:T(4,128)S(1)}, u32[]{:S(2)}, u32[]{:S(2)}) collective-permute-start(f32[3,3,16]{2,1,0:T(4,128)S(1)} %get-tuple-element.18), channel_id=1, source_target_pairs={{0,32},{32,64},{64,96},{1,33},{33,65},{65,97},{2,34},{34,66},{66,9... | collective-permute-start | bytes 1736 | tf_op jit(solution)/shard_map/ppermute | solution.py:422
  106.9 1.9 %collective-permute-start.5 = (f32[3,3,16]{2,1,0:T(4,128)S(1)}, f32[3,3,16]{2,1,0:T(4,128)S(1)}, u32[]{:S(2)}, u32[]{:S(2)}) collective-permute-start(f32[3,3,16]{2,1,0:T(4,128)S(1)} %get-tuple-element.19), channel_id=1, source_target_pairs={{32,0},{64,32},{96,64},{33,1},{65,33},{97,65},{34,2},{66,34},{98,6... | collective-permute-start | bytes 1736 | tf_op jit(solution)/shard_map/ppermute | solution.py:425
  108.8 0.0 collective-permute-done.4
  108.8 2.4 %collective-permute-done.5 = f32[3,3,16]{2,1,0:T(4,128)S(1)} collective-permute-done((f32[3,3,16]{2,1,0:T(4,128)S(1)}, f32[3,3,16]{2,1,0:T(4,128)S(1)}, u32[]{:S(2)}, u32[]{:S(2)}) %collective-permute-start.5) | collective-permute-done | bytes 608 | tf_op jit(solution)/shard_map/ppermute | solution.py:425
  111.3 0.1 fusion.9
  111.3 7.9 %collective-permute-start.6 = (f32[3,18,3]{2,1,0:T(8,128)S(1)}, f32[3,18,3]{2,1,0:T(8,128)S(1)}, u32[]{:S(2)}, u32[]{:S(2)}) collective-permute-start(f32[3,18,3]{2,1,0:T(8,128)S(1)} %get-tuple-element.16), channel_id=1, source_target_pairs={{0,1},{1,2},{2,3},{3,4},{4,5},{5,6},{6,7},{7,8},{8,9},{9,10},{10,1... | collective-permute-start | bytes 1952 | tf_op jit(solution)/shard_map/ppermute | solution.py:422
  119.2 1.9 %collective-permute-start.7 = (f32[3,18,3]{2,1,0:T(8,128)S(1)}, f32[3,18,3]{2,1,0:T(8,128)S(1)}, u32[]{:S(2)}, u32[]{:S(2)}) collective-permute-start(f32[3,18,3]{2,1,0:T(8,128)S(1)} %get-tuple-element.17), channel_id=1, source_target_pairs={{1,0},{2,1},{3,2},{4,3},{5,4},{6,5},{7,6},{8,7},{9,8},{10,9},{11,1... | collective-permute-start | bytes 1952 | tf_op jit(solution)/shard_map/ppermute | solution.py:425
  121.2 0.6 copy.24
  121.8 0.0 collective-permute-done.6
  121.8 4.8 %collective-permute-done.7 = f32[3,18,3]{2,1,0:T(8,128)S(1)} collective-permute-done((f32[3,18,3]{2,1,0:T(8,128)S(1)}, f32[3,18,3]{2,1,0:T(8,128)S(1)}, u32[]{:S(2)}, u32[]{:S(2)}) %collective-permute-start.7) | collective-permute-done | bytes 680 | tf_op jit(solution)/shard_map/ppermute | solution.py:425
  126.6 0.1 pad_maximum_fusion.1
  126.8 0.1 slice.160
  126.8 0.1 slice.165
  126.9 0.1 slice.170
  127.0 0.1 fusion.5
  127.1 0.1 fusion.3
  127.2 0.1 fusion.1
  127.3 0.6 copy.25
  (11 shorter events, 0.1 us)
Async XLA Ops:
  47.5 20.7 %copy-start.2 = (s32[12,16]{1,0:T(8,128)S(1)}, s32[12,16]{1,0:T(8,128)}, u32[]{:S(2)}) copy-start(s32[12,16]{1,0:T(8,128)} %param.20) | copy-start | bytes 2308
  48.4 8.5 %collective-permute-start = (bf16[2,8,64,128]{3,2,0,1:T(8,128)(2,1)S(1)}, bf16[2,8,64,128]{3,2,0,1:T(8,128)(2,1)S(1)}, u32[]{:S(2)}, u32[]{:S(2)}) collective-permute-start(bf16[2,8,64,128]{3,2,0,1:T(8,128)(2,1)S(1)} %copy.18), channel_id=1, source_target_pairs={{0,32},{32,64},{64,96},{1,33},{33,65},{65,97},{2,34},{34,66},{66,9... | collective-permute-start | bytes 786440 | tf_op jit(solution)/shard_map/ppermute | solution.py:433
  51.4 8.3 %collective-permute-start.1 = (bf16[2,8,64,128]{3,2,0,1:T(8,128)(2,1)S(1)}, bf16[2,8,64,128]{3,2,0,1:T(8,128)(2,1)S(1)}, u32[]{:S(2)}, u32[]{:S(2)}) collective-permute-start(bf16[2,8,64,128]{3,2,0,1:T(8,128)(2,1)S(1)} %copy.19), channel_id=1, source_target_pairs={{32,0},{64,32},{96,64},{33,1},{65,33},{97,65},{34,2},{66,34},{98,6... | collective-permute-start | bytes 786440 | tf_op jit(solution)/shard_map/ppermute | solution.py:433
  59.8 11.0 %collective-permute-start.3 = (bf16[2,608,128]{2,1,0:T(8,128)(2,1)S(1)}, bf16[2,608,128]{2,1,0:T(8,128)(2,1)S(1)}, u32[]{:S(2)}, u32[]{:S(2)}) collective-permute-start(bf16[2,608,128]{2,1,0:T(8,128)(2,1)S(1)} %pad_add_fusion), channel_id=1, source_target_pairs={{1,0},{2,1},{3,2},{4,3},{5,4},{6,5},{7,6},{8,7},{9,8},{10,9},{11,1... | collective-permute-start | bytes 933896 | tf_op jit(solution)/shard_map/ppermute | solution.py:433
  64.0 8.0 %collective-permute-start.2 = (bf16[2,608,128]{2,1,0:T(8,128)(2,1)S(1)}, bf16[2,608,128]{2,1,0:T(8,128)(2,1)S(1)}, u32[]{:S(2)}, u32[]{:S(2)}) collective-permute-start(bf16[2,608,128]{2,1,0:T(8,128)(2,1)S(1)} %pad_add_fusion.1), channel_id=1, source_target_pairs={{0,1},{1,2},{2,3},{3,4},{4,5},{5,6},{6,7},{7,8},{8,9},{9,10},{10,1... | collective-permute-start | bytes 933896 | tf_op jit(solution)/shard_map/ppermute | solution.py:433
  70.8 1.2 copy-start
  72.0 0.7 copy-start.1
  103.5 5.3 %collective-permute-start.4 = (f32[3,3,16]{2,1,0:T(4,128)S(1)}, f32[3,3,16]{2,1,0:T(4,128)S(1)}, u32[]{:S(2)}, u32[]{:S(2)}) collective-permute-start(f32[3,3,16]{2,1,0:T(4,128)S(1)} %get-tuple-element.18), channel_id=1, source_target_pairs={{0,32},{32,64},{64,96},{1,33},{33,65},{65,97},{2,34},{34,66},{66,9... | collective-permute-start | bytes 1736 | tf_op jit(solution)/shard_map/ppermute | solution.py:422
  106.9 4.4 %collective-permute-start.5 = (f32[3,3,16]{2,1,0:T(4,128)S(1)}, f32[3,3,16]{2,1,0:T(4,128)S(1)}, u32[]{:S(2)}, u32[]{:S(2)}) collective-permute-start(f32[3,3,16]{2,1,0:T(4,128)S(1)} %get-tuple-element.19), channel_id=1, source_target_pairs={{32,0},{64,32},{96,64},{33,1},{65,33},{97,65},{34,2},{66,34},{98,6... | collective-permute-start | bytes 1736 | tf_op jit(solution)/shard_map/ppermute | solution.py:425
  111.3 10.5 %collective-permute-start.6 = (f32[3,18,3]{2,1,0:T(8,128)S(1)}, f32[3,18,3]{2,1,0:T(8,128)S(1)}, u32[]{:S(2)}, u32[]{:S(2)}) collective-permute-start(f32[3,18,3]{2,1,0:T(8,128)S(1)} %get-tuple-element.16), channel_id=1, source_target_pairs={{0,1},{1,2},{2,3},{3,4},{4,5},{5,6},{6,7},{7,8},{8,9},{9,10},{10,1... | collective-permute-start | bytes 1952 | tf_op jit(solution)/shard_map/ppermute | solution.py:422
  119.2 7.4 %collective-permute-start.7 = (f32[3,18,3]{2,1,0:T(8,128)S(1)}, f32[3,18,3]{2,1,0:T(8,128)S(1)}, u32[]{:S(2)}, u32[]{:S(2)}) collective-permute-start(f32[3,18,3]{2,1,0:T(8,128)S(1)} %get-tuple-element.17), channel_id=1, source_target_pairs={{1,0},{2,1},{3,2},{4,3},{5,4},{6,5},{7,6},{8,7},{9,8},{10,9},{11,1... | collective-permute-start | bytes 1952 | tf_op jit(solution)/shard_map/ppermute | solution.py:425

commit v3 on v2

--- a/solution.py
+++ b/solution.py
@@ -18,8 +18,7 @@
 FREQ = HALF + 1
 WIN = 3
 GROUPS = 6
-BLOCKS = 11
-ROWS = 16 * BLOCKS
+ROWS = PATCH
 TILE_H = 40
 TILE_W = 80
 SPLIT = 128 - TILE_W
@@ -29,6 +28,7 @@
 FORM_H = 488
 EDGE_H = 64
 TOP = 56
+TMAJOR = True
 FIRST_H = FRAME_H
 
 stiffness = 1.0
@@ -52,40 +52,32 @@
         rows = slice(STRIDE * w, STRIDE * w + PATCH)
         first[rows, FREQ * w : FREQ * (w + 1)] = cosine.T
         first[rows, 256 + FREQ * w : 256 + FREQ * (w + 1)] = sine.T
-    cos_pad = np.zeros((8 * BLOCKS, PATCH))
-    sin_pad = np.zeros((8 * BLOCKS, PATCH))
-    cos_pad[:FREQ] = cosine
-    sin_pad[:FREQ] = sine
-    mixed = np.stack([cos_pad.reshape(BLOCKS, 8, PATCH), sin_pad.reshape(BLOCKS, 8, PATCH)], 1)
-    mixed = mixed.reshape(ROWS, PATCH)
-    second = np.zeros((2, ROWS, ROWS))
-    second[0, :, :PATCH] = mixed
-    second[1, :, 8 : 8 + PATCH] = mixed
+    mixed = np.concatenate([cosine[HALF:], sine[1:HALF], cosine[:HALF]])
+    second = np.zeros((2, ROWS, 176))
+    for parity in range(2):
+        second[parity, :, 8 * parity : 8 * parity + PATCH] = mixed
     half = np.ones((FREQ, 1))
     half[0] = half[HALF] = 0.5
-    even = (cosine * half)[:, :HALF].copy()
-    even[:, 0] = (cosine * half)[:, HALF]
-    odd = sine[:, :HALF].copy()
-    rows_inv = np.zeros((PATCH, BLOCKS, 2, 8))
-    even_pad = np.zeros((8 * BLOCKS, HALF))
-    odd_pad = np.zeros((8 * BLOCKS, HALF))
-    even_pad[:FREQ] = even
-    odd_pad[:FREQ] = odd
-    rows_inv[:HALF, :, 0] = even_pad.T.reshape(HALF, BLOCKS, 8)
-    rows_inv[HALF:, :, 1] = odd_pad.T.reshape(HALF, BLOCKS, 8)
-    rows_inv[HALF, :, 0] = even_pad.T.reshape(HALF, BLOCKS, 8)[0]
-    rows_inv = rows_inv.reshape(PATCH, ROWS)
-    cols_even = np.zeros((256, 256))
-    cols_odd = np.zeros((256, 256))
+    shift = np.where(np.arange(PATCH) < HALF, np.arange(PATCH), np.arange(PATCH) - PATCH) * (16.0 / PATCH)
+    shift[HALF] = 0.0
+    rounded = lambda x: x.astype(jnp.bfloat16).astype(np.float64)
+    mix = 2.0 * half * ((rounded(cosine) * shift) @ rounded(sine).T)
+    sign = half[:, 0] * cosine[:, HALF]
+    mix_rows = np.zeros((HALF + 8, ROWS))
+    mix_rows[:FREQ, 1:HALF] = mix[:, 1:HALF]
+    mix_rows[FREQ, HALF:] = sign[:HALF]
+    mix_rows[FREQ, 0] = sign[HALF]
+    mix_cols = np.zeros((256, 256))
+    sign_cols = np.zeros((16, 256))
     for w in range(WIN):
-        cols_even[FREQ * w : FREQ * (w + 1), HALF * w : HALF * (w + 1)] = even
-        cols_odd[FREQ * w : FREQ * (w + 1), HALF * w : HALF * (w + 1)] = odd
+        mix_cols[FREQ * w : FREQ * (w + 1), FREQ * w : FREQ * (w + 1)] = mix.T
+        sign_cols[w, FREQ * w : FREQ * (w + 1)] = sign
     select = np.zeros((1280, 128))
     for w in range(WIN):
         lanes = np.arange(FREQ) + FREQ * w
         select[lanes, w] = half[:, 0]
         select[256 + lanes, w] = 1.0
-        select[512 + HALF * w + np.arange(HALF), 32 + w] = 1.0
+        select[512 + lanes, 32 + w] = 1.0
         select[768 + lanes, 64 + w] = half[:, 0]
         select[1024 + lanes, 64 + w] = 1.0
     window = np.zeros((256, 128))
@@ -93,7 +85,7 @@
         for kind in range(3):
             window[STRIDE * w : STRIDE * w + PATCH, 32 * kind + w] = 1.0
     as_bf16 = lambda x: jnp.asarray(x.astype(jnp.bfloat16))
-    return tuple(as_bf16(x) for x in (first, second, rows_inv, cols_even, cols_odd, select, window))
+    return tuple(as_bf16(x) for x in (first, second, mix_rows, mix_cols, sign_cols, select, window))
 
 
 def dot(a, b):
@@ -120,9 +112,6 @@
 
 
 def window_means(grp, sec, cells, window):
-    row = lax.broadcasted_iota(jnp.int32, (16, 16), 0)
-    col = lax.broadcasted_iota(jnp.int32, (16, 16), 1)
-    band = ((col >= row) & (col < row + 4)).astype(jnp.float32)
     for g in range(GROUPS):
         for c in range(7):
             values = grp[sec, g, 80 * c : 80 * c + 80, :].astype(jnp.float32)
@@ -132,8 +121,8 @@
         cells[14:15, 256 * g : 256 * g + 256] = (
             (values * values).reshape(5, 8, 256).sum(axis=0).sum(axis=0, keepdims=True)
         )
-    cells[15:16, :] = jnp.zeros((1, 256 * GROUPS), jnp.float32)
-    sums = dot_exact(band, cells[...])
+    cells[15:24, :] = jnp.zeros((9, 256 * GROUPS), jnp.float32)
+    sums = cells[0:16, :] + cells[1:17, :] + cells[2:18, :] + cells[3:19, :]
     stacked = jnp.concatenate([sums[:, 256 * g : 256 * g + 256] for g in range(GROUPS)], axis=0)
     total = dot_exact(stacked, window).reshape(GROUPS, 16, 128)
     return spread_groups(total) / (PATCH * PATCH) + tiny
@@ -157,12 +146,12 @@
         for c in range(10):
             if 1 <= c <= 8:
                 t = c - 1
-                frame[sec, c, 0:TOP, :] = top[sec, t, 0:TOP, :]
-                frame[sec, c, TOP : TOP + FORM_H, :] = form[sec, t]
-                frame[sec, c, 544:600, :] = bottom[sec, t, 8:EDGE_H, :]
+                frame[sec, c, 0:TOP, :] = top[t, sec, 0:TOP, :]
+                frame[sec, c, TOP : TOP + FORM_H, :] = form[t, sec]
+                frame[sec, c, 544:600, :] = bottom[t, sec, 8:EDGE_H, :]
                 frame[sec, c, 600:608, :] = jnp.zeros((8, 128), jnp.bfloat16)
-                for dst, own, other in ((TOP, form[sec, t, 0:8, :], top[sec, t, TOP:EDGE_H, :]),
-                                        (536, form[sec, t, 480:488, :], bottom[sec, t, 0:8, :])):
+                for dst, own, other in ((TOP, form[t, sec, 0:8, :], top[t, sec, TOP:EDGE_H, :]),
+                                        (536, form[t, sec, 480:488, :], bottom[t, sec, 0:8, :])):
                     both = own.astype(jnp.float32) + other.astype(jnp.float32)
                     frame[sec, c, dst : dst + 8, :] = both.astype(jnp.bfloat16)
             else:
@@ -170,8 +159,8 @@
 
 
 def correlate_kernel(
-    form, top, bottom, left, right, first, second, rows_inv, cols_even, cols_odd, select, window,
-    out, frame, grp, fa, fb, cells, raw, cross,
+    form, top, bottom, left, right, first, second, mix_rows, mix_cols, sign_cols,
+    select, window, out, frame, grp, fa, fb, cells, raw, raw_end, spec, cross, flow_rows, flow_cols,
 ):
     gather_frame(form, top, bottom, left, right, frame)
     for sec, dst in ((0, fa), (1, fb)):
@@ -189,78 +178,114 @@
     mean_b = window_means(grp, 1, cells, window_f32)
 
     sub = lax.broadcasted_iota(jnp.int32, (8, 256), 0)
-    lane = lax.broadcasted_iota(jnp.int32, (8, 256), 1)
-    top_half = jnp.where(sub == 0, 0.5, 1.0)
-    top_half2 = jnp.concatenate([top_half, top_half], axis=1)
-    slot_zero = lane % HALF == 0
-    shift_x = jnp.where(slot_zero, -8.0, 0.4 * (lane % HALF).astype(jnp.float32))[:1]
-    sub_f = jnp.concatenate([sub, sub], axis=1).astype(jnp.float32)
-
-    def weighted_rows(x):
-        total = x[1, 0] + x[1, 1]
-        for t in range(2, BLOCKS - 1):
-            total = total + (x[t, 0] + x[t, 1])
-        return total + x[0, 1] + (x[0, 0] * (top_half2 if x.shape[-1] == 512 else top_half) + 0.5 * x[BLOCKS - 1, 0])
-
-    def spectra(g, q, parity):
+    top = sub == 0
+    top_half = jnp.where(top, 0.5, 1.0)
+    lane128 = lax.broadcasted_iota(jnp.int32, (8, 128), 1)
+    k_lane = lax.broadcasted_iota(jnp.int32, (8, ROWS), 1)
+    end_weight = jnp.where((k_lane == 0) | (k_lane == HALF), -4.0, -8.0)
+
+    def row_of(m):
+        valid = (m >= 0) & (m < GROUPS * 12)
+        near = jnp.clip(m, 0, GROUPS * 12 - 1)
+        return near // 12, jnp.where(valid, near % 12, 15), (near % 12) // 2
+
+    def spectra(m, parity):
+        g, _, q = row_of(m)
         start = pl.multiple_of(80 * q + 32 * parity, 16)
-        spec = []
-        for src in (fa, fb):
-            s = dot(second[parity], src[g, pl.ds(start, ROWS), :]).reshape(BLOCKS, 2, 8, 512)
-            cc, cs = s[:, 0, :, :256], s[:, 0, :, 256:]
-            sc, ss = s[:, 1, :, :256], s[:, 1, :, 256:]
-            spec.append((cc - ss, sc + cs, cc + ss, sc - cs))
-        (a1, a2, a3, a4), (b1, b2, b3, b4) = spec
-        plus_r = a1 * b1 + a2 * b2
-        plus_i = a1 * b2 - a2 * b1
-        minus_r = a3 * b3 + a4 * b4
-        minus_i = a3 * b4 - a4 * b3
-        dcc = plus_r + minus_r
-        dss = minus_r - plus_r
-        dsc = plus_i + minus_i
-        dcs = plus_i - minus_i
-        d = jnp.stack(
-            [jnp.concatenate([dcc, dcs], axis=2), jnp.concatenate([dsc, dss], axis=2)], axis=1
-        )
-        weight = weighted_rows(d * d)
-        raw[g, pl.ds(2 * q + parity, 1), 768:1280] = jnp.sum(weight, axis=0, keepdims=True)
-        cross[parity] = d.reshape(ROWS, 512).astype(jnp.bfloat16)
-
-    def flows(g, q, parity):
-        d16 = cross[parity]
-        inv = dot(rows_inv[...], d16)
-        prod = (inv[:HALF] * inv[HALF:]).reshape(10, 8, 512)
-        run = prod[9]
-        ramp = prod[9]
-        for t in range(8, 0, -1):
-            run = run + prod[t]
-            ramp = ramp + run
-        run = run + prod[0]
-        flow_y = 3.2 * ramp + 0.4 * sub_f * run
-        flow_y = jnp.where(sub_f == 0.0, flow_y - 8.0 * prod[0], flow_y)
-        even = dot(d16[:, :256], cols_even[...]).reshape(BLOCKS, 2, 8, 256)
-        odd = dot(d16[:, 256:], cols_odd[...]).reshape(BLOCKS, 2, 8, 256)
-        flow_x = weighted_rows(even * jnp.where(slot_zero[None, None], even, odd))
-        i = 2 * q + parity
-        raw[g, pl.ds(i, 1), 0:512] = jnp.sum(flow_y, axis=0, keepdims=True)
-        raw[g, pl.ds(i, 1), 512:768] = jnp.sum(flow_x, axis=0, keepdims=True) * shift_x
-
+        spec[parity, 0] = dot(second[parity], fa[g, pl.ds(start, 176), :])
+        spec[parity, 1] = dot(second[parity], fb[g, pl.ds(start, 176), :])
+
+    def products(m, parity):
+        g, i, _ = row_of(m)
+        total = None
+        for half in range(2):
+            sides = []
+            for sec in range(2):
+                sides.append([])
+                for base in (HALF, 0):
+                    for lo in (0, 256):
+                        sides[sec].append(
+                            spec[parity, sec, base : base + HALF, lo : lo + 256].reshape(10, 8, 256)[5 * half : 5 * half + 5]
+                        )
+            terms = [(cc - ss, sc + cs, cc + ss, sc - cs) for cc, cs, sc, ss in sides]
+            (a1, a2, a3, a4), (b1, b2, b3, b4) = terms
+            plus_r = a1 * b1 + a2 * b2
+            plus_i = a1 * b2 - a2 * b1
+            minus_r = a3 * b3 + a4 * b4
+            minus_i = a3 * b4 - a4 * b3
+            dcc = plus_r + minus_r
+            dss = minus_r - plus_r
+            dsc = plus_i + minus_i
+            dcs = plus_i - minus_i
+            if half == 0:
+                (ac, asn, ae, aes), (bc, bsn, be, bes) = [[x[0] for x in side] for side in sides]
+                fix = lambda new, old: jnp.concatenate([jnp.where(top, new, old[0])[None], old[1:]], axis=0)
+                dcc = fix(2.0 * (ac * bc + asn * bsn), dcc)
+                dcs = fix(2.0 * (ac * bsn - asn * bc), dcs)
+                dsc = fix(2.0 * (ae * be + aes * bes), dsc)
+                dss = fix(2.0 * (ae * bes - aes * be), dss)
+            rows = slice(40 * half, 40 * half + 40)
+            cos_rows = slice(HALF + 40 * half, HALF + 40 * half + 40)
+            cross[parity, rows, 0:256] = dsc.reshape(40, 256).astype(jnp.bfloat16)
+            cross[parity, rows, 256:512] = dss.reshape(40, 256).astype(jnp.bfloat16)
+            cross[parity, cos_rows, 0:256] = dcc.reshape(40, 256).astype(jnp.bfloat16)
+            cross[parity, cos_rows, 256:512] = dcs.reshape(40, 256).astype(jnp.bfloat16)
+            low = dcc * dcc + dsc * dsc
+            high = dcs * dcs + dss * dss
+            if half == 0:
+                total = [low[0] * top_half + low[1:].sum(axis=0), high[0] * top_half + high[1:].sum(axis=0)]
+            else:
+                total = [total[0] + low.sum(axis=0), total[1] + high.sum(axis=0)]
+        total = jnp.concatenate(total, axis=1)
+        raw[g, pl.ds(i, 1), 768:1280] = jnp.sum(total, axis=0, keepdims=True)
+
+    def flows(m, parity):
+        g, i, _ = row_of(m)
+        flow_rows[parity] = dot(mix_rows[...], cross[parity])
+        flow_cols[parity] = dot(cross[parity, :, 256:512], mix_cols[...])
+        end = lax.dot_general(
+            sign_cols[...], cross[parity, :, 0:256], (((1,), (1,)), ((), ())), preferred_element_type=jnp.float32
+        )[:8]
+        end = jnp.sum(end * end * end_weight, axis=1, keepdims=True)
+        raw_end[g] = jnp.where(lane128 == i, end, raw_end[g])
+
+    def flow_sums(m, parity):
+        g, i, _ = row_of(m)
+        cosines = cross[parity, HALF:, :].astype(jnp.float32).reshape(10, 8, 512)
+        mixed = flow_rows[parity].reshape(11, 8, 512)
+        flow_y = cosines[0] * mixed[0]
+        for t in range(1, 10):
+            flow_y = flow_y + cosines[t] * mixed[t]
+        end = cross[parity, 0:16, :].astype(jnp.float32)[:1] * mixed[10, 0:1] - 8.0 * mixed[10, 1:2] * mixed[10, 1:2]
+        raw[g, pl.ds(i, 1), 0:512] = jnp.sum(flow_y, axis=0, keepdims=True) + end
+        cosines = cross[parity, :, 0:256].astype(jnp.float32).reshape(20, 8, 256)
+        mixed = flow_cols[parity].reshape(20, 8, 256)
+        flow_x = (cosines[0] * mixed[0] + cosines[10] * mixed[10]) * top_half
+        for t in range(1, 20):
+            if t != 10:
+                flow_x = flow_x + cosines[t] * mixed[t]
+        raw[g, pl.ds(i, 1), 512:768] = jnp.sum(flow_x, axis=0, keepdims=True)
+
+    raw_end[...] = jnp.zeros((GROUPS, 8, 128), jnp.float32)
     raw[:, 12:16, :] = jnp.zeros((GROUPS, 4, 1280), jnp.float32)
-
-    spectra(0, 0, 0)
-    spectra(0, 0, 1)
 
     def step(n, carry):
         for parity in range(2):
-            flows((n - 1) // 6, (n - 1) % 6, parity)
-            spectra(n // 6, n % 6, parity)
+            m = 2 * n + parity
+            flow_sums(m - 3, 1 - parity)
+            flows(m - 2, parity)
+            products(m - 1, 1 - parity)
+            spectra(m, parity)
         return carry
 
-    lax.fori_loop(1, GROUPS * 6, step, 0)
-    flows(GROUPS - 1, 5, 0)
-    flows(GROUPS - 1, 5, 1)
+    lax.fori_loop(0, GROUPS * 6 + 2, step, 0)
     sums = dot_exact(raw[...].reshape(GROUPS * 16, 1280), select[...].astype(jnp.float32))
-    total = spread_groups(sums.reshape(GROUPS, 16, 128))
+    sums = sums.reshape(GROUPS, 16, 128)
+    ends = [
+        pltpu.roll(jnp.concatenate([raw_end[g], jnp.zeros((120, 128), jnp.float32)], axis=0).T[:16], 32, axis=1)
+        for g in range(GROUPS)
+    ]
+    total = spread_groups([sums[g] + ends[g] for g in range(GROUPS)])
     scale = (1.0 / (PATCH * PATCH)) / (mean_a * mean_b)
     unit = (2.0 / (PATCH * PATCH)) ** 2 * HALF / (PATCH * PATCH)
     total = total * (scale * unit)
@@ -279,10 +304,15 @@
             pltpu.VMEM((2, GROUPS, FRAME_H, 256), jnp.bfloat16),
             pltpu.VMEM((GROUPS, FIRST_H, 512), jnp.bfloat16),
             pltpu.VMEM((GROUPS, FIRST_H, 512), jnp.bfloat16),
-            pltpu.VMEM((16, 256 * GROUPS), jnp.float32),
+            pltpu.VMEM((24, 256 * GROUPS), jnp.float32),
             pltpu.VMEM((GROUPS, 16, 1280), jnp.float32),
+            pltpu.VMEM((GROUPS, 8, 128), jnp.float32),
+            pltpu.VMEM((2, 2, ROWS, 512), jnp.float32),
             pltpu.VMEM((2, ROWS, 512), jnp.bfloat16),
+            pltpu.VMEM((2, HALF + 8, 512), jnp.float32),
+            pltpu.VMEM((2, ROWS, 256), jnp.float32),
         ],
+        compiler_params=pltpu.CompilerParams(vmem_limit_bytes=40 << 20),
     )(form, top, bottom, left, right, *tables())
 
 
@@ -294,10 +324,11 @@
     zero = lambda width: jnp.zeros((count, width), jnp.bfloat16)
 
     def position(offset):
-        row = offset[:, 0:1].astype(jnp.float32)
-        col = offset[:, 1:2].astype(jnp.float32)
-        code = row * (TX / TILE_H) + col * (1.0 / TILE_W) + 1.0
-        return jnp.floor(code + 0.5)
+        row = offset[0:1, :].astype(jnp.float32)
+        col = offset[1:2, :].astype(jnp.float32)
+        code = jnp.floor(row * (TX / TILE_H) + col * (1.0 / TILE_W) + 1.5)
+        code = jnp.concatenate([code, jnp.zeros((1, 128 - count), jnp.float32)], axis=1)
+        return jnp.broadcast_to(code, (128, 128)).T[:count]
 
     def piece(tiles, start, width):
         return tiles[:, start : start + width]
@@ -340,7 +371,7 @@
     lax.fori_loop(0, 16, flush, 0)
 
 
-def place_kernel(got, form, up, down, rows, plane_a, plane_b):
+def place_kernel(got, form, up, down, low, high, rows, plane_a, plane_b):
     def widen(n, carry):
         start = pl.multiple_of(8 * SLOT_H * n, 8)
         block = got[pl.ds(8 * n, 8)].astype(jnp.float32)
@@ -388,9 +419,17 @@
     for sec, plane in ((0, plane_a), (1, plane_b)):
         for t in range(TX):
             block = plane[FORM_H * t : FORM_H * t + FORM_H, :].astype(jnp.bfloat16)
-            form[sec, t] = block
-            up[sec, t] = plane[FORM_H * t : FORM_H * t + EDGE_H, :].astype(jnp.bfloat16)
-            down[sec, t] = plane[FORM_H * t + 424 : FORM_H * t + 488, :].astype(jnp.bfloat16)
+            form[t, sec] = block
+            for side, at in ((low, 0), (high, TX - 1)):
+                if t == at:
+                    side[sec, 0:TOP, :] = jnp.zeros((TOP, 128), jnp.bfloat16)
+                    side[sec, TOP : TOP + FORM_H, :] = block
+                    side[sec, TOP + FORM_H :, :] = jnp.zeros((FRAME_H - TOP - FORM_H, 128), jnp.bfloat16)
+            up[t, sec] = plane[FORM_H * t : FORM_H * t + EDGE_H, :].astype(jnp.bfloat16)
+            down[t, sec] = plane[FORM_H * t + 424 : FORM_H * t + 488, :].astype(jnp.bfloat16)
+
+
+VMEM_SPEC = pl.BlockSpec(memory_space=pltpu.VMEM)
 
 
 def pack(a_tiles, b_tiles, a_owner, b_owner, a_offset, b_offset):
@@ -398,19 +437,24 @@
         pack_kernel,
         out_shape=jax.ShapeDtypeStruct((128, SLOT_H, 128), jnp.bfloat16),
         scratch_shapes=[pltpu.VMEM((128 * SLOT_H, 128), jnp.float32)],
-    )(a_tiles, b_tiles, a_owner[None], b_owner[None], a_offset, b_offset)
+        compiler_params=pltpu.CompilerParams(vmem_limit_bytes=16 << 20),
+    )(a_tiles, b_tiles, a_owner[None], b_owner[None], a_offset.T, b_offset.T)
 
 
 def place(got):
-    edge = jax.ShapeDtypeStruct((2, TX, EDGE_H, 128), jnp.bfloat16)
+    edge = jax.ShapeDtypeStruct((TX, 2, EDGE_H, 128), jnp.bfloat16)
+    side = jax.ShapeDtypeStruct((2, FRAME_H, 128), jnp.bfloat16)
     return pl.pallas_call(
         place_kernel,
-        out_shape=(jax.ShapeDtypeStruct((2, TX, FORM_H, 128), jnp.bfloat16), edge, edge),
+        out_shape=(jax.ShapeDtypeStruct((TX, 2, FORM_H, 128), jnp.bfloat16), edge, edge, side, side),
         scratch_shapes=[
             pltpu.VMEM((128 * SLOT_H, 128), jnp.float32),
             pltpu.VMEM((TX * FORM_H, 128), jnp.float32),
             pltpu.VMEM((TX * FORM_H, 128), jnp.float32),
         ],
+        in_specs=[VMEM_SPEC],
+        out_specs=(VMEM_SPEC,) * 5,
+        compiler_params=pltpu.CompilerParams(vmem_limit_bytes=24 << 20),
     )(got)
 
 
@@ -433,24 +477,20 @@
     return lax.ppermute(block, axis, pairs)
 
 
-def column(form, top, bottom, t):
-    grow = lambda x, low, high: jnp.pad(x[:, t], ((0, 0), (low, high), (0, 0)))
-    return (
-        grow(form, TOP, FRAME_H - TOP - FORM_H)
-        + grow(top, 0, FRAME_H - EDGE_H)
-        + grow(bottom, 536, FRAME_H - 536 - EDGE_H)
-    )
+def column(side, top, bottom, t):
+    grow = lambda x, low, high: jnp.pad(x[t], ((0, 0), (low, high), (0, 0)))
+    return side + grow(top, 0, FRAME_H - EDGE_H) + grow(bottom, 536, FRAME_H - 536 - EDGE_H)
 
 
 def per_device(a_tiles, a_owner, a_offset, b_tiles, b_owner, b_offset, patch_valid):
     grid_rows, grid_cols = patch_valid.shape
     packed = pack(a_tiles, b_tiles, a_owner, b_owner, a_offset, b_offset)
     got = lax.all_to_all(packed, ("row", "col"), split_axis=0, concat_axis=0, tiled=True)
-    form, up, down = place(got)
+    form, up, down, low, high = place(got)
     top = shifted(down, "row", 1)
     bottom = shifted(up, "row", -1)
-    left = shifted(column(form, top, bottom, TX - 1), "col", 1)
-    right = shifted(column(form, top, bottom, 0), "col", -1)
+    left = shifted(column(high, top, bottom, TX - 1), "col", 1)
+    right = shifted(column(low, top, bottom, 0), "col", -1)
     result = correlate(form, top, bottom, left, right)
     flow_field = jnp.stack([result[:grid_rows, :grid_cols], result[:grid_rows, 32 : 32 + grid_cols]])
     confidence = result[:grid_rows, 64 : 64 + grid_cols]

time: 128 us -> 118 us (0.922)
  Pallas kernels: 38.9 us -> 30.2 us
  local copies, waits for them, and re-layouts: 9.54 us -> 6.37 us
  waiting for transfers between devices: 13.6 us -> 16.1 us
    pallas_call x1, Pallas kernels: 29.9 us -> 26.6 us  [correlate(): pl.pallas_call(correlate_kernel, out_shape=jax.ShapeDtypeStruct((16, 128)...]
    pallas_call x1, Pallas kernels: 4.92 us -> 2.06 us  [place(): pl.pallas_call(place_kernel, out_shape=(jax.ShapeDtypeStruct((TX, 2, FORM...]
    ppermute x4, waiting for transfers between devices: 6.28 us -> 8.84 us  [shifted(): return lax.ppermute(block, axis, pairs)]
    pallas_call x1, Pallas kernels: 4.08 us -> 1.53 us  [pack(): pl.pallas_call(pack_kernel, out_shape=jax.ShapeDtypeStruct((128, SLOT_H,...]
    pallas_call x2 -> x0, local copies, waits for them, and re-layouts: 1.95 us -> none  [place(): pl.pallas_call(place_kernel, out_shape=(jax.ShapeDtypeStruct((2, TX, FORM...]
    ppermute x2 -> x0, local copies, waits for them, and re-layouts: 1.46 us -> none  [shifted(): return lax.ppermute(block, axis, pairs)]
    unnamed x10 -> x30, local copies, waits for them, and re-layouts: 4.72 us -> 6.06 us
  transfers between devices with their start and end apart: 8 -> 8, of which waited for: 6 -> 6; matrix products, arithmetic and copies ran while one was open for 3% -> 1% of each run, Pallas kernels for 0% -> 0%
where the time goes in v3:
time: 118 us
  blocking collectives  34.7 us (29%)
  Pallas kernels  30.2 us (26%)
  starting transfers between devices  28.7 us (24%)
  waiting for transfers between devices  16.1 us (14%)
  local copies, waits for them, and re-layouts  6.37 us (5%)
    all_to_all x1, blocking collectives, per_device(): lax.all_to_all(packed, ('row', 'col'), split_axis=0, concat_axis=0, tiled...  34.7 us
    pallas_call x1, Pallas kernels, correlate(): pl.pallas_call(correlate_kernel, out_shape=jax.ShapeDtypeStruct((16, 128)...  26.6 us
    ppermute x4, starting transfers between devices, shifted(): return lax.ppermute(block, axis, pairs)  13.6 us
    ppermute x2, starting transfers between devices, extended_2(): lax.ppermute(lax.slice_in_dim(block, block.shape[dim] - width, None, axis...  11.3 us
    ppermute x4, waiting for transfers between devices, shifted(): return lax.ppermute(block, axis, pairs)  8.84 us
    ppermute x2, waiting for transfers between devices, extended_2(): lax.ppermute(lax.slice_in_dim(block, 0, width, axis=dim), axis, backward)  7.28 us
    unnamed x30, local copies, waits for them, and re-layouts  6.06 us
    ppermute x2, starting transfers between devices, extended_2(): lax.ppermute(lax.slice_in_dim(block, 0, width, axis=dim), axis, backward)  3.84 us
  transfers between devices with their start and end apart: 8, of which 6 were waited for; matrix products, arithmetic and copies ran while one was open for 1% of the time, Pallas kernels for 0%

profile of v3, /device:TPU:27, one launch (start us, length us, event | category | flops | bytes accessed | tf_op | source)
XLA Modules:
  0.0 117.6 jit_solution(331484308676598707)
XLA Ops:
  0.6 0.0 copy-start
  0.6 1.1 copy-done
  1.7 0.0 copy-start.1
  1.7 1.1 copy-done.1
  2.8 0.0 copy-start.9
  2.8 0.7 copy-done.9
  3.5 0.0 copy-start.10
  3.5 0.7 copy-done.10
  4.1 0.0 copy-start.11
  4.1 0.7 copy-done.11
  4.8 0.0 copy-start.12
  4.8 0.7 copy-done.12
  5.5 1.5 %shard_map.149 = bf16[128,56,128]{2,1,0:T(8,128)(2,1)S(1)} custom-call(bf16[96,3200]{1,0:T(8,128)(2,1)S(1)} %copy-done, bf16[96,3200]{1,0:T(8,128)(2,1)S(1)} %copy-done.1, s32[1,96]{1,0:T(1,128)S(1)} %bitcast.24, s32[1,96]{1,0:T(1,128)S(1)} %bitcast.25, s32[2,96]{1,0:T(2,128)S(1)} %bitcast.22, s32[2,96]{1,0:T(2,128)S(1)} %bitcast.23), custom_call_target="tpu_custom_call" | custom-call | tf_op jit(solution)/shard_map/pallas_call | solution.py:436
  7.0 34.7 %all_to_all.5.got = bf16[128,56,128]{2,1,0:T(8,128)(2,1)S(1)} all-to-all(bf16[128,56,128]{2,1,0:T(8,128)(2,1)S(1)} %shard_map.149), channel_id=1, replica_groups=mesh['row'=4,'col'=32] {'row','col'}, dimensions={0} | all-to-all | bytes 3670016 | tf_op jit(solution)/shard_map/all_to_all | solution.py:488
  41.7 0.0 copy-start.13
  41.7 0.0 copy-start.2
  41.7 0.0 copy-start.3
  41.7 0.0 copy-start.4
  41.7 0.0 copy-start.5
  41.7 0.0 copy-start.6
  41.8 0.0 copy-start.7
  41.8 0.0 copy-start.8
  41.8 2.1 %shard_map.150 = (bf16[8,2,488,128]{3,2,1,0:T(8,128)(2,1)S(1)}, bf16[8,2,64,128]{3,2,1,0:T(8,128)(2,1)S(1)}, bf16[8,2,64,128]{3,2,1,0:T(8,128)(2,1)S(1)}, bf16[2...) custom-call(bf16[128,56,128]{2,1,0:T(8,128)(2,1)S(1)} %all_to_all.5.got), custom_call_target="tpu_custom_call" | custom-call | tf_op jit(solution)/shard_map/pallas_call | solution.py:447
  43.9 2.0 %collective-permute-start = (bf16[8,2,64,128]{3,2,1,0:T(8,128)(2,1)S(1)}, bf16[8,2,64,128]{3,2,1,0:T(8,128)(2,1)S(1)}, u32[]{:S(2)}, u32[]{:S(2)}) collective-permute-start(bf16[8,2,64,128]{3,2,1,0:T(8,128)(2,1)S(1)} %get-tuple-element.8), channel_id=1, source_target_pairs={{0,32},{32,64},{64,96},{1,33},{33,65},{65,97},{2,34},{34,66},{66,9... | collective-permute-start | bytes 786440 | tf_op jit(solution)/shard_map/ppermute | solution.py:477
  45.9 3.3 %collective-permute-start.1 = (bf16[8,2,64,128]{3,2,1,0:T(8,128)(2,1)S(1)}, bf16[8,2,64,128]{3,2,1,0:T(8,128)(2,1)S(1)}, u32[]{:S(2)}, u32[]{:S(2)}) collective-permute-start(bf16[8,2,64,128]{3,2,1,0:T(8,128)(2,1)S(1)} %get-tuple-element.9), channel_id=1, source_target_pairs={{32,0},{64,32},{96,64},{33,1},{65,33},{97,65},{34,2},{66,34},{98,6... | collective-permute-start | bytes 786440 | tf_op jit(solution)/shard_map/ppermute | solution.py:477
  49.2 3.2 %collective-permute-done.top = bf16[8,2,64,128]{3,2,1,0:T(8,128)(2,1)S(1)} collective-permute-done((bf16[8,2,64,128]{3,2,1,0:T(8,128)(2,1)S(1)}, bf16[8,2,64,128]{3,2,1,0:T(8,128)(2,1)S(1)}, u32[]{:S(2)}, u32[]{:S(2)}) %collective-permute-start) | collective-permute-done | bytes 262176 | tf_op jit(solution)/shard_map/ppermute | solution.py:477
  52.4 1.8 %collective-permute-done.1.bottom = bf16[8,2,64,128]{3,2,1,0:T(8,128)(2,1)S(1)} collective-permute-done((bf16[8,2,64,128]{3,2,1,0:T(8,128)(2,1)S(1)}, bf16[8,2,64,128]{3,2,1,0:T(8,128)(2,1)S(1)}, u32[]{:S(2)}, u32[]{:S(2)}) %collective-permute-start.1) | collective-permute-done | bytes 262176 | tf_op jit(solution)/shard_map/ppermute | solution.py:477
  54.3 4.2 %collective-permute-start.3 = (bf16[2,608,128]{2,1,0:T(8,128)(2,1)S(1)}, bf16[2,608,128]{2,1,0:T(8,128)(2,1)S(1)}, u32[]{:S(2)}, u32[]{:S(2)}) collective-permute-start(bf16[2,608,128]{2,1,0:T(8,128)(2,1)S(1)} %pad_add_fusion), channel_id=1, source_target_pairs={{1,0},{2,1},{3,2},{4,3},{5,4},{6,5},{7,6},{8,7},{9,8},{10,9},{11,1... | collective-permute-start | bytes 933896 | tf_op jit(solution)/shard_map/ppermute | solution.py:477
  58.5 4.1 %collective-permute-start.2 = (bf16[2,608,128]{2,1,0:T(8,128)(2,1)S(1)}, bf16[2,608,128]{2,1,0:T(8,128)(2,1)S(1)}, u32[]{:S(2)}, u32[]{:S(2)}) collective-permute-start(bf16[2,608,128]{2,1,0:T(8,128)(2,1)S(1)} %pad_add_fusion.1), channel_id=1, source_target_pairs={{0,1},{1,2},{2,3},{3,4},{4,5},{5,6},{6,7},{7,8},{8,9},{9,10},{10,1... | collective-permute-start | bytes 933896 | tf_op jit(solution)/shard_map/ppermute | solution.py:477
  62.6 0.0 copy-done.13
  62.7 2.6 %collective-permute-done.3.right = bf16[2,608,128]{2,1,0:T(8,128)(2,1)S(1)} collective-permute-done((bf16[2,608,128]{2,1,0:T(8,128)(2,1)S(1)}, bf16[2,608,128]{2,1,0:T(8,128)(2,1)S(1)}, u32[]{:S(2)}, u32[]{:S(2)}) %collective-permute-start.3) | collective-permute-done | bytes 311328 | tf_op jit(solution)/shard_map/ppermute | solution.py:477
  65.2 1.2 %collective-permute-done.2.left = bf16[2,608,128]{2,1,0:T(8,128)(2,1)S(1)} collective-permute-done((bf16[2,608,128]{2,1,0:T(8,128)(2,1)S(1)}, bf16[2,608,128]{2,1,0:T(8,128)(2,1)S(1)}, u32[]{:S(2)}, u32[]{:S(2)}) %collective-permute-start.2) | collective-permute-done | bytes 311328 | tf_op jit(solution)/shard_map/ppermute | solution.py:477
  66.5 0.0 copy-done.2
  66.5 0.0 copy-done.3
  66.5 0.0 copy-done.4
  66.5 0.0 copy-done.5
  66.5 0.0 copy-done.6
  66.5 0.0 copy-done.7
  66.5 0.0 copy-done.8
  66.5 26.6 %shard_map.151 = f32[16,128]{1,0:T(8,128)S(1)} custom-call(bf16[8,2,488,128]{3,2,1,0:T(8,128)(2,1)S(1)} %get-tuple-element.7.form, bf16[8,2,64,128]{3,2,1,0:T(8,128)(2,1)S(1)} %collective-permute-done.top, bf16[8,2,64,128]{3,2,1,0:T(8,128)(2,1)S(1)} %collective-permute-done.1.bottom, bf16[2,608,128]{2,1,0:T(8,128)(2,1)S(1)} %collective-permute-done.2.left, ...), custom_call_target="tpu_custom_call" | custom-call | tf_op jit(solution)/shard_map/pallas_call | solution.py:299
  93.1 0.1 fusion.8
  93.2 3.4 %collective-permute-start.4 = (f32[3,3,16]{2,1,0:T(4,128)S(1)}, f32[3,3,16]{2,1,0:T(4,128)S(1)}, u32[]{:S(2)}, u32[]{:S(2)}) collective-permute-start(f32[3,3,16]{2,1,0:T(4,128)S(1)} %get-tuple-element.20), channel_id=1, source_target_pairs={{0,32},{32,64},{64,96},{1,33},{33,65},{65,97},{2,34},{34,66},{66,9... | collective-permute-start | bytes 1736 | tf_op jit(solution)/shard_map/ppermute | solution.py:466
  96.6 1.9 %collective-permute-start.5 = (f32[3,3,16]{2,1,0:T(4,128)S(1)}, f32[3,3,16]{2,1,0:T(4,128)S(1)}, u32[]{:S(2)}, u32[]{:S(2)}) collective-permute-start(f32[3,3,16]{2,1,0:T(4,128)S(1)} %get-tuple-element.21), channel_id=1, source_target_pairs={{32,0},{64,32},{96,64},{33,1},{65,33},{97,65},{34,2},{66,34},{98,6... | collective-permute-start | bytes 1736 | tf_op jit(solution)/shard_map/ppermute | solution.py:469
  98.5 0.0 collective-permute-done.4
  98.5 2.4 %collective-permute-done.5 = f32[3,3,16]{2,1,0:T(4,128)S(1)} collective-permute-done((f32[3,3,16]{2,1,0:T(4,128)S(1)}, f32[3,3,16]{2,1,0:T(4,128)S(1)}, u32[]{:S(2)}, u32[]{:S(2)}) %collective-permute-start.5) | collective-permute-done | bytes 608 | tf_op jit(solution)/shard_map/ppermute | solution.py:469
  101.0 0.1 fusion.9
  101.1 7.9 %collective-permute-start.6 = (f32[3,18,3]{2,1,0:T(8,128)S(1)}, f32[3,18,3]{2,1,0:T(8,128)S(1)}, u32[]{:S(2)}, u32[]{:S(2)}) collective-permute-start(f32[3,18,3]{2,1,0:T(8,128)S(1)} %get-tuple-element.18), channel_id=1, source_target_pairs={{0,1},{1,2},{2,3},{3,4},{4,5},{5,6},{6,7},{7,8},{8,9},{9,10},{10,1... | collective-permute-start | bytes 1952 | tf_op jit(solution)/shard_map/ppermute | solution.py:466
  109.0 1.9 %collective-permute-start.7 = (f32[3,18,3]{2,1,0:T(8,128)S(1)}, f32[3,18,3]{2,1,0:T(8,128)S(1)}, u32[]{:S(2)}, u32[]{:S(2)}) collective-permute-start(f32[3,18,3]{2,1,0:T(8,128)S(1)} %get-tuple-element.19), channel_id=1, source_target_pairs={{1,0},{2,1},{3,2},{4,3},{5,4},{6,5},{7,6},{8,7},{9,8},{10,9},{11,1... | collective-permute-start | bytes 1952 | tf_op jit(solution)/shard_map/ppermute | solution.py:469
  110.9 0.6 copy.16
  111.5 0.0 collective-permute-done.6
  111.5 4.8 %collective-permute-done.7 = f32[3,18,3]{2,1,0:T(8,128)S(1)} collective-permute-done((f32[3,18,3]{2,1,0:T(8,128)S(1)}, f32[3,18,3]{2,1,0:T(8,128)S(1)}, u32[]{:S(2)}, u32[]{:S(2)}) %collective-permute-start.7) | collective-permute-done | bytes 680 | tf_op jit(solution)/shard_map/ppermute | solution.py:469
  116.4 0.1 pad_maximum_fusion.1
  116.5 0.1 slice.150
  116.6 0.1 slice.155
  116.7 0.1 slice.160
  116.7 0.1 fusion.5
  116.8 0.1 fusion.3
  116.9 0.1 fusion.1
  117.0 0.6 copy.17
  (11 shorter events, 0.1 us)
Async XLA Ops:
  0.6 1.1 copy-start
  1.7 1.1 copy-start.1
  2.8 0.7 copy-start.9
  3.5 0.7 copy-start.10
  4.1 0.7 copy-start.11
  4.8 0.7 copy-start.12
  41.7 20.9 %copy-start.13 = (s32[12,16]{1,0:T(8,128)S(1)}, s32[12,16]{1,0:T(8,128)}, u32[]{:S(2)}) copy-start(s32[12,16]{1,0:T(8,128)} %param.20) | copy-start | bytes 2308
  41.7 24.7 %copy-start.2 = (bf16[1280,128]{1,0:T(8,128)(2,1)S(1)}, bf16[1280,128]{1,0:T(8,128)(2,1)}, u32[]{:S(2)}) copy-start(bf16[1280,128]{1,0:T(8,128)(2,1)} %constant.33.clone.select) | copy-start | bytes 983044
  41.7 24.7 %copy-start.3 = (bf16[256,512]{1,0:T(8,128)(2,1)S(1)}, bf16[256,512]{1,0:T(8,128)(2,1)}, u32[]{:S(2)}) copy-start(bf16[256,512]{1,0:T(8,128)(2,1)} %constant.28.clone.first) | copy-start | bytes 786436
  41.7 24.7 %copy-start.4 = (bf16[2,160,176]{2,1,0:T(8,128)(2,1)S(1)}, bf16[2,160,176]{2,1,0:T(8,128)(2,1)}, u32[]{:S(2)}) copy-start(bf16[2,160,176]{2,1,0:T(8,128)(2,1)} %constant.29.clone.second) | copy-start | bytes 337924
  41.7 24.7 %copy-start.5 = (bf16[256,256]{1,0:T(8,128)(2,1)S(1)}, bf16[256,256]{1,0:T(8,128)(2,1)}, u32[]{:S(2)}) copy-start(bf16[256,256]{1,0:T(8,128)(2,1)} %constant.31.clone.mix_cols) | copy-start | bytes 393220
  41.7 24.7 %copy-start.6 = (bf16[256,128]{1,0:T(8,128)(2,1)S(1)}, bf16[256,128]{1,0:T(8,128)(2,1)}, u32[]{:S(2)}) copy-start(bf16[256,128]{1,0:T(8,128)(2,1)} %constant.34.clone.window) | copy-start | bytes 196612
  41.8 24.7 %copy-start.7 = (bf16[88,160]{1,0:T(8,128)(2,1)S(1)}, bf16[88,160]{1,0:T(8,128)(2,1)}, u32[]{:S(2)}) copy-start(bf16[88,160]{1,0:T(8,128)(2,1)} %constant.30.clone.mix_rows) | copy-start | bytes 84484
  41.8 24.7 %copy-start.8 = (bf16[16,256]{1,0:T(8,128)(2,1)S(1)}, bf16[16,256]{1,0:T(8,128)(2,1)}, u32[]{:S(2)}) copy-start(bf16[16,256]{1,0:T(8,128)(2,1)} %constant.32.clone.sign_cols) | copy-start | bytes 24580
  43.9 8.5 %collective-permute-start = (bf16[8,2,64,128]{3,2,1,0:T(8,128)(2,1)S(1)}, bf16[8,2,64,128]{3,2,1,0:T(8,128)(2,1)S(1)}, u32[]{:S(2)}, u32[]{:S(2)}) collective-permute-start(bf16[8,2,64,128]{3,2,1,0:T(8,128)(2,1)S(1)} %get-tuple-element.8), channel_id=1, source_target_pairs={{0,32},{32,64},{64,96},{1,33},{33,65},{65,97},{2,34},{34,66},{66,9... | collective-permute-start | bytes 786440 | tf_op jit(solution)/shard_map/ppermute | solution.py:477
  45.9 8.3 %collective-permute-start.1 = (bf16[8,2,64,128]{3,2,1,0:T(8,128)(2,1)S(1)}, bf16[8,2,64,128]{3,2,1,0:T(8,128)(2,1)S(1)}, u32[]{:S(2)}, u32[]{:S(2)}) collective-permute-start(bf16[8,2,64,128]{3,2,1,0:T(8,128)(2,1)S(1)} %get-tuple-element.9), channel_id=1, source_target_pairs={{32,0},{64,32},{96,64},{33,1},{65,33},{97,65},{34,2},{66,34},{98,6... | collective-permute-start | bytes 786440 | tf_op jit(solution)/shard_map/ppermute | solution.py:477
  54.3 11.0 %collective-permute-start.3 = (bf16[2,608,128]{2,1,0:T(8,128)(2,1)S(1)}, bf16[2,608,128]{2,1,0:T(8,128)(2,1)S(1)}, u32[]{:S(2)}, u32[]{:S(2)}) collective-permute-start(bf16[2,608,128]{2,1,0:T(8,128)(2,1)S(1)} %pad_add_fusion), channel_id=1, source_target_pairs={{1,0},{2,1},{3,2},{4,3},{5,4},{6,5},{7,6},{8,7},{9,8},{10,9},{11,1... | collective-permute-start | bytes 933896 | tf_op jit(solution)/shard_map/ppermute | solution.py:477
  58.5 8.0 %collective-permute-start.2 = (bf16[2,608,128]{2,1,0:T(8,128)(2,1)S(1)}, bf16[2,608,128]{2,1,0:T(8,128)(2,1)S(1)}, u32[]{:S(2)}, u32[]{:S(2)}) collective-permute-start(bf16[2,608,128]{2,1,0:T(8,128)(2,1)S(1)} %pad_add_fusion.1), channel_id=1, source_target_pairs={{0,1},{1,2},{2,3},{3,4},{4,5},{5,6},{6,7},{7,8},{8,9},{9,10},{10,1... | collective-permute-start | bytes 933896 | tf_op jit(solution)/shard_map/ppermute | solution.py:477
  93.2 5.3 %collective-permute-start.4 = (f32[3,3,16]{2,1,0:T(4,128)S(1)}, f32[3,3,16]{2,1,0:T(4,128)S(1)}, u32[]{:S(2)}, u32[]{:S(2)}) collective-permute-start(f32[3,3,16]{2,1,0:T(4,128)S(1)} %get-tuple-element.20), channel_id=1, source_target_pairs={{0,32},{32,64},{64,96},{1,33},{33,65},{65,97},{2,34},{34,66},{66,9... | collective-permute-start | bytes 1736 | tf_op jit(solution)/shard_map/ppermute | solution.py:466
  96.6 4.4 %collective-permute-start.5 = (f32[3,3,16]{2,1,0:T(4,128)S(1)}, f32[3,3,16]{2,1,0:T(4,128)S(1)}, u32[]{:S(2)}, u32[]{:S(2)}) collective-permute-start(f32[3,3,16]{2,1,0:T(4,128)S(1)} %get-tuple-element.21), channel_id=1, source_target_pairs={{32,0},{64,32},{96,64},{33,1},{65,33},{97,65},{34,2},{66,34},{98,6... | collective-permute-start | bytes 1736 | tf_op jit(solution)/shard_map/ppermute | solution.py:469
  101.1 10.5 %collective-permute-start.6 = (f32[3,18,3]{2,1,0:T(8,128)S(1)}, f32[3,18,3]{2,1,0:T(8,128)S(1)}, u32[]{:S(2)}, u32[]{:S(2)}) collective-permute-start(f32[3,18,3]{2,1,0:T(8,128)S(1)} %get-tuple-element.18), channel_id=1, source_target_pairs={{0,1},{1,2},{2,3},{3,4},{4,5},{5,6},{6,7},{7,8},{8,9},{9,10},{10,1... | collective-permute-start | bytes 1952 | tf_op jit(solution)/shard_map/ppermute | solution.py:466
  109.0 7.4 %collective-permute-start.7 = (f32[3,18,3]{2,1,0:T(8,128)S(1)}, f32[3,18,3]{2,1,0:T(8,128)S(1)}, u32[]{:S(2)}, u32[]{:S(2)}) collective-permute-start(f32[3,18,3]{2,1,0:T(8,128)S(1)} %get-tuple-element.19), channel_id=1, source_target_pairs={{1,0},{2,1},{3,2},{4,3},{5,4},{6,5},{7,6},{8,7},{9,8},{10,9},{11,1... | collective-permute-start | bytes 1952 | tf_op jit(solution)/shard_map/ppermute | solution.py:469

commit v4 on v3

--- a/solution.py
+++ b/solution.py
@@ -13,7 +13,6 @@
 TY = 12
 TX = 8
 SWEEPS = 3
-MARGIN = 60
 HALF = PATCH // 2
 FREQ = HALF + 1
 WIN = 3
@@ -28,8 +27,8 @@
 FORM_H = 488
 EDGE_H = 64
 TOP = 56
-TMAJOR = True
-FIRST_H = FRAME_H
+
+VMEM_SPEC = pl.BlockSpec(memory_space=pltpu.VMEM)
 
 stiffness = 1.0
 tiny = 1e-06
@@ -102,81 +101,80 @@
     )
 
 
-def spread_groups(sums):
+EDGE_GROUPS = (0, 4, 5)
+INNER_GROUPS = (1, 2, 3)
+INNER_LO = 64
+INNER_HI = 528
+
+
+def spread_groups(sums, groups):
     lane = lax.broadcasted_iota(jnp.int32, (16, 128), 1) % 32
-    total = sums[0]
-    for g in range(1, GROUPS):
-        piece = sums[g] if g < GROUPS - 1 else jnp.where(lane == 0, sums[g], 0.0)
-        total = total + pltpu.roll(piece, WIN * g, axis=1)
+    total = jnp.zeros((16, 128), jnp.float32)
+    for piece, g in zip(sums, groups):
+        piece = piece if g < GROUPS - 1 else jnp.where(lane == 0, piece, 0.0)
+        total = total + (pltpu.roll(piece, WIN * g, axis=1) if g else piece)
     return total
 
 
-def window_means(grp, sec, cells, window):
-    for g in range(GROUPS):
-        for c in range(7):
-            values = grp[sec, g, 80 * c : 80 * c + 80, :].astype(jnp.float32)
-            squares = (values * values).reshape(2, 5, 8, 256).sum(axis=1)
-            cells[2 * c : 2 * c + 2, 256 * g : 256 * g + 256] = squares.sum(axis=1)
-        values = grp[sec, g, 560:608, :].astype(jnp.float32)[:40]
-        cells[14:15, 256 * g : 256 * g + 256] = (
-            (values * values).reshape(5, 8, 256).sum(axis=0).sum(axis=0, keepdims=True)
-        )
-    cells[15:24, :] = jnp.zeros((9, 256 * GROUPS), jnp.float32)
-    sums = cells[0:16, :] + cells[1:17, :] + cells[2:18, :] + cells[3:19, :]
-    stacked = jnp.concatenate([sums[:, 256 * g : 256 * g + 256] for g in range(GROUPS)], axis=0)
-    total = dot_exact(stacked, window).reshape(GROUPS, 16, 128)
-    return spread_groups(total) / (PATCH * PATCH) + tiny
-
-
-def pixel_places(sec, odd_group):
-    row = lax.broadcasted_iota(jnp.int32, (512, 256), 0)
-    col = lax.broadcasted_iota(jnp.int32, (512, 256), 1)
-    tile, lane = row // 128, row % 128
-    if sec == 0:
-        pixel = jnp.where(lane < TILE_W, lane, -1000)
+def cell_squares(grp, sec, n, cells, lo, hi, base):
+    for c in range(lo, hi):
+        at = STRIDE * c - base
+        near = at // 16 * 16
+        values = grp[sec, n, near : near + 48, :].astype(jnp.float32)[at - near : at - near + STRIDE]
+        squares = (values * values).reshape(5, 8, 256).sum(axis=0)
+        cells[sec, c : c + 1, 256 * n : 256 * n + 256] = jnp.sum(squares, axis=0, keepdims=True)
+
+
+def window_means(cells, sec, window, groups):
+    sums = cells[sec, 0:16, :] + cells[sec, 1:17, :] + cells[sec, 2:18, :] + cells[sec, 3:19, :]
+    stacked = jnp.concatenate([sums[:, 256 * n : 256 * n + 256] for n in range(WIN)], axis=0)
+    total = dot_exact(stacked, window).reshape(WIN, 16, 128)
+    return spread_groups([total[n] for n in range(WIN)], groups) / (PATCH * PATCH) + tiny
+
+
+def group_pixels(tile, sec, g):
+    c = 3 * (g // 2) + g % 2
+    offset = 20 + 40 * (g % 2)
+    pieces = []
+    left = 240
+    while left > 0 and c < 10:
+        values = tile(c)
+        width = min(TILE_W - offset, left)
+        if sec == 0:
+            pieces.append(values[:, offset : offset + width])
+        else:
+            if offset < SPLIT:
+                pieces.append(values[:, TILE_W + offset : TILE_W + min(SPLIT, offset + width)])
+            if offset + width > SPLIT:
+                pieces.append(values[:, max(0, offset - SPLIT) : offset + width - SPLIT])
+        left -= width
+        offset = 0
+        c += 1
+    rows = pieces[0].shape[0]
+    pieces.append(jnp.zeros((rows, 256 - 240 + left), pieces[0].dtype))
+    return jnp.concatenate(pieces, axis=1)
+
+
+def frame_column(form, top, bottom, frame, sec, c, upper, lower):
+    t = c - 1
+    if upper == lower:
+        frame[sec, c, TOP : TOP + FORM_H, :] = form[t, sec]
     else:
-        tail = jnp.where(lane < LANES, lane + SPLIT, -1000)
-        pixel = jnp.where(lane >= TILE_W, lane - TILE_W, tail)
-    offset = 20 + 40 * odd_group
-    return jnp.where((tile * TILE_W + pixel - offset == col) & (col < 240), 1.0, 0.0).astype(jnp.bfloat16)
-
-
-def gather_frame(form, top, bottom, left, right, frame):
-    for sec in range(2):
-        for c in range(10):
-            if 1 <= c <= 8:
-                t = c - 1
-                frame[sec, c, 0:TOP, :] = top[t, sec, 0:TOP, :]
-                frame[sec, c, TOP : TOP + FORM_H, :] = form[t, sec]
-                frame[sec, c, 544:600, :] = bottom[t, sec, 8:EDGE_H, :]
-                frame[sec, c, 600:608, :] = jnp.zeros((8, 128), jnp.bfloat16)
-                for dst, own, other in ((TOP, form[t, sec, 0:8, :], top[t, sec, TOP:EDGE_H, :]),
-                                        (536, form[t, sec, 480:488, :], bottom[t, sec, 0:8, :])):
-                    both = own.astype(jnp.float32) + other.astype(jnp.float32)
-                    frame[sec, c, dst : dst + 8, :] = both.astype(jnp.bfloat16)
-            else:
-                frame[sec, c] = (left if c == 0 else right)[sec]
-
-
-def correlate_kernel(
-    form, top, bottom, left, right, first, second, mix_rows, mix_cols, sign_cols,
-    select, window, out, frame, grp, fa, fb, cells, raw, raw_end, spec, cross, flow_rows, flow_cols,
-):
-    gather_frame(form, top, bottom, left, right, frame)
-    for sec, dst in ((0, fa), (1, fb)):
-        for odd_group in range(2):
-            places = pixel_places(sec, odd_group)
-            for g in range(odd_group, GROUPS, 2):
-                c = 3 * (g // 2) + odd_group
-                count = min(4, 10 - c)
-                wide = jnp.concatenate([frame[sec, c + k] for k in range(count)], axis=1)
-                pixels = dot(wide, places[: 128 * count]).astype(jnp.bfloat16)
-                grp[sec, g] = pixels
-                dst[g] = dot(pixels, first[...]).astype(jnp.bfloat16)
-    window_f32 = window[...].astype(jnp.float32)
-    mean_a = window_means(grp, 0, cells, window_f32)
-    mean_b = window_means(grp, 1, cells, window_f32)
-
+        frame[sec, c, TOP:upper, :] = form[t, sec, 0 : upper - TOP, :]
+        frame[sec, c, lower : TOP + FORM_H, :] = form[t, sec, lower - TOP :, :]
+    frame[sec, c, 0:TOP, :] = top[t, sec, 0:TOP, :]
+    frame[sec, c, 544:600, :] = bottom[t, sec, 8:EDGE_H, :]
+    frame[sec, c, 600:608, :] = jnp.zeros((8, 128), jnp.bfloat16)
+    for dst, own, other in (
+        (TOP, form[t, sec, 0:8, :], top[t, sec, TOP:EDGE_H, :]),
+        (536, form[t, sec, 480:488, :], bottom[t, sec, 0:8, :]),
+    ):
+        both = own.astype(jnp.float32) + other.astype(jnp.float32)
+        frame[sec, c, dst : dst + 8, :] = both.astype(jnp.bfloat16)
+
+
+def run_steps(step_of, count, base, fa, fb, second, mix_rows, mix_cols, sign_cols, raw, raw_end, work):
+    spec, cross, flow_rows, flow_cols = work
     sub = lax.broadcasted_iota(jnp.int32, (8, 256), 0)
     top = sub == 0
     top_half = jnp.where(top, 0.5, 1.0)
@@ -185,13 +183,13 @@
     end_weight = jnp.where((k_lane == 0) | (k_lane == HALF), -4.0, -8.0)
 
     def row_of(m):
-        valid = (m >= 0) & (m < GROUPS * 12)
-        near = jnp.clip(m, 0, GROUPS * 12 - 1)
-        return near // 12, jnp.where(valid, near % 12, 15), (near % 12) // 2
+        valid = (m >= 0) & (m < count)
+        n, i = step_of(jnp.clip(m, 0, count - 1))
+        return n, jnp.where(valid, i, 15), i // 2
 
     def spectra(m, parity):
         g, _, q = row_of(m)
-        start = pl.multiple_of(80 * q + 32 * parity, 16)
+        start = pl.multiple_of(80 * q + (32 * parity - base), 16)
         spec[parity, 0] = dot(second[parity], fa[g, pl.ds(start, 176), :])
         spec[parity, 1] = dot(second[parity], fb[g, pl.ds(start, 176), :])
 
@@ -266,9 +264,6 @@
                 flow_x = flow_x + cosines[t] * mixed[t]
         raw[g, pl.ds(i, 1), 512:768] = jnp.sum(flow_x, axis=0, keepdims=True)
 
-    raw_end[...] = jnp.zeros((GROUPS, 8, 128), jnp.float32)
-    raw[:, 12:16, :] = jnp.zeros((GROUPS, 4, 1280), jnp.float32)
-
     def step(n, carry):
         for parity in range(2):
             m = 2 * n + parity
@@ -278,45 +273,253 @@
             spectra(m, parity)
         return carry
 
-    lax.fori_loop(0, GROUPS * 6 + 2, step, 0)
-    sums = dot_exact(raw[...].reshape(GROUPS * 16, 1280), select[...].astype(jnp.float32))
-    sums = sums.reshape(GROUPS, 16, 128)
+    lax.fori_loop(0, count // 2 + 2, step, 0)
+
+
+def finish(raw, raw_end, cells, select, window, groups):
+    window = window[...].astype(jnp.float32)
+    scale = (1.0 / (PATCH * PATCH)) / (
+        window_means(cells, 0, window, groups) * window_means(cells, 1, window, groups)
+    )
+    sums = dot_exact(raw[...].reshape(WIN * 16, 1280), select[...].astype(jnp.float32)).reshape(WIN, 16, 128)
+    pad = jnp.zeros((120, 128), jnp.float32)
     ends = [
-        pltpu.roll(jnp.concatenate([raw_end[g], jnp.zeros((120, 128), jnp.float32)], axis=0).T[:16], 32, axis=1)
-        for g in range(GROUPS)
+        pltpu.roll(jnp.concatenate([raw_end[n], pad], axis=0).T[:16], 32, axis=1) for n in range(WIN)
     ]
-    total = spread_groups([sums[g] + ends[g] for g in range(GROUPS)])
-    scale = (1.0 / (PATCH * PATCH)) / (mean_a * mean_b)
+    total = spread_groups([sums[n] + ends[n] for n in range(WIN)], groups)
     unit = (2.0 / (PATCH * PATCH)) ** 2 * HALF / (PATCH * PATCH)
     total = total * (scale * unit)
     lane_all = lax.broadcasted_iota(jnp.int32, (16, 128), 1)
     weight = jnp.where(lane_all >= 64, total * HALF, 0.0)
     down = 1.0 + weight + pltpu.roll(weight, 96, axis=1) + pltpu.roll(weight, 64, axis=1)
-    out[...] = jnp.where(lane_all >= 64, weight, total) / down
-
-
-def correlate(form, top, bottom, left, right):
+    return jnp.where(lane_all >= 64, weight, total) / down
+
+
+def clear_sums(raw, raw_end):
+    raw[:, 12:16, :] = jnp.zeros((WIN, 4, 1280), jnp.float32)
+    raw_end[...] = jnp.zeros((WIN, 8, 128), jnp.float32)
+
+
+def early_step(m):
+    return m // 8, 2 + m % 8
+
+
+def edge_step(m):
+    return m // 12, m % 12
+
+
+def late_step(m):
+    return m // 4, m % 4 + jnp.where(m % 4 >= 2, 8, 0)
+
+
+def early_kernel(
+    form, first, second, mix_rows, mix_cols, sign_cols, select, window, out, grp, fa, fb, cells, raw, raw_end, *work
+):
+    lo, hi = INNER_LO - TOP, INNER_HI - TOP
+    clear_sums(raw, raw_end)
+    raw[:, 0:2, :] = jnp.zeros((WIN, 2, 1280), jnp.float32)
+    raw[:, 10:12, :] = jnp.zeros((WIN, 2, 1280), jnp.float32)
+    for sec, dst in ((0, fa), (1, fb)):
+        cells[sec] = jnp.zeros((24, 256 * WIN), jnp.float32)
+        for n, g in enumerate(INNER_GROUPS):
+            pixels = group_pixels(lambda c: form[c - 1, sec, lo:hi, :], sec, g)
+            grp[sec, n] = pixels
+            dst[n] = dot(pixels, first[...]).astype(jnp.bfloat16)
+            cell_squares(grp, sec, n, cells, 2, 13, INNER_LO)
+    run_steps(
+        early_step, 24, INNER_LO, fa, fb, second, mix_rows, mix_cols, sign_cols, raw, raw_end, work
+    )
+    out[...] = finish(raw, raw_end, cells, select, window, INNER_GROUPS)
+
+
+def mesh_fields(result, valid):
+    row = lax.broadcasted_iota(jnp.int32, (16, 128), 0)
+    lane = lax.broadcasted_iota(jnp.int32, (16, 128), 1)
+    column = lane % 32
+    inside = (row < 12) & (lane < 96) & (column >= SWEEPS) & (column < SWEEPS + 16)
+    flags = jnp.concatenate([valid[...].astype(jnp.float32), jnp.zeros((12, 112), jnp.float32)], axis=1)
+    flags = jnp.concatenate([flags, jnp.zeros((4, 128), jnp.float32)], axis=0)
+    flags = sum(pltpu.roll(flags, SWEEPS + 32 * kind, axis=1) for kind in range(3))
+    fields = flags * pltpu.roll(jnp.where(row < 12, result, 0.0), SWEEPS, axis=1)
+    fields = fields + jnp.where(lane >= 64, 4.0 * stiffness, 0.0)
+    return jnp.where(inside, fields, 0.0), column
+
+
+def edge_kernel(
+    form, top, bottom, left, right, valid, first, second, mix_rows, mix_cols, sign_cols, select, window,
+    out, to_right, to_left, frame, grp, fa, fb, cells, raw, raw_end, *work,
+):
+    clear_sums(raw, raw_end)
+    for sec, dst in ((0, fa), (1, fb)):
+        frame[sec, 0] = left[sec]
+        frame[sec, 9] = right[sec]
+        for c in (1, 2, 3, 6, 7, 8):
+            frame_column(form, top, bottom, frame, sec, c, FRAME_H, FRAME_H)
+        for n, g in enumerate(EDGE_GROUPS):
+            pixels = group_pixels(lambda c: frame[sec, c], sec, g)
+            grp[sec, n] = pixels
+            dst[n] = dot(pixels, first[...]).astype(jnp.bfloat16)
+            cell_squares(grp, sec, n, cells, 0, 15, 0)
+        cells[sec, 15:24, :] = jnp.zeros((9, 256 * WIN), jnp.float32)
+    run_steps(edge_step, 36, 0, fa, fb, second, mix_rows, mix_cols, sign_cols, raw, raw_end, work)
+    result = finish(raw, raw_end, cells, select, window, EDGE_GROUPS)
+    out[...] = result
+    fields, column = mesh_fields(result, valid)
+    last = jnp.where((column >= 16) & (column < 16 + SWEEPS), fields, 0.0)
+    to_right[...] = pltpu.roll(last, 112, axis=1)
+    head = jnp.where((column >= SWEEPS) & (column < 2 * SWEEPS), fields, 0.0)
+    to_left[...] = pltpu.roll(head, 16, axis=1)
+
+
+def late_kernel(
+    form, top, bottom, early, edge, valid, first, second, mix_rows, mix_cols, sign_cols, select, window,
+    out, fields, frame, grp, fa, fb, cells, raw, raw_end, *work,
+):
+    upper, lower = 208, 400
+    clear_sums(raw, raw_end)
+    raw[:, 2:10, :] = jnp.zeros((WIN, 8, 1280), jnp.float32)
+    for sec, dst in ((0, fa), (1, fb)):
+        cells[sec] = jnp.zeros((24, 256 * WIN), jnp.float32)
+        for c in range(1, 8):
+            frame_column(form, top, bottom, frame, sec, c, upper, lower)
+        for n, g in enumerate(INNER_GROUPS):
+            for lo, hi in ((0, upper), (lower, FRAME_H)):
+                pixels = group_pixels(lambda c: frame[sec, c, lo:hi, :], sec, g)
+                grp[sec, n, lo:hi, :] = pixels
+                dst[n, lo:hi, :] = dot(pixels, first[...]).astype(jnp.bfloat16)
+            cell_squares(grp, sec, n, cells, 0, 5, 0)
+            cell_squares(grp, sec, n, cells, 10, 15, 0)
+    run_steps(late_step, 12, 0, fa, fb, second, mix_rows, mix_cols, sign_cols, raw, raw_end, work)
+    row = lax.broadcasted_iota(jnp.int32, (16, 128), 0)
+    lane = lax.broadcasted_iota(jnp.int32, (16, 128), 1) % 32
+    own = finish(raw, raw_end, cells, select, window, INNER_GROUPS)
+    own = jnp.where((row >= 2) & (row < 10), early[...], own)
+    result = jnp.where((lane >= 3) & (lane < 12), own, edge[...])
+    out[...] = result
+    fields[...] = mesh_fields(result, valid)[0]
+
+
+def relax_kernel(result, fields, above, beneath, flow, mesh_out):
+    frame = jnp.concatenate(
+        [above[...][1:4], fields[...][:12], beneath[...][:SWEEPS], jnp.zeros((6, 128), jnp.float32)],
+        axis=0,
+    )
+    lane = lax.broadcasted_iota(jnp.int32, (24, 128), 1)
+    below = jnp.where(lane < 32, pltpu.roll(frame, 64, axis=1), pltpu.roll(frame, 96, axis=1))
+    inside = (below > 0.0) & (lane < 64)
+    rest = jnp.where(inside, 1.0 / jnp.where(inside, below, 1.0), 0.0)
+    mesh = jnp.where(lane < 64, frame, 0.0)
+    pull = mesh * jnp.where(inside, below - 4.0 * stiffness, 0.0)
+    for _ in range(SWEEPS):
+        around = (
+            pltpu.roll(mesh, 1, axis=0)
+            + pltpu.roll(mesh, 23, axis=0)
+            + pltpu.roll(mesh, 1, axis=1)
+            + pltpu.roll(mesh, 127, axis=1)
+        )
+        mesh = (pull + stiffness * around) * rest
+    for kind in range(2):
+        flow[kind] = result[0:12, 32 * kind : 32 * kind + 16]
+        mesh_out[kind] = mesh[SWEEPS : SWEEPS + 12, 32 * kind + SWEEPS : 32 * kind + SWEEPS + 16]
+
+
+def work_shapes():
+    return [
+        pltpu.VMEM((2, 2, ROWS, 512), jnp.float32),
+        pltpu.VMEM((2, ROWS, 512), jnp.bfloat16),
+        pltpu.VMEM((2, HALF + 8, 512), jnp.float32),
+        pltpu.VMEM((2, ROWS, 256), jnp.float32),
+    ]
+
+
+SUM_SHAPES = (
+    ((2, 24, 256 * WIN), jnp.float32),
+    ((WIN, 16, 1280), jnp.float32),
+    ((WIN, 8, 128), jnp.float32),
+)
+
+
+def sum_shapes(make):
+    return [make(*shape) for shape in SUM_SHAPES]
+
+
+def grow_params(mib):
+    return pltpu.CompilerParams(vmem_limit_bytes=mib << 20)
+
+
+def frame_shapes():
+    return [
+        pltpu.VMEM((2, 10, FRAME_H, 128), jnp.bfloat16),
+        pltpu.VMEM((2, WIN, FRAME_H, 256), jnp.bfloat16),
+        pltpu.VMEM((WIN, FRAME_H, 512), jnp.bfloat16),
+        pltpu.VMEM((WIN, FRAME_H, 512), jnp.bfloat16),
+        *sum_shapes(pltpu.VMEM),
+        *work_shapes(),
+    ]
+
+
+SMALL = jax.ShapeDtypeStruct((16, 128), jnp.float32)
+
+
+def correlate_early(form, consts):
+    height = INNER_HI - INNER_LO
     return pl.pallas_call(
-        correlate_kernel,
-        out_shape=jax.ShapeDtypeStruct((16, 128), jnp.float32),
+        early_kernel,
+        out_shape=SMALL,
+        in_specs=[VMEM_SPEC] * 8,
+        out_specs=VMEM_SPEC,
         scratch_shapes=[
-            pltpu.VMEM((2, 10, FRAME_H, 128), jnp.bfloat16),
-            pltpu.VMEM((2, GROUPS, FRAME_H, 256), jnp.bfloat16),
-            pltpu.VMEM((GROUPS, FIRST_H, 512), jnp.bfloat16),
-            pltpu.VMEM((GROUPS, FIRST_H, 512), jnp.bfloat16),
-            pltpu.VMEM((24, 256 * GROUPS), jnp.float32),
-            pltpu.VMEM((GROUPS, 16, 1280), jnp.float32),
-            pltpu.VMEM((GROUPS, 8, 128), jnp.float32),
-            pltpu.VMEM((2, 2, ROWS, 512), jnp.float32),
-            pltpu.VMEM((2, ROWS, 512), jnp.bfloat16),
-            pltpu.VMEM((2, HALF + 8, 512), jnp.float32),
-            pltpu.VMEM((2, ROWS, 256), jnp.float32),
+            pltpu.VMEM((2, WIN, height, 256), jnp.bfloat16),
+            pltpu.VMEM((WIN, height, 512), jnp.bfloat16),
+            pltpu.VMEM((WIN, height, 512), jnp.bfloat16),
+            *sum_shapes(pltpu.VMEM),
+            *work_shapes(),
         ],
-        compiler_params=pltpu.CompilerParams(vmem_limit_bytes=40 << 20),
-    )(form, top, bottom, left, right, *tables())
-
-
-def pack_kernel(a_tiles, b_tiles, a_owner, b_owner, a_offset, b_offset, out, rows):
+        compiler_params=grow_params(20),
+    )(form, *consts)
+
+
+def correlate_edge(form, top, bottom, left, right, valid, consts):
+    return pl.pallas_call(
+        edge_kernel,
+        out_shape=(SMALL,) * 3,
+        in_specs=[VMEM_SPEC] * 13,
+        out_specs=(VMEM_SPEC,) * 3,
+        scratch_shapes=frame_shapes(),
+        compiler_params=grow_params(24),
+    )(form, top, bottom, left, right, valid, *consts)
+
+
+def correlate_late(form, top, bottom, early, edge, valid, consts):
+    return pl.pallas_call(
+        late_kernel,
+        out_shape=(SMALL,) * 2,
+        in_specs=[VMEM_SPEC] * 13,
+        out_specs=(VMEM_SPEC,) * 2,
+        scratch_shapes=frame_shapes(),
+        compiler_params=grow_params(24),
+    )(form, top, bottom, early, edge, valid, *consts)
+
+
+def relax(result, fields, above, beneath):
+    field = jax.ShapeDtypeStruct((2, 12, 16), jnp.float32)
+    return pl.pallas_call(
+        relax_kernel,
+        out_shape=(field, field),
+        in_specs=[VMEM_SPEC] * 4,
+        out_specs=(VMEM_SPEC,) * 2,
+        compiler_params=grow_params(8),
+    )(result, fields, above, beneath)
+
+
+def pack_kernel(*refs):
+    sources, out, rows, held, arrived = refs[:6], refs[6], refs[7], refs[8:14], refs[14]
+    copies = [pltpu.make_async_copy(src, dst, arrived.at[n]) for n, (src, dst) in enumerate(zip(sources, held))]
+    for copy in copies:
+        copy.start()
+    for copy in copies:
+        copy.wait()
+    a_tiles, b_tiles, a_owner, b_owner, a_offset, b_offset = held
     count = a_tiles.shape[0]
     owners = jnp.concatenate([a_owner[...], b_owner[...]], axis=1)
     slot = lax.broadcasted_iota(jnp.int32, (128, 2 * count), 0)
@@ -400,7 +603,6 @@
     for u in range(0, 8, 2):
         tails = jnp.concatenate([slot_row(TILE_H + u + v + w) for v in range(2) for w in (0, 8)], axis=1)
         tails = dot(select_b, tails)
-        mains = {}
         for k in range(5):
             y = 8 * k + u
             main = dot(select, jnp.concatenate([slot_row(y), slot_row(y + 1)], axis=1))
@@ -429,16 +631,19 @@
             down[t, sec] = plane[FORM_H * t + 424 : FORM_H * t + 488, :].astype(jnp.bfloat16)
 
 
-VMEM_SPEC = pl.BlockSpec(memory_space=pltpu.VMEM)
-
-
-def pack(a_tiles, b_tiles, a_owner, b_owner, a_offset, b_offset):
+def pack(*arrays):
     return pl.pallas_call(
         pack_kernel,
         out_shape=jax.ShapeDtypeStruct((128, SLOT_H, 128), jnp.bfloat16),
-        scratch_shapes=[pltpu.VMEM((128 * SLOT_H, 128), jnp.float32)],
-        compiler_params=pltpu.CompilerParams(vmem_limit_bytes=16 << 20),
-    )(a_tiles, b_tiles, a_owner[None], b_owner[None], a_offset.T, b_offset.T)
+        in_specs=[pl.BlockSpec(memory_space=pltpu.HBM)] * 6,
+        out_specs=VMEM_SPEC,
+        scratch_shapes=[
+            pltpu.VMEM((128 * SLOT_H, 128), jnp.float32),
+            *[pltpu.VMEM(x.shape, x.dtype) for x in arrays],
+            pltpu.SemaphoreType.DMA((6,)),
+        ],
+        compiler_params=pltpu.CompilerParams(vmem_limit_bytes=60 << 20),
+    )(*arrays)
 
 
 def place(got):
@@ -458,19 +663,6 @@
     )(got)
 
 
-def extended_2(block, sides, width):
-    for axis, dim in sides:
-        count = lax.axis_size(axis)
-        forward = [(i, i + 1) for i in range(count - 1)]
-        backward = [(target, source) for source, target in forward]
-        low = lax.ppermute(
-            lax.slice_in_dim(block, block.shape[dim] - width, None, axis=dim), axis, forward
-        )
-        high = lax.ppermute(lax.slice_in_dim(block, 0, width, axis=dim), axis, backward)
-        block = jnp.concatenate([low, block, high], axis=dim)
-    return block
-
-
 def shifted(block, axis, step):
     count = lax.axis_size(axis)
     pairs = [(i, i + step) for i in range(count) if 0 <= i + step < count]
@@ -483,33 +675,23 @@
 
 
 def per_device(a_tiles, a_owner, a_offset, b_tiles, b_owner, b_offset, patch_valid):
-    grid_rows, grid_cols = patch_valid.shape
-    packed = pack(a_tiles, b_tiles, a_owner, b_owner, a_offset, b_offset)
+    packed = pack(a_tiles, b_tiles, a_owner[None], b_owner[None], a_offset.T, b_offset.T)
     got = lax.all_to_all(packed, ("row", "col"), split_axis=0, concat_axis=0, tiled=True)
     form, up, down, low, high = place(got)
+    consts = tables()
     top = shifted(down, "row", 1)
     bottom = shifted(up, "row", -1)
+    early = correlate_early(form, consts)
     left = shifted(column(high, top, bottom, TX - 1), "col", 1)
     right = shifted(column(low, top, bottom, 0), "col", -1)
-    result = correlate(form, top, bottom, left, right)
-    flow_field = jnp.stack([result[:grid_rows, :grid_cols], result[:grid_rows, 32 : 32 + grid_cols]])
-    confidence = result[:grid_rows, 64 : 64 + grid_cols]
-    valid_float = patch_valid.astype(jnp.float32)
-    strength = valid_float * confidence
-    start = valid_float[None] * flow_field
-    fields = jnp.concatenate([start, (strength + 4.0 * stiffness)[None]])
-    fields = extended_2(fields, (("row", 1), ("col", 2)), SWEEPS)
-    mesh = fields[:2]
-    below = fields[2]
-    inside = below > 0.0
-    rest = jnp.where(inside, 1.0 / jnp.where(inside, below, 1.0), 0.0)
-    pull = mesh * jnp.where(inside, below - 4.0 * stiffness, 0.0)
-    for sweep_index in range(SWEEPS):
-        around = mesh[:, :-2, 1:-1] + mesh[:, 2:, 1:-1] + mesh[:, 1:-1, :-2] + mesh[:, 1:-1, 2:]
-        rest = rest[1:-1, 1:-1]
-        pull = pull[:, 1:-1, 1:-1]
-        mesh = (pull + stiffness * around) * rest
-    return (flow_field, mesh)
+    edge, to_right, to_left = correlate_edge(form, top, bottom, left, right, patch_valid, consts)
+    from_left = shifted(to_right, "col", 1)
+    from_right = shifted(to_left, "col", -1)
+    result, fields = correlate_late(form, top, bottom, early, edge, patch_valid, consts)
+    fields = fields + from_left + from_right
+    above = shifted(fields[8:16], "row", 1)
+    beneath = shifted(fields[0:8], "row", -1)
+    return relax(result, fields, above, beneath)
 
 
 def solution(mesh):

time: 118 us -> 116 us (0.983)
  the two profiles are of different devices: /device:TPU:27 before, /device:TPU:34 now
where the time goes in v4:
time: 116 us
  blocking collectives  36.7 us (32%)
  Pallas kernels  36.5 us (31%)
  starting transfers between devices  23.7 us (20%)
  waiting for transfers between devices  16.6 us (14%)
  local copies, waits for them, and re-layouts  1.28 us (1%)
    all_to_all x1, blocking collectives, per_device(): lax.all_to_all(packed, ('row', 'col'), split_axis=0, concat_axis=0, tiled...  36.7 us
    ppermute x8, starting transfers between devices, shifted(): return lax.ppermute(block, axis, pairs)  23.7 us
    ppermute x8, waiting for transfers between devices, shifted(): return lax.ppermute(block, axis, pairs)  16.6 us
    pallas_call x1, Pallas kernels, correlate_edge(): pl.pallas_call(edge_kernel, out_shape=(SMALL,) * 3, in_specs=[VMEM_SPEC]...  13.8 us
    pallas_call x1, Pallas kernels, correlate_early(): pl.pallas_call(early_kernel, out_shape=SMALL, in_specs=[VMEM_SPEC] * 8, o...  9.82 us
    pallas_call x1, Pallas kernels, correlate_late(): pl.pallas_call(late_kernel, out_shape=(SMALL,) * 2, in_specs=[VMEM_SPEC]...  6.43 us
    pallas_call x1, Pallas kernels, pack(): pl.pallas_call(pack_kernel, out_shape=jax.ShapeDtypeStruct((128, SLOT_H,...  4.11 us
  transfers between devices with their start and end apart: 8, of which 5 were waited for; matrix products, arithmetic and copies ran while one was open for 0% of the time, Pallas kernels for 14%

profile of v4, /device:TPU:34, one launch (start us, length us, event | category | flops | bytes accessed | tf_op | source)
XLA Modules:
  0.0 115.6 jit_solution(6224409594286010230)
XLA Ops:
  0.6 4.1 %shard_map.149 = bf16[128,56,128]{2,1,0:T(8,128)(2,1)} custom-call(bf16[96,3200]{1,0:T(8,128)(2,1)} %refs_0_.1, bf16[96,3200]{1,0:T(8,128)(2,1)} %refs_1_.1, s32[1,96]{1,0:T(1,128)} %bitcast.14, s32[1,96]{1,0:T(1,128)} %bitcast.15, s32[2,96]{1,0:T(2,128)} %bitcast.12, s32[2,96]{1,0:T(2,128)} %bitcast.13), custom_call_target="tpu_custom_call" | custom-call | tf_op jit(solution)/shard_map/pallas_call | solution.py:635
  4.8 36.7 %all_to_all.5.got = bf16[128,56,128]{2,1,0:T(8,128)(2,1)S(1)} all-to-all(bf16[128,56,128]{2,1,0:T(8,128)(2,1)} %shard_map.149), channel_id=1, replica_groups=mesh['row'=4,'col'=32] {'row','col'}, dimensions={0} | all-to-all | bytes 3670016 | tf_op jit(solution)/shard_map/all_to_all | solution.py:679
  41.4 0.0 copy-start
  41.4 0.0 copy-start.1
  41.4 0.0 copy-start.2
  41.4 0.0 copy-start.3
  41.4 0.0 copy-start.4
  41.4 0.0 copy-start.5
  41.4 0.0 copy-start.6
  41.5 0.0 copy-start.7
  41.5 2.1 %shard_map.150 = (bf16[8,2,488,128]{3,2,1,0:T(8,128)(2,1)S(1)}, bf16[8,2,64,128]{3,2,1,0:T(8,128)(2,1)S(1)}, bf16[8,2,64,128]{3,2,1,0:T(8,128)(2,1)S(1)}, bf16[2...) custom-call(bf16[128,56,128]{2,1,0:T(8,128)(2,1)S(1)} %all_to_all.5.got), custom_call_target="tpu_custom_call" | custom-call | tf_op jit(solution)/shard_map/pallas_call | solution.py:652
  43.5 1.9 %collective-permute-start = (bf16[8,2,64,128]{3,2,1,0:T(8,128)(2,1)S(1)}, bf16[8,2,64,128]{3,2,1,0:T(8,128)(2,1)S(1)}, u32[]{:S(2)}, u32[]{:S(2)}) collective-permute-start(bf16[8,2,64,128]{3,2,1,0:T(8,128)(2,1)S(1)} %get-tuple-element.13), channel_id=1, source_target_pairs={{0,32},{32,64},{64,96},{1,33},{33,65},{65,97},{2,34},{34,66},{66,9... | collective-permute-start | bytes 786440 | tf_op jit(solution)/shard_map/ppermute | solution.py:669
  45.5 3.9 %collective-permute-start.1 = (bf16[8,2,64,128]{3,2,1,0:T(8,128)(2,1)S(1)}, bf16[8,2,64,128]{3,2,1,0:T(8,128)(2,1)S(1)}, u32[]{:S(2)}, u32[]{:S(2)}) collective-permute-start(bf16[8,2,64,128]{3,2,1,0:T(8,128)(2,1)S(1)} %get-tuple-element.14), channel_id=1, source_target_pairs={{32,0},{64,32},{96,64},{33,1},{65,33},{97,65},{34,2},{66,34},{98,6... | collective-permute-start | bytes 786440 | tf_op jit(solution)/shard_map/ppermute | solution.py:669
  49.4 3.5 %collective-permute-done.top = bf16[8,2,64,128]{3,2,1,0:T(8,128)(2,1)S(1)} collective-permute-done((bf16[8,2,64,128]{3,2,1,0:T(8,128)(2,1)S(1)}, bf16[8,2,64,128]{3,2,1,0:T(8,128)(2,1)S(1)}, u32[]{:S(2)}, u32[]{:S(2)}) %collective-permute-start) | collective-permute-done | bytes 262176 | tf_op jit(solution)/shard_map/ppermute | solution.py:669
  52.9 1.9 %collective-permute-done.1.bottom = bf16[8,2,64,128]{3,2,1,0:T(8,128)(2,1)S(1)} collective-permute-done((bf16[8,2,64,128]{3,2,1,0:T(8,128)(2,1)S(1)}, bf16[8,2,64,128]{3,2,1,0:T(8,128)(2,1)S(1)}, u32[]{:S(2)}, u32[]{:S(2)}) %collective-permute-start.1) | collective-permute-done | bytes 262176 | tf_op jit(solution)/shard_map/ppermute | solution.py:669
  54.9 1.9 %collective-permute-start.3 = (bf16[2,608,128]{2,1,0:T(8,128)(2,1)S(1)}, bf16[2,608,128]{2,1,0:T(8,128)(2,1)S(1)}, u32[]{:S(2)}, u32[]{:S(2)}) collective-permute-start(bf16[2,608,128]{2,1,0:T(8,128)(2,1)S(1)} %pad_add_fusion), channel_id=1, source_target_pairs={{1,0},{2,1},{3,2},{4,3},{5,4},{6,5},{7,6},{8,7},{9,8},{10,9},{11,1... | collective-permute-start | bytes 933896 | tf_op jit(solution)/shard_map/ppermute | solution.py:669
  56.8 2.4 %collective-permute-start.2 = (bf16[2,608,128]{2,1,0:T(8,128)(2,1)S(1)}, bf16[2,608,128]{2,1,0:T(8,128)(2,1)S(1)}, u32[]{:S(2)}, u32[]{:S(2)}) collective-permute-start(bf16[2,608,128]{2,1,0:T(8,128)(2,1)S(1)} %pad_add_fusion.1), channel_id=1, source_target_pairs={{0,1},{1,2},{2,3},{3,4},{4,5},{5,6},{6,7},{7,8},{8,9},{9,10},{10,1... | collective-permute-start | bytes 933896 | tf_op jit(solution)/shard_map/ppermute | solution.py:669
  59.2 1.9 %collective-permute-done.3.right = bf16[2,608,128]{2,1,0:T(8,128)(2,1)S(1)} collective-permute-done((bf16[2,608,128]{2,1,0:T(8,128)(2,1)S(1)}, bf16[2,608,128]{2,1,0:T(8,128)(2,1)S(1)}, u32[]{:S(2)}, u32[]{:S(2)}) %collective-permute-start.3) | collective-permute-done | bytes 311328 | tf_op jit(solution)/shard_map/ppermute | solution.py:669
  61.2 6.0 %collective-permute-done.2.left = bf16[2,608,128]{2,1,0:T(8,128)(2,1)S(1)} collective-permute-done((bf16[2,608,128]{2,1,0:T(8,128)(2,1)S(1)}, bf16[2,608,128]{2,1,0:T(8,128)(2,1)S(1)}, u32[]{:S(2)}, u32[]{:S(2)}) %collective-permute-start.2) | collective-permute-done | bytes 311328 | tf_op jit(solution)/shard_map/ppermute | solution.py:669
  67.2 0.0 copy-done
  67.2 0.0 copy-done.1
  67.2 0.0 copy-done.2
  67.2 0.0 copy-done.3
  67.2 0.0 copy-done.4
  67.2 0.0 copy-done.5
  67.2 0.0 copy-done.6
  67.2 0.0 copy-done.7
  67.2 13.8 %shard_map.152 = (f32[16,128]{1,0:T(8,128)S(1)}, f32[16,128]{1,0:T(8,128)S(1)}, f32[16,128]{1,0:T(8,128)S(1)}) custom-call(bf16[8,2,488,128]{3,2,1,0:T(8,128)(2,1)S(1)} %get-tuple-element.12.form, bf16[8,2,64,128]{3,2,1,0:T(8,128)(2,1)S(1)} %collective-permute-done.top, bf16[8,2,64,128]{3,2,1,0:T(8,128)(2,1)S(1)} %collective-permute-done.1.bottom, ...), custom_call_target="tpu_custom_call" | custom-call | tf_op jit(solution)/shard_map/pallas_call | solution.py:483
  81.0 1.9 %collective-permute-start.4 = (f32[16,128]{1,0:T(8,128)S(1)}, f32[16,128]{1,0:T(8,128)S(1)}, u32[]{:S(2)}, u32[]{:S(2)}) collective-permute-start(f32[16,128]{1,0:T(8,128)S(1)} %get-tuple-element.20), channel_id=1, source_target_pairs={{0,1},{1,2},{2,3},{3,4},{4,5},{5,6},{6,7},{7,8},{8,9},{9,10},{10,1... | collective-permute-start | bytes 24584 | tf_op jit(solution)/shard_map/ppermute | solution.py:669
  82.9 5.8 %collective-permute-start.5 = (f32[16,128]{1,0:T(8,128)S(1)}, f32[16,128]{1,0:T(8,128)S(1)}, u32[]{:S(2)}, u32[]{:S(2)}) collective-permute-start(f32[16,128]{1,0:T(8,128)S(1)} %get-tuple-element.21), channel_id=1, source_target_pairs={{1,0},{2,1},{3,2},{4,3},{5,4},{6,5},{7,6},{8,7},{9,8},{10,9},{11,1... | collective-permute-start | bytes 24584 | tf_op jit(solution)/shard_map/ppermute | solution.py:669
  88.7 9.8 %shard_map.151.early = f32[16,128]{1,0:T(8,128)S(1)} custom-call(bf16[8,2,488,128]{3,2,1,0:T(8,128)(2,1)S(1)} %get-tuple-element.12.form, bf16[256,512]{1,0:T(8,128)(2,1)S(1)} %copy-done.1, bf16[2,160,176]{2,1,0:T(8,128)(2,1)S(1)} %copy-done.2, bf16[88,160]{1,0:T(8,128)(2,1)S(1)} %copy-done.5, bf16[256,256]{1,0:T(8,128)(2,1)S(1)} %copy-done.3, ...), custom_call_target="tpu_custom_call" | custom-call | tf_op jit(solution)/shard_map/pallas_call | solution.py:466
  98.5 6.4 %shard_map.153 = (f32[16,128]{1,0:T(8,128)S(1)}, f32[16,128]{1,0:T(8,128)S(1)}) custom-call(bf16[8,2,488,128]{3,2,1,0:T(8,128)(2,1)S(1)} %get-tuple-element.12.form, bf16[8,2,64,128]{3,2,1,0:T(8,128)(2,1)S(1)} %collective-permute-done.top, bf16[8,2,64,128]{3,2,1,0:T(8,128)(2,1)S(1)} %collective-permute-done.1.bottom, f32[16,128]{1,0:T(8,128)S(1)} %shard_map.151.early, ...), custom_call_target="tpu_custom_call" | custom-call | tf_op jit(solution)/shard_map/pallas_call | solution.py:494
  104.9 0.0 collective-permute-done.4
  104.9 0.0 collective-permute-done.5
  105.0 3.7 %collective-permute-start.7 = (f32[8,128]{1,0:T(8,128)S(1)}, f32[8,128]{1,0:T(8,128)S(1)}, u32[]{:S(2)}, u32[]{:S(2)}) collective-permute-start(f32[8,128]{1,0:T(8,128)S(1)} %get-tuple-element.28), channel_id=1, source_target_pairs={{32,0},{64,32},{96,64},{33,1},{65,33},{97,65},{34,2},{66,34},{98,6... | collective-permute-start | bytes 12296 | tf_op jit(solution)/shard_map/ppermute | solution.py:669
  108.6 2.2 %collective-permute-start.6 = (f32[8,128]{1,0:T(8,128)S(1)}, f32[8,128]{1,0:T(8,128)S(1)}, u32[]{:S(2)}, u32[]{:S(2)}) collective-permute-start(f32[8,128]{1,0:T(8,128)S(1)} %get-tuple-element.29), channel_id=1, source_target_pairs={{0,32},{32,64},{64,96},{1,33},{33,65},{65,97},{2,34},{34,66},{66,9... | collective-permute-start | bytes 12296 | tf_op jit(solution)/shard_map/ppermute | solution.py:669
  110.8 0.0 collective-permute-done.7.beneath
  110.8 3.3 %collective-permute-done.6.above = f32[8,128]{1,0:T(8,128)S(1)} collective-permute-done((f32[8,128]{1,0:T(8,128)S(1)}, f32[8,128]{1,0:T(8,128)S(1)}, u32[]{:S(2)}, u32[]{:S(2)}) %collective-permute-start.6) | collective-permute-done | bytes 4128 | tf_op jit(solution)/shard_map/ppermute | solution.py:669
  114.1 0.3 shard_map.154
  114.4 0.6 copy.16
  115.0 0.6 copy.17
  (6 shorter events, 0.1 us)
Async XLA Ops:
  41.4 25.7 %copy-start = (bf16[1280,128]{1,0:T(8,128)(2,1)S(1)}, bf16[1280,128]{1,0:T(8,128)(2,1)}, u32[]{:S(2)}) copy-start(bf16[1280,128]{1,0:T(8,128)(2,1)} %constant.22.clone.select) | copy-start | bytes 983044
  41.4 25.8 %copy-start.1 = (bf16[256,512]{1,0:T(8,128)(2,1)S(1)}, bf16[256,512]{1,0:T(8,128)(2,1)}, u32[]{:S(2)}) copy-start(bf16[256,512]{1,0:T(8,128)(2,1)} %constant.17.clone.first) | copy-start | bytes 786436
  41.4 25.8 %copy-start.2 = (bf16[2,160,176]{2,1,0:T(8,128)(2,1)S(1)}, bf16[2,160,176]{2,1,0:T(8,128)(2,1)}, u32[]{:S(2)}) copy-start(bf16[2,160,176]{2,1,0:T(8,128)(2,1)} %constant.18.clone.second) | copy-start | bytes 337924
  41.4 25.8 %copy-start.3 = (bf16[256,256]{1,0:T(8,128)(2,1)S(1)}, bf16[256,256]{1,0:T(8,128)(2,1)}, u32[]{:S(2)}) copy-start(bf16[256,256]{1,0:T(8,128)(2,1)} %constant.20.clone.mix_cols) | copy-start | bytes 393220
  41.4 25.8 %copy-start.4 = (bf16[256,128]{1,0:T(8,128)(2,1)S(1)}, bf16[256,128]{1,0:T(8,128)(2,1)}, u32[]{:S(2)}) copy-start(bf16[256,128]{1,0:T(8,128)(2,1)} %constant.23.clone.window) | copy-start | bytes 196612
  41.4 25.8 %copy-start.5 = (bf16[88,160]{1,0:T(8,128)(2,1)S(1)}, bf16[88,160]{1,0:T(8,128)(2,1)}, u32[]{:S(2)}) copy-start(bf16[88,160]{1,0:T(8,128)(2,1)} %constant.19.clone.mix_rows) | copy-start | bytes 84484
  41.4 25.8 %copy-start.6 = (bf16[16,256]{1,0:T(8,128)(2,1)S(1)}, bf16[16,256]{1,0:T(8,128)(2,1)}, u32[]{:S(2)}) copy-start(bf16[16,256]{1,0:T(8,128)(2,1)} %constant.21.clone.sign_cols) | copy-start | bytes 24580
  41.5 25.8 %copy-start.7 = (s32[12,16]{1,0:T(8,128)S(1)}, s32[12,16]{1,0:T(8,128)}, u32[]{:S(2)}) copy-start(s32[12,16]{1,0:T(8,128)} %valid.3) | copy-start | bytes 2308
  43.5 9.4 %collective-permute-start = (bf16[8,2,64,128]{3,2,1,0:T(8,128)(2,1)S(1)}, bf16[8,2,64,128]{3,2,1,0:T(8,128)(2,1)S(1)}, u32[]{:S(2)}, u32[]{:S(2)}) collective-permute-start(bf16[8,2,64,128]{3,2,1,0:T(8,128)(2,1)S(1)} %get-tuple-element.13), channel_id=1, source_target_pairs={{0,32},{32,64},{64,96},{1,33},{33,65},{65,97},{2,34},{34,66},{66,9... | collective-permute-start | bytes 786440 | tf_op jit(solution)/shard_map/ppermute | solution.py:669
  45.5 9.4 %collective-permute-start.1 = (bf16[8,2,64,128]{3,2,1,0:T(8,128)(2,1)S(1)}, bf16[8,2,64,128]{3,2,1,0:T(8,128)(2,1)S(1)}, u32[]{:S(2)}, u32[]{:S(2)}) collective-permute-start(bf16[8,2,64,128]{3,2,1,0:T(8,128)(2,1)S(1)} %get-tuple-element.14), channel_id=1, source_target_pairs={{32,0},{64,32},{96,64},{33,1},{65,33},{97,65},{34,2},{66,34},{98,6... | collective-permute-start | bytes 786440 | tf_op jit(solution)/shard_map/ppermute | solution.py:669
  54.9 6.3 %collective-permute-start.3 = (bf16[2,608,128]{2,1,0:T(8,128)(2,1)S(1)}, bf16[2,608,128]{2,1,0:T(8,128)(2,1)S(1)}, u32[]{:S(2)}, u32[]{:S(2)}) collective-permute-start(bf16[2,608,128]{2,1,0:T(8,128)(2,1)S(1)} %pad_add_fusion), channel_id=1, source_target_pairs={{1,0},{2,1},{3,2},{4,3},{5,4},{6,5},{7,6},{8,7},{9,8},{10,9},{11,1... | collective-permute-start | bytes 933896 | tf_op jit(solution)/shard_map/ppermute | solution.py:669
  56.8 10.3 %collective-permute-start.2 = (bf16[2,608,128]{2,1,0:T(8,128)(2,1)S(1)}, bf16[2,608,128]{2,1,0:T(8,128)(2,1)S(1)}, u32[]{:S(2)}, u32[]{:S(2)}) collective-permute-start(bf16[2,608,128]{2,1,0:T(8,128)(2,1)S(1)} %pad_add_fusion.1), channel_id=1, source_target_pairs={{0,1},{1,2},{2,3},{3,4},{4,5},{5,6},{6,7},{7,8},{8,9},{9,10},{10,1... | collective-permute-start | bytes 933896 | tf_op jit(solution)/shard_map/ppermute | solution.py:669
  81.0 23.9 %collective-permute-start.4 = (f32[16,128]{1,0:T(8,128)S(1)}, f32[16,128]{1,0:T(8,128)S(1)}, u32[]{:S(2)}, u32[]{:S(2)}) collective-permute-start(f32[16,128]{1,0:T(8,128)S(1)} %get-tuple-element.20), channel_id=1, source_target_pairs={{0,1},{1,2},{2,3},{3,4},{4,5},{5,6},{6,7},{7,8},{8,9},{9,10},{10,1... | collective-permute-start | bytes 24584 | tf_op jit(solution)/shard_map/ppermute | solution.py:669
  82.9 22.0 %collective-permute-start.5 = (f32[16,128]{1,0:T(8,128)S(1)}, f32[16,128]{1,0:T(8,128)S(1)}, u32[]{:S(2)}, u32[]{:S(2)}) collective-permute-start(f32[16,128]{1,0:T(8,128)S(1)} %get-tuple-element.21), channel_id=1, source_target_pairs={{1,0},{2,1},{3,2},{4,3},{5,4},{6,5},{7,6},{8,7},{9,8},{10,9},{11,1... | collective-permute-start | bytes 24584 | tf_op jit(solution)/shard_map/ppermute | solution.py:669
  105.0 5.9 %collective-permute-start.7 = (f32[8,128]{1,0:T(8,128)S(1)}, f32[8,128]{1,0:T(8,128)S(1)}, u32[]{:S(2)}, u32[]{:S(2)}) collective-permute-start(f32[8,128]{1,0:T(8,128)S(1)} %get-tuple-element.28), channel_id=1, source_target_pairs={{32,0},{64,32},{96,64},{33,1},{65,33},{97,65},{34,2},{66,34},{98,6... | collective-permute-start | bytes 12296 | tf_op jit(solution)/shard_map/ppermute | solution.py:669
  108.6 5.5 %collective-permute-start.6 = (f32[8,128]{1,0:T(8,128)S(1)}, f32[8,128]{1,0:T(8,128)S(1)}, u32[]{:S(2)}, u32[]{:S(2)}) collective-permute-start(f32[8,128]{1,0:T(8,128)S(1)} %get-tuple-element.29), channel_id=1, source_target_pairs={{0,32},{32,64},{64,96},{1,33},{33,65},{65,97},{2,34},{34,66},{66,9... | collective-permute-start | bytes 12296 | tf_op jit(solution)/shard_map/ppermute | solution.py:669

commit v5 on v4

--- a/solution.py
+++ b/solution.py
@@ -18,6 +18,7 @@
 WIN = 3
 GROUPS = 6
 ROWS = PATCH
+PAIR_H = 208
 TILE_H = 40
 TILE_W = 80
 SPLIT = 128 - TILE_W
@@ -52,9 +53,10 @@
         first[rows, FREQ * w : FREQ * (w + 1)] = cosine.T
         first[rows, 256 + FREQ * w : 256 + FREQ * (w + 1)] = sine.T
     mixed = np.concatenate([cosine[HALF:], sine[1:HALF], cosine[:HALF]])
-    second = np.zeros((2, ROWS, 176))
+    second = np.zeros((2, ROWS, PAIR_H))
     for parity in range(2):
-        second[parity, :, 8 * parity : 8 * parity + PATCH] = mixed
+        second[parity, :, STRIDE * parity : STRIDE * parity + PATCH] = mixed
+    second = second.reshape(2 * ROWS, PAIR_H)
     half = np.ones((FREQ, 1))
     half[0] = half[HALF] = 0.5
     shift = np.where(np.arange(PATCH) < HALF, np.arange(PATCH), np.arange(PATCH) - PATCH) * (16.0 / PATCH)
@@ -173,7 +175,7 @@
         frame[sec, c, dst : dst + 8, :] = both.astype(jnp.bfloat16)
 
 
-def run_steps(step_of, count, base, fa, fb, second, mix_rows, mix_cols, sign_cols, raw, raw_end, work):
+def run_steps(step_of, pairs, base, fa, fb, second, mix_rows, mix_cols, sign_cols, raw, raw_end, work):
     spec, cross, flow_rows, flow_cols = work
     sub = lax.broadcasted_iota(jnp.int32, (8, 256), 0)
     top = sub == 0
@@ -182,98 +184,121 @@
     k_lane = lax.broadcasted_iota(jnp.int32, (8, ROWS), 1)
     end_weight = jnp.where((k_lane == 0) | (k_lane == HALF), -4.0, -8.0)
 
-    def row_of(m):
-        valid = (m >= 0) & (m < count)
-        n, i = step_of(jnp.clip(m, 0, count - 1))
-        return n, jnp.where(valid, i, 15), i // 2
-
-    def spectra(m, parity):
-        g, _, q = row_of(m)
-        start = pl.multiple_of(80 * q + (32 * parity - base), 16)
-        spec[parity, 0] = dot(second[parity], fa[g, pl.ds(start, 176), :])
-        spec[parity, 1] = dot(second[parity], fb[g, pl.ds(start, 176), :])
-
-    def products(m, parity):
-        g, i, _ = row_of(m)
-        total = None
-        for half in range(2):
-            sides = []
-            for sec in range(2):
-                sides.append([])
-                for base in (HALF, 0):
-                    for lo in (0, 256):
-                        sides[sec].append(
-                            spec[parity, sec, base : base + HALF, lo : lo + 256].reshape(10, 8, 256)[5 * half : 5 * half + 5]
-                        )
-            terms = [(cc - ss, sc + cs, cc + ss, sc - cs) for cc, cs, sc, ss in sides]
-            (a1, a2, a3, a4), (b1, b2, b3, b4) = terms
-            plus_r = a1 * b1 + a2 * b2
-            plus_i = a1 * b2 - a2 * b1
-            minus_r = a3 * b3 + a4 * b4
-            minus_i = a3 * b4 - a4 * b3
-            dcc = plus_r + minus_r
-            dss = minus_r - plus_r
-            dsc = plus_i + minus_i
-            dcs = plus_i - minus_i
-            if half == 0:
-                (ac, asn, ae, aes), (bc, bsn, be, bes) = [[x[0] for x in side] for side in sides]
-                fix = lambda new, old: jnp.concatenate([jnp.where(top, new, old[0])[None], old[1:]], axis=0)
-                dcc = fix(2.0 * (ac * bc + asn * bsn), dcc)
-                dcs = fix(2.0 * (ac * bsn - asn * bc), dcs)
-                dsc = fix(2.0 * (ae * be + aes * bes), dsc)
-                dss = fix(2.0 * (ae * bes - aes * be), dss)
-            rows = slice(40 * half, 40 * half + 40)
-            cos_rows = slice(HALF + 40 * half, HALF + 40 * half + 40)
-            cross[parity, rows, 0:256] = dsc.reshape(40, 256).astype(jnp.bfloat16)
-            cross[parity, rows, 256:512] = dss.reshape(40, 256).astype(jnp.bfloat16)
-            cross[parity, cos_rows, 0:256] = dcc.reshape(40, 256).astype(jnp.bfloat16)
-            cross[parity, cos_rows, 256:512] = dcs.reshape(40, 256).astype(jnp.bfloat16)
-            low = dcc * dcc + dsc * dsc
-            high = dcs * dcs + dss * dss
-            if half == 0:
-                total = [low[0] * top_half + low[1:].sum(axis=0), high[0] * top_half + high[1:].sum(axis=0)]
-            else:
-                total = [total[0] + low.sum(axis=0), total[1] + high.sum(axis=0)]
-        total = jnp.concatenate(total, axis=1)
-        raw[g, pl.ds(i, 1), 768:1280] = jnp.sum(total, axis=0, keepdims=True)
-
-    def flows(m, parity):
-        g, i, _ = row_of(m)
-        flow_rows[parity] = dot(mix_rows[...], cross[parity])
-        flow_cols[parity] = dot(cross[parity, :, 256:512], mix_cols[...])
-        end = lax.dot_general(
-            sign_cols[...], cross[parity, :, 0:256], (((1,), (1,)), ((), ())), preferred_element_type=jnp.float32
-        )[:8]
-        end = jnp.sum(end * end * end_weight, axis=1, keepdims=True)
-        raw_end[g] = jnp.where(lane128 == i, end, raw_end[g])
-
-    def flow_sums(m, parity):
-        g, i, _ = row_of(m)
-        cosines = cross[parity, HALF:, :].astype(jnp.float32).reshape(10, 8, 512)
-        mixed = flow_rows[parity].reshape(11, 8, 512)
+    def spectra(pair, buf):
+        n, q = step_of(pair)
+        start = 80 * q - base
+        if not isinstance(start, int):
+            start = pl.multiple_of(start, 16)
+        for sec, src in ((0, fa), (1, fb)):
+            spec[buf, sec] = dot(second[...], src[n, pl.ds(start, PAIR_H), :])
+
+    def products(pair, buf, parity):
+        n, q = step_of(pair)
+        shift = ROWS * parity
+        totals = []
+        top16 = lax.broadcasted_iota(jnp.int32, (16, 128), 0) == 0
+        for lane in (0, 128):
+            low = high = None
+            for r in range(0, HALF, 16):
+                sides = [
+                    [
+                        spec[buf, sec, shift + at + r : shift + at + r + 16, lo + lane : lo + lane + 128]
+                        for at in (HALF, 0)
+                        for lo in (0, 256)
+                    ]
+                    for sec in range(2)
+                ]
+                (a1, a2, a3, a4), (b1, b2, b3, b4) = [
+                    (cc - ss, sc + cs, cc + ss, sc - cs) for cc, cs, sc, ss in sides
+                ]
+                plus_r = a1 * b1 + a2 * b2
+                plus_i = a1 * b2 - a2 * b1
+                minus_r = a3 * b3 + a4 * b4
+                minus_i = a3 * b4 - a4 * b3
+                dcc = plus_r + minus_r
+                dss = minus_r - plus_r
+                dsc = plus_i + minus_i
+                dcs = plus_i - minus_i
+                if r == 0:
+                    (ac, asn, ae, aes), (bc, bsn, be, bes) = sides
+                    dcc = jnp.where(top16, 2.0 * (ac * bc + asn * bsn), dcc)
+                    dcs = jnp.where(top16, 2.0 * (ac * bsn - asn * bc), dcs)
+                    dsc = jnp.where(top16, 2.0 * (ae * be + aes * bes), dsc)
+                    dss = jnp.where(top16, 2.0 * (ae * bes - aes * be), dss)
+                cross[buf, shift + r : shift + r + 16, lane : lane + 128] = dsc.astype(jnp.bfloat16)
+                cross[buf, shift + r : shift + r + 16, 256 + lane : 384 + lane] = dss.astype(jnp.bfloat16)
+                cross[buf, shift + HALF + r : shift + HALF + r + 16, lane : lane + 128] = dcc.astype(jnp.bfloat16)
+                cross[buf, shift + HALF + r : shift + HALF + r + 16, 256 + lane : 384 + lane] = dcs.astype(jnp.bfloat16)
+                near = dcc * dcc + dsc * dsc
+                far = dcs * dcs + dss * dss
+                if r == 0:
+                    near = jnp.where(top16, 0.5 * near, near)
+                    far = jnp.where(top16, 0.5 * far, far)
+                low = near[:8] + near[8:] if low is None else low + (near[:8] + near[8:])
+                high = far[:8] + far[8:] if high is None else high + (far[:8] + far[8:])
+            totals.append((low, high))
+        total = jnp.concatenate([totals[0][0], totals[1][0], totals[0][1], totals[1][1]], axis=1)
+        raw[n, pl.ds(2 * q + parity, 1), 768:1280] = jnp.sum(total, axis=0, keepdims=True)
+
+    def flows(pair, buf):
+        n, q = step_of(pair)
+        flow_cols[buf] = dot(cross[buf, :, 256:512], mix_cols[...])
+        for parity in range(2):
+            rows = slice(ROWS * parity, ROWS * parity + ROWS)
+            flow_rows[buf, parity] = dot(mix_rows[...], cross[buf, rows, :])
+            end = lax.dot_general(
+                sign_cols[...], cross[buf, rows, 0:256], (((1,), (1,)), ((), ())), preferred_element_type=jnp.float32
+            )[:8]
+            end = jnp.sum(end * end * end_weight, axis=1, keepdims=True)
+            raw_end[n] = jnp.where(lane128 == 2 * q + parity, end, raw_end[n])
+
+    def flow_sums(pair, buf, parity):
+        n, q = step_of(pair)
+        shift = ROWS * parity
+        where = pl.ds(2 * q + parity, 1)
+        cosines = cross[buf, shift + HALF : shift + ROWS, :].astype(jnp.float32).reshape(10, 8, 512)
+        mixed = flow_rows[buf, parity].reshape(11, 8, 512)
         flow_y = cosines[0] * mixed[0]
         for t in range(1, 10):
             flow_y = flow_y + cosines[t] * mixed[t]
-        end = cross[parity, 0:16, :].astype(jnp.float32)[:1] * mixed[10, 0:1] - 8.0 * mixed[10, 1:2] * mixed[10, 1:2]
-        raw[g, pl.ds(i, 1), 0:512] = jnp.sum(flow_y, axis=0, keepdims=True) + end
-        cosines = cross[parity, :, 0:256].astype(jnp.float32).reshape(20, 8, 256)
-        mixed = flow_cols[parity].reshape(20, 8, 256)
+        last = cross[buf, shift : shift + 16, :].astype(jnp.float32)[:1]
+        end = last * mixed[10, 0:1] - 8.0 * mixed[10, 1:2] * mixed[10, 1:2]
+        raw[n, where, 0:512] = jnp.sum(flow_y, axis=0, keepdims=True) + end
+        cosines = cross[buf, shift : shift + ROWS, 0:256].astype(jnp.float32).reshape(20, 8, 256)
+        mixed = flow_cols[buf, shift : shift + ROWS].reshape(20, 8, 256)
         flow_x = (cosines[0] * mixed[0] + cosines[10] * mixed[10]) * top_half
         for t in range(1, 20):
             if t != 10:
                 flow_x = flow_x + cosines[t] * mixed[t]
-        raw[g, pl.ds(i, 1), 512:768] = jnp.sum(flow_x, axis=0, keepdims=True)
-
-    def step(n, carry):
-        for parity in range(2):
-            m = 2 * n + parity
-            flow_sums(m - 3, 1 - parity)
-            flows(m - 2, parity)
-            products(m - 1, 1 - parity)
-            spectra(m, parity)
+        raw[n, where, 512:768] = jnp.sum(flow_x, axis=0, keepdims=True)
+
+    def body(t, buf, stages):
+        if 3 in stages:
+            for parity in range(2):
+                flow_sums(t - 3, 1 - buf, parity)
+        if 2 in stages:
+            flows(t - 2, buf)
+        if 1 in stages:
+            for parity in range(2):
+                products(t - 1, 1 - buf, parity)
+        if 0 in stages:
+            spectra(t, buf)
+
+    def some(t):
+        body(t, t % 2, [k for k in range(4) if 0 <= t - k < pairs])
+
+    begin = 3 + (pairs - 3) % 2
+    for t in range(begin):
+        some(t)
+
+    def step(k, carry):
+        body(begin + 2 * k, begin % 2, range(4))
+        body(begin + 2 * k + 1, 1 - begin % 2, range(4))
         return carry
 
-    lax.fori_loop(0, count // 2 + 2, step, 0)
+    lax.fori_loop(0, (pairs - begin) // 2, step, 0)
+    for t in range(pairs, pairs + 3):
+        some(t)
 
 
 def finish(raw, raw_end, cells, select, window, groups):
@@ -300,16 +325,16 @@
     raw_end[...] = jnp.zeros((WIN, 8, 128), jnp.float32)
 
 
-def early_step(m):
-    return m // 8, 2 + m % 8
-
-
-def edge_step(m):
-    return m // 12, m % 12
-
-
-def late_step(m):
-    return m // 4, m % 4 + jnp.where(m % 4 >= 2, 8, 0)
+def early_step(pair):
+    return pair // 4, 1 + pair % 4
+
+
+def edge_step(pair):
+    return pair // 6, pair % 6
+
+
+def late_step(pair):
+    return pair // 2, 5 * (pair % 2)
 
 
 def early_kernel(
@@ -327,7 +352,7 @@
             dst[n] = dot(pixels, first[...]).astype(jnp.bfloat16)
             cell_squares(grp, sec, n, cells, 2, 13, INNER_LO)
     run_steps(
-        early_step, 24, INNER_LO, fa, fb, second, mix_rows, mix_cols, sign_cols, raw, raw_end, work
+        early_step, 12, INNER_LO, fa, fb, second, mix_rows, mix_cols, sign_cols, raw, raw_end, work
     )
     out[...] = finish(raw, raw_end, cells, select, window, INNER_GROUPS)
 
@@ -361,7 +386,7 @@
             dst[n] = dot(pixels, first[...]).astype(jnp.bfloat16)
             cell_squares(grp, sec, n, cells, 0, 15, 0)
         cells[sec, 15:24, :] = jnp.zeros((9, 256 * WIN), jnp.float32)
-    run_steps(edge_step, 36, 0, fa, fb, second, mix_rows, mix_cols, sign_cols, raw, raw_end, work)
+    run_steps(edge_step, 18, 0, fa, fb, second, mix_rows, mix_cols, sign_cols, raw, raw_end, work)
     result = finish(raw, raw_end, cells, select, window, EDGE_GROUPS)
     out[...] = result
     fields, column = mesh_fields(result, valid)
@@ -389,7 +414,7 @@
                 dst[n, lo:hi, :] = dot(pixels, first[...]).astype(jnp.bfloat16)
             cell_squares(grp, sec, n, cells, 0, 5, 0)
             cell_squares(grp, sec, n, cells, 10, 15, 0)
-    run_steps(late_step, 12, 0, fa, fb, second, mix_rows, mix_cols, sign_cols, raw, raw_end, work)
+    run_steps(late_step, 6, 0, fa, fb, second, mix_rows, mix_cols, sign_cols, raw, raw_end, work)
     row = lax.broadcasted_iota(jnp.int32, (16, 128), 0)
     lane = lax.broadcasted_iota(jnp.int32, (16, 128), 1) % 32
     own = finish(raw, raw_end, cells, select, window, INNER_GROUPS)
@@ -425,10 +450,10 @@
 
 def work_shapes():
     return [
-        pltpu.VMEM((2, 2, ROWS, 512), jnp.float32),
-        pltpu.VMEM((2, ROWS, 512), jnp.bfloat16),
-        pltpu.VMEM((2, HALF + 8, 512), jnp.float32),
-        pltpu.VMEM((2, ROWS, 256), jnp.float32),
+        pltpu.VMEM((2, 2, 2 * ROWS, 512), jnp.float32),
+        pltpu.VMEM((2, 2 * ROWS, 512), jnp.bfloat16),
+        pltpu.VMEM((2, 2, HALF + 8, 512), jnp.float32),
+        pltpu.VMEM((2, 2 * ROWS, 256), jnp.float32),
     ]
 
 

time: 116 us -> 111 us (0.957)
  Pallas kernels: 36.5 us -> 30.9 us
    pallas_call x1, Pallas kernels: 6.43 us -> 4.43 us  [correlate_late(): pl.pallas_call(late_kernel, out_shape=(SMALL,) * 2, in_specs=[VMEM_SPEC]...]
    pallas_call x1, Pallas kernels: 13.8 us -> 11.9 us  [correlate_edge(): pl.pallas_call(edge_kernel, out_shape=(SMALL,) * 3, in_specs=[VMEM_SPEC]...]
    pallas_call x1, Pallas kernels: 9.82 us -> 8.09 us  [correlate_early(): pl.pallas_call(early_kernel, out_shape=SMALL, in_specs=[VMEM_SPEC] * 8, o...]
  transfers between devices with their start and end apart: 8 -> 8, of which waited for: 5 -> 5; matrix products, arithmetic and copies ran while one was open for 0% -> 0% of each run, Pallas kernels for 14% -> 11%
where the time goes in v5:
time: 111 us; the launch traced here: 110 us
  blocking collectives  36.7 us (33%)
  Pallas kernels  30.9 us (28%)
  starting transfers between devices  23.9 us (22%)
  waiting for transfers between devices  16.6 us (15%)
  local copies, waits for them, and re-layouts  1.28 us (1%)
    all_to_all x1, blocking collectives, per_device(): lax.all_to_all(packed, ('row', 'col'), split_axis=0, concat_axis=0, tiled...  36.7 us
    ppermute x8, starting transfers between devices, shifted(): return lax.ppermute(block, axis, pairs)  23.9 us
    ppermute x8, waiting for transfers between devices, shifted(): return lax.ppermute(block, axis, pairs)  16.6 us
    pallas_call x1, Pallas kernels, correlate_edge(): pl.pallas_call(edge_kernel, out_shape=(SMALL,) * 3, in_specs=[VMEM_SPEC]...  11.9 us
    pallas_call x1, Pallas kernels, correlate_early(): pl.pallas_call(early_kernel, out_shape=SMALL, in_specs=[VMEM_SPEC] * 8, o...  8.09 us
    pallas_call x1, Pallas kernels, correlate_late(): pl.pallas_call(late_kernel, out_shape=(SMALL,) * 2, in_specs=[VMEM_SPEC]...  4.43 us
    pallas_call x1, Pallas kernels, pack(): pl.pallas_call(pack_kernel, out_shape=jax.ShapeDtypeStruct((128, SLOT_H,...  4.11 us
  transfers between devices with their start and end apart: 8, of which 5 were waited for; matrix products, arithmetic and copies ran while one was open for 0% of the time, Pallas kernels for 11%

profile of v5, /device:TPU:34, one launch (start us, length us, event | category | flops | bytes accessed | tf_op | source)
XLA Modules:
  0.0 110.2 jit_solution(12328270063968063030)
XLA Ops:
  0.6 4.1 %shard_map.149 = bf16[128,56,128]{2,1,0:T(8,128)(2,1)} custom-call(bf16[96,3200]{1,0:T(8,128)(2,1)} %refs_0_.1, bf16[96,3200]{1,0:T(8,128)(2,1)} %refs_1_.1, s32[1,96]{1,0:T(1,128)} %bitcast.14, s32[1,96]{1,0:T(1,128)} %bitcast.15, s32[2,96]{1,0:T(2,128)} %bitcast.12, s32[2,96]{1,0:T(2,128)} %bitcast.13), custom_call_target="tpu_custom_call" | custom-call | tf_op jit(solution)/shard_map/pallas_call | solution.py:660
  4.8 36.7 %all_to_all.5.got = bf16[128,56,128]{2,1,0:T(8,128)(2,1)S(1)} all-to-all(bf16[128,56,128]{2,1,0:T(8,128)(2,1)} %shard_map.149), channel_id=1, replica_groups=mesh['row'=4,'col'=32] {'row','col'}, dimensions={0} | all-to-all | bytes 3670016 | tf_op jit(solution)/shard_map/all_to_all | solution.py:704
  41.4 0.0 copy-start
  41.4 0.0 copy-start.1
  41.4 0.0 copy-start.2
  41.4 0.0 copy-start.3
  41.4 0.0 copy-start.4
  41.4 0.0 copy-start.5
  41.4 0.0 copy-start.6
  41.5 0.0 copy-start.7
  41.5 2.1 %shard_map.150 = (bf16[8,2,488,128]{3,2,1,0:T(8,128)(2,1)S(1)}, bf16[8,2,64,128]{3,2,1,0:T(8,128)(2,1)S(1)}, bf16[8,2,64,128]{3,2,1,0:T(8,128)(2,1)S(1)}, bf16[2...) custom-call(bf16[128,56,128]{2,1,0:T(8,128)(2,1)S(1)} %all_to_all.5.got), custom_call_target="tpu_custom_call" | custom-call | tf_op jit(solution)/shard_map/pallas_call | solution.py:677
  43.5 1.9 %collective-permute-start = (bf16[8,2,64,128]{3,2,1,0:T(8,128)(2,1)S(1)}, bf16[8,2,64,128]{3,2,1,0:T(8,128)(2,1)S(1)}, u32[]{:S(2)}, u32[]{:S(2)}) collective-permute-start(bf16[8,2,64,128]{3,2,1,0:T(8,128)(2,1)S(1)} %get-tuple-element.13), channel_id=1, source_target_pairs={{0,32},{32,64},{64,96},{1,33},{33,65},{65,97},{2,34},{34,66},{66,9... | collective-permute-start | bytes 786440 | tf_op jit(solution)/shard_map/ppermute | solution.py:694
  45.5 3.9 %collective-permute-start.1 = (bf16[8,2,64,128]{3,2,1,0:T(8,128)(2,1)S(1)}, bf16[8,2,64,128]{3,2,1,0:T(8,128)(2,1)S(1)}, u32[]{:S(2)}, u32[]{:S(2)}) collective-permute-start(bf16[8,2,64,128]{3,2,1,0:T(8,128)(2,1)S(1)} %get-tuple-element.14), channel_id=1, source_target_pairs={{32,0},{64,32},{96,64},{33,1},{65,33},{97,65},{34,2},{66,34},{98,6... | collective-permute-start | bytes 786440 | tf_op jit(solution)/shard_map/ppermute | solution.py:694
  49.4 3.5 %collective-permute-done.top = bf16[8,2,64,128]{3,2,1,0:T(8,128)(2,1)S(1)} collective-permute-done((bf16[8,2,64,128]{3,2,1,0:T(8,128)(2,1)S(1)}, bf16[8,2,64,128]{3,2,1,0:T(8,128)(2,1)S(1)}, u32[]{:S(2)}, u32[]{:S(2)}) %collective-permute-start) | collective-permute-done | bytes 262176 | tf_op jit(solution)/shard_map/ppermute | solution.py:694
  52.9 1.9 %collective-permute-done.1.bottom = bf16[8,2,64,128]{3,2,1,0:T(8,128)(2,1)S(1)} collective-permute-done((bf16[8,2,64,128]{3,2,1,0:T(8,128)(2,1)S(1)}, bf16[8,2,64,128]{3,2,1,0:T(8,128)(2,1)S(1)}, u32[]{:S(2)}, u32[]{:S(2)}) %collective-permute-start.1) | collective-permute-done | bytes 262176 | tf_op jit(solution)/shard_map/ppermute | solution.py:694
  54.9 1.9 %collective-permute-start.3 = (bf16[2,608,128]{2,1,0:T(8,128)(2,1)S(1)}, bf16[2,608,128]{2,1,0:T(8,128)(2,1)S(1)}, u32[]{:S(2)}, u32[]{:S(2)}) collective-permute-start(bf16[2,608,128]{2,1,0:T(8,128)(2,1)S(1)} %pad_add_fusion), channel_id=1, source_target_pairs={{1,0},{2,1},{3,2},{4,3},{5,4},{6,5},{7,6},{8,7},{9,8},{10,9},{11,1... | collective-permute-start | bytes 933896 | tf_op jit(solution)/shard_map/ppermute | solution.py:694
  56.8 2.4 %collective-permute-start.2 = (bf16[2,608,128]{2,1,0:T(8,128)(2,1)S(1)}, bf16[2,608,128]{2,1,0:T(8,128)(2,1)S(1)}, u32[]{:S(2)}, u32[]{:S(2)}) collective-permute-start(bf16[2,608,128]{2,1,0:T(8,128)(2,1)S(1)} %pad_add_fusion.1), channel_id=1, source_target_pairs={{0,1},{1,2},{2,3},{3,4},{4,5},{5,6},{6,7},{7,8},{8,9},{9,10},{10,1... | collective-permute-start | bytes 933896 | tf_op jit(solution)/shard_map/ppermute | solution.py:694
  59.2 1.9 %collective-permute-done.3.right = bf16[2,608,128]{2,1,0:T(8,128)(2,1)S(1)} collective-permute-done((bf16[2,608,128]{2,1,0:T(8,128)(2,1)S(1)}, bf16[2,608,128]{2,1,0:T(8,128)(2,1)S(1)}, u32[]{:S(2)}, u32[]{:S(2)}) %collective-permute-start.3) | collective-permute-done | bytes 311328 | tf_op jit(solution)/shard_map/ppermute | solution.py:694
  61.2 6.0 %collective-permute-done.2.left = bf16[2,608,128]{2,1,0:T(8,128)(2,1)S(1)} collective-permute-done((bf16[2,608,128]{2,1,0:T(8,128)(2,1)S(1)}, bf16[2,608,128]{2,1,0:T(8,128)(2,1)S(1)}, u32[]{:S(2)}, u32[]{:S(2)}) %collective-permute-start.2) | collective-permute-done | bytes 311328 | tf_op jit(solution)/shard_map/ppermute | solution.py:694
  67.2 0.0 copy-done
  67.2 0.0 copy-done.1
  67.2 0.0 copy-done.2
  67.2 0.0 copy-done.3
  67.2 0.0 copy-done.4
  67.2 0.0 copy-done.5
  67.2 0.0 copy-done.6
  67.2 0.0 copy-done.7
  67.2 11.9 %shard_map.152 = (f32[16,128]{1,0:T(8,128)S(1)}, f32[16,128]{1,0:T(8,128)S(1)}, f32[16,128]{1,0:T(8,128)S(1)}) custom-call(bf16[8,2,488,128]{3,2,1,0:T(8,128)(2,1)S(1)} %get-tuple-element.12.form, bf16[8,2,64,128]{3,2,1,0:T(8,128)(2,1)S(1)} %collective-permute-done.top, bf16[8,2,64,128]{3,2,1,0:T(8,128)(2,1)S(1)} %collective-permute-done.1.bottom, ...), custom_call_target="tpu_custom_call" | custom-call | tf_op jit(solution)/shard_map/pallas_call | solution.py:508
  79.2 1.9 %collective-permute-start.4 = (f32[16,128]{1,0:T(8,128)S(1)}, f32[16,128]{1,0:T(8,128)S(1)}, u32[]{:S(2)}, u32[]{:S(2)}) collective-permute-start(f32[16,128]{1,0:T(8,128)S(1)} %get-tuple-element.20), channel_id=1, source_target_pairs={{0,1},{1,2},{2,3},{3,4},{4,5},{5,6},{6,7},{7,8},{8,9},{9,10},{10,1... | collective-permute-start | bytes 24584 | tf_op jit(solution)/shard_map/ppermute | solution.py:694
  81.1 5.9 %collective-permute-start.5 = (f32[16,128]{1,0:T(8,128)S(1)}, f32[16,128]{1,0:T(8,128)S(1)}, u32[]{:S(2)}, u32[]{:S(2)}) collective-permute-start(f32[16,128]{1,0:T(8,128)S(1)} %get-tuple-element.21), channel_id=1, source_target_pairs={{1,0},{2,1},{3,2},{4,3},{5,4},{6,5},{7,6},{8,7},{9,8},{10,9},{11,1... | collective-permute-start | bytes 24584 | tf_op jit(solution)/shard_map/ppermute | solution.py:694
  87.0 8.1 %shard_map.151.early = f32[16,128]{1,0:T(8,128)S(1)} custom-call(bf16[8,2,488,128]{3,2,1,0:T(8,128)(2,1)S(1)} %get-tuple-element.12.form, bf16[256,512]{1,0:T(8,128)(2,1)S(1)} %copy-done.1, bf16[320,208]{1,0:T(8,128)(2,1)S(1)} %copy-done.2, bf16[88,160]{1,0:T(8,128)(2,1)S(1)} %copy-done.5, bf16[256,256]{1,0:T(8,128)(2,1)S(1)} %copy-done.3, ...), custom_call_target="tpu_custom_call" | custom-call | tf_op jit(solution)/shard_map/pallas_call | solution.py:491
  95.1 4.4 %shard_map.153 = (f32[16,128]{1,0:T(8,128)S(1)}, f32[16,128]{1,0:T(8,128)S(1)}) custom-call(bf16[8,2,488,128]{3,2,1,0:T(8,128)(2,1)S(1)} %get-tuple-element.12.form, bf16[8,2,64,128]{3,2,1,0:T(8,128)(2,1)S(1)} %collective-permute-done.top, bf16[8,2,64,128]{3,2,1,0:T(8,128)(2,1)S(1)} %collective-permute-done.1.bottom, f32[16,128]{1,0:T(8,128)S(1)} %shard_map.151.early, ...), custom_call_target="tpu_custom_call" | custom-call | tf_op jit(solution)/shard_map/pallas_call | solution.py:519
  99.5 0.0 collective-permute-done.4
  99.5 0.0 collective-permute-done.5
  99.6 3.6 %collective-permute-start.7 = (f32[8,128]{1,0:T(8,128)S(1)}, f32[8,128]{1,0:T(8,128)S(1)}, u32[]{:S(2)}, u32[]{:S(2)}) collective-permute-start(f32[8,128]{1,0:T(8,128)S(1)} %get-tuple-element.28), channel_id=1, source_target_pairs={{32,0},{64,32},{96,64},{33,1},{65,33},{97,65},{34,2},{66,34},{98,6... | collective-permute-start | bytes 12296 | tf_op jit(solution)/shard_map/ppermute | solution.py:694
  103.2 2.2 %collective-permute-start.6 = (f32[8,128]{1,0:T(8,128)S(1)}, f32[8,128]{1,0:T(8,128)S(1)}, u32[]{:S(2)}, u32[]{:S(2)}) collective-permute-start(f32[8,128]{1,0:T(8,128)S(1)} %get-tuple-element.29), channel_id=1, source_target_pairs={{0,32},{32,64},{64,96},{1,33},{33,65},{65,97},{2,34},{34,66},{66,9... | collective-permute-start | bytes 12296 | tf_op jit(solution)/shard_map/ppermute | solution.py:694
  105.4 0.0 collective-permute-done.7.beneath
  105.4 3.3 %collective-permute-done.6.above = f32[8,128]{1,0:T(8,128)S(1)} collective-permute-done((f32[8,128]{1,0:T(8,128)S(1)}, f32[8,128]{1,0:T(8,128)S(1)}, u32[]{:S(2)}, u32[]{:S(2)}) %collective-permute-start.6) | collective-permute-done | bytes 4128 | tf_op jit(solution)/shard_map/ppermute | solution.py:694
  108.7 0.3 shard_map.154
  109.0 0.6 copy.16
  109.6 0.6 copy.17
  (6 shorter events, 0.1 us)
Async XLA Ops:
  41.4 25.8 %copy-start = (bf16[1280,128]{1,0:T(8,128)(2,1)S(1)}, bf16[1280,128]{1,0:T(8,128)(2,1)}, u32[]{:S(2)}) copy-start(bf16[1280,128]{1,0:T(8,128)(2,1)} %constant.22.clone.select) | copy-start | bytes 983044
  41.4 25.8 %copy-start.1 = (bf16[256,512]{1,0:T(8,128)(2,1)S(1)}, bf16[256,512]{1,0:T(8,128)(2,1)}, u32[]{:S(2)}) copy-start(bf16[256,512]{1,0:T(8,128)(2,1)} %constant.17.clone.first) | copy-start | bytes 786436
  41.4 25.8 %copy-start.2 = (bf16[320,208]{1,0:T(8,128)(2,1)S(1)}, bf16[320,208]{1,0:T(8,128)(2,1)}, u32[]{:S(2)}) copy-start(bf16[320,208]{1,0:T(8,128)(2,1)} %constant.18.clone.second) | copy-start | bytes 399364
  41.4 25.8 %copy-start.3 = (bf16[256,256]{1,0:T(8,128)(2,1)S(1)}, bf16[256,256]{1,0:T(8,128)(2,1)}, u32[]{:S(2)}) copy-start(bf16[256,256]{1,0:T(8,128)(2,1)} %constant.20.clone.mix_cols) | copy-start | bytes 393220
  41.4 25.8 %copy-start.4 = (bf16[256,128]{1,0:T(8,128)(2,1)S(1)}, bf16[256,128]{1,0:T(8,128)(2,1)}, u32[]{:S(2)}) copy-start(bf16[256,128]{1,0:T(8,128)(2,1)} %constant.23.clone.window) | copy-start | bytes 196612
  41.4 25.8 %copy-start.5 = (bf16[88,160]{1,0:T(8,128)(2,1)S(1)}, bf16[88,160]{1,0:T(8,128)(2,1)}, u32[]{:S(2)}) copy-start(bf16[88,160]{1,0:T(8,128)(2,1)} %constant.19.clone.mix_rows) | copy-start | bytes 84484
  41.4 25.8 %copy-start.6 = (bf16[16,256]{1,0:T(8,128)(2,1)S(1)}, bf16[16,256]{1,0:T(8,128)(2,1)}, u32[]{:S(2)}) copy-start(bf16[16,256]{1,0:T(8,128)(2,1)} %constant.21.clone.sign_cols) | copy-start | bytes 24580
  41.5 25.8 %copy-start.7 = (s32[12,16]{1,0:T(8,128)S(1)}, s32[12,16]{1,0:T(8,128)}, u32[]{:S(2)}) copy-start(s32[12,16]{1,0:T(8,128)} %valid.3) | copy-start | bytes 2308
  43.5 9.4 %collective-permute-start = (bf16[8,2,64,128]{3,2,1,0:T(8,128)(2,1)S(1)}, bf16[8,2,64,128]{3,2,1,0:T(8,128)(2,1)S(1)}, u32[]{:S(2)}, u32[]{:S(2)}) collective-permute-start(bf16[8,2,64,128]{3,2,1,0:T(8,128)(2,1)S(1)} %get-tuple-element.13), channel_id=1, source_target_pairs={{0,32},{32,64},{64,96},{1,33},{33,65},{65,97},{2,34},{34,66},{66,9... | collective-permute-start | bytes 786440 | tf_op jit(solution)/shard_map/ppermute | solution.py:694
  45.5 9.4 %collective-permute-start.1 = (bf16[8,2,64,128]{3,2,1,0:T(8,128)(2,1)S(1)}, bf16[8,2,64,128]{3,2,1,0:T(8,128)(2,1)S(1)}, u32[]{:S(2)}, u32[]{:S(2)}) collective-permute-start(bf16[8,2,64,128]{3,2,1,0:T(8,128)(2,1)S(1)} %get-tuple-element.14), channel_id=1, source_target_pairs={{32,0},{64,32},{96,64},{33,1},{65,33},{97,65},{34,2},{66,34},{98,6... | collective-permute-start | bytes 786440 | tf_op jit(solution)/shard_map/ppermute | solution.py:694
  54.9 6.3 %collective-permute-start.3 = (bf16[2,608,128]{2,1,0:T(8,128)(2,1)S(1)}, bf16[2,608,128]{2,1,0:T(8,128)(2,1)S(1)}, u32[]{:S(2)}, u32[]{:S(2)}) collective-permute-start(bf16[2,608,128]{2,1,0:T(8,128)(2,1)S(1)} %pad_add_fusion), channel_id=1, source_target_pairs={{1,0},{2,1},{3,2},{4,3},{5,4},{6,5},{7,6},{8,7},{9,8},{10,9},{11,1... | collective-permute-start | bytes 933896 | tf_op jit(solution)/shard_map/ppermute | solution.py:694
  56.8 10.3 %collective-permute-start.2 = (bf16[2,608,128]{2,1,0:T(8,128)(2,1)S(1)}, bf16[2,608,128]{2,1,0:T(8,128)(2,1)S(1)}, u32[]{:S(2)}, u32[]{:S(2)}) collective-permute-start(bf16[2,608,128]{2,1,0:T(8,128)(2,1)S(1)} %pad_add_fusion.1), channel_id=1, source_target_pairs={{0,1},{1,2},{2,3},{3,4},{4,5},{5,6},{6,7},{7,8},{8,9},{9,10},{10,1... | collective-permute-start | bytes 933896 | tf_op jit(solution)/shard_map/ppermute | solution.py:694
  79.2 20.4 %collective-permute-start.4 = (f32[16,128]{1,0:T(8,128)S(1)}, f32[16,128]{1,0:T(8,128)S(1)}, u32[]{:S(2)}, u32[]{:S(2)}) collective-permute-start(f32[16,128]{1,0:T(8,128)S(1)} %get-tuple-element.20), channel_id=1, source_target_pairs={{0,1},{1,2},{2,3},{3,4},{4,5},{5,6},{6,7},{7,8},{8,9},{9,10},{10,1... | collective-permute-start | bytes 24584 | tf_op jit(solution)/shard_map/ppermute | solution.py:694
  81.1 18.5 %collective-permute-start.5 = (f32[16,128]{1,0:T(8,128)S(1)}, f32[16,128]{1,0:T(8,128)S(1)}, u32[]{:S(2)}, u32[]{:S(2)}) collective-permute-start(f32[16,128]{1,0:T(8,128)S(1)} %get-tuple-element.21), channel_id=1, source_target_pairs={{1,0},{2,1},{3,2},{4,3},{5,4},{6,5},{7,6},{8,7},{9,8},{10,9},{11,1... | collective-permute-start | bytes 24584 | tf_op jit(solution)/shard_map/ppermute | solution.py:694
  99.6 5.9 %collective-permute-start.7 = (f32[8,128]{1,0:T(8,128)S(1)}, f32[8,128]{1,0:T(8,128)S(1)}, u32[]{:S(2)}, u32[]{:S(2)}) collective-permute-start(f32[8,128]{1,0:T(8,128)S(1)} %get-tuple-element.28), channel_id=1, source_target_pairs={{32,0},{64,32},{96,64},{33,1},{65,33},{97,65},{34,2},{66,34},{98,6... | collective-permute-start | bytes 12296 | tf_op jit(solution)/shard_map/ppermute | solution.py:694
  103.2 5.5 %collective-permute-start.6 = (f32[8,128]{1,0:T(8,128)S(1)}, f32[8,128]{1,0:T(8,128)S(1)}, u32[]{:S(2)}, u32[]{:S(2)}) collective-permute-start(f32[8,128]{1,0:T(8,128)S(1)} %get-tuple-element.29), channel_id=1, source_target_pairs={{0,32},{32,64},{64,96},{1,33},{33,65},{65,97},{2,34},{34,66},{66,9... | collective-permute-start | bytes 12296 | tf_op jit(solution)/shard_map/ppermute | solution.py:694

commit v6 on v5

--- a/solution.py
+++ b/solution.py
@@ -329,6 +329,10 @@
     return pair // 4, 1 + pair % 4
 
 
+def tail_step(pair):
+    return 2, 1 + pair
+
+
 def edge_step(pair):
     return pair // 6, pair % 6
 
@@ -337,24 +341,39 @@
     return pair // 2, 5 * (pair % 2)
 
 
-def early_kernel(
-    form, first, second, mix_rows, mix_cols, sign_cols, select, window, out, grp, fa, fb, cells, raw, raw_end, *work
+def inner_rows(
+    members, step_of, pairs, form, first, second, mix_rows, mix_cols, sign_cols, select, window,
+    grp, fa, fb, cells, raw, raw_end, *work,
 ):
     lo, hi = INNER_LO - TOP, INNER_HI - TOP
-    clear_sums(raw, raw_end)
-    raw[:, 0:2, :] = jnp.zeros((WIN, 2, 1280), jnp.float32)
-    raw[:, 10:12, :] = jnp.zeros((WIN, 2, 1280), jnp.float32)
+    raw[...] = jnp.zeros((WIN, 16, 1280), jnp.float32)
+    raw_end[...] = jnp.zeros((WIN, 8, 128), jnp.float32)
     for sec, dst in ((0, fa), (1, fb)):
         cells[sec] = jnp.zeros((24, 256 * WIN), jnp.float32)
-        for n, g in enumerate(INNER_GROUPS):
-            pixels = group_pixels(lambda c: form[c - 1, sec, lo:hi, :], sec, g)
+        for n in members:
+            pixels = group_pixels(lambda c: form[c - 1, sec, lo:hi, :], sec, INNER_GROUPS[n])
             grp[sec, n] = pixels
             dst[n] = dot(pixels, first[...]).astype(jnp.bfloat16)
             cell_squares(grp, sec, n, cells, 2, 13, INNER_LO)
-    run_steps(
-        early_step, 12, INNER_LO, fa, fb, second, mix_rows, mix_cols, sign_cols, raw, raw_end, work
-    )
-    out[...] = finish(raw, raw_end, cells, select, window, INNER_GROUPS)
+    run_steps(step_of, pairs, INNER_LO, fa, fb, second, mix_rows, mix_cols, sign_cols, raw, raw_end, work)
+    return finish(raw, raw_end, cells, select, window, INNER_GROUPS)
+
+
+def early_kernel(*refs):
+    out = refs[8]
+    out[...] = inner_rows((0, 1), early_step, 8, *refs[:8], *refs[9:])
+
+
+def tail_kernel(early, late, edge, valid, *refs):
+    out, fields = refs[8:10]
+    row = lax.broadcasted_iota(jnp.int32, (16, 128), 0)
+    lane = lax.broadcasted_iota(jnp.int32, (16, 128), 1) % 32
+    own = inner_rows((2,), tail_step, 4, *refs[:8], *refs[10:])
+    own = jnp.where(lane < 9, early[...], own)
+    own = jnp.where((row >= 2) & (row < 10), own, late[...])
+    result = jnp.where((lane >= 3) & (lane < 12), own, edge[...])
+    out[...] = result
+    fields[...] = mesh_fields(result, valid)[0]
 
 
 def mesh_fields(result, valid):
@@ -397,8 +416,8 @@
 
 
 def late_kernel(
-    form, top, bottom, early, edge, valid, first, second, mix_rows, mix_cols, sign_cols, select, window,
-    out, fields, frame, grp, fa, fb, cells, raw, raw_end, *work,
+    form, top, bottom, first, second, mix_rows, mix_cols, sign_cols, select, window,
+    out, frame, grp, fa, fb, cells, raw, raw_end, *work,
 ):
     upper, lower = 208, 400
     clear_sums(raw, raw_end)
@@ -415,13 +434,7 @@
             cell_squares(grp, sec, n, cells, 0, 5, 0)
             cell_squares(grp, sec, n, cells, 10, 15, 0)
     run_steps(late_step, 6, 0, fa, fb, second, mix_rows, mix_cols, sign_cols, raw, raw_end, work)
-    row = lax.broadcasted_iota(jnp.int32, (16, 128), 0)
-    lane = lax.broadcasted_iota(jnp.int32, (16, 128), 1) % 32
-    own = finish(raw, raw_end, cells, select, window, INNER_GROUPS)
-    own = jnp.where((row >= 2) & (row < 10), early[...], own)
-    result = jnp.where((lane >= 3) & (lane < 12), own, edge[...])
-    out[...] = result
-    fields[...] = mesh_fields(result, valid)[0]
+    out[...] = finish(raw, raw_end, cells, select, window, INNER_GROUPS)
 
 
 def relax_kernel(result, fields, above, beneath, flow, mesh_out):
@@ -444,8 +457,8 @@
         )
         mesh = (pull + stiffness * around) * rest
     for kind in range(2):
-        flow[kind] = result[0:12, 32 * kind : 32 * kind + 16]
-        mesh_out[kind] = mesh[SWEEPS : SWEEPS + 12, 32 * kind + SWEEPS : 32 * kind + SWEEPS + 16]
+        flow[:, kind, :] = result[0:12, 32 * kind : 32 * kind + 16]
+        mesh_out[:, kind, :] = mesh[SWEEPS : SWEEPS + 12, 32 * kind + SWEEPS : 32 * kind + SWEEPS + 16]
 
 
 def work_shapes():
@@ -486,22 +499,37 @@
 SMALL = jax.ShapeDtypeStruct((16, 128), jnp.float32)
 
 
+def inner_shapes():
+    height = INNER_HI - INNER_LO
+    return [
+        pltpu.VMEM((2, WIN, height, 256), jnp.bfloat16),
+        pltpu.VMEM((WIN, height, 512), jnp.bfloat16),
+        pltpu.VMEM((WIN, height, 512), jnp.bfloat16),
+        *sum_shapes(pltpu.VMEM),
+        *work_shapes(),
+    ]
+
+
 def correlate_early(form, consts):
-    height = INNER_HI - INNER_LO
     return pl.pallas_call(
         early_kernel,
         out_shape=SMALL,
         in_specs=[VMEM_SPEC] * 8,
         out_specs=VMEM_SPEC,
-        scratch_shapes=[
-            pltpu.VMEM((2, WIN, height, 256), jnp.bfloat16),
-            pltpu.VMEM((WIN, height, 512), jnp.bfloat16),
-            pltpu.VMEM((WIN, height, 512), jnp.bfloat16),
-            *sum_shapes(pltpu.VMEM),
-            *work_shapes(),
-        ],
+        scratch_shapes=inner_shapes(),
         compiler_params=grow_params(20),
     )(form, *consts)
+
+
+def correlate_tail(early, late, edge, valid, form, consts):
+    return pl.pallas_call(
+        tail_kernel,
+        out_shape=(SMALL,) * 2,
+        in_specs=[VMEM_SPEC] * 12,
+        out_specs=(VMEM_SPEC,) * 2,
+        scratch_shapes=inner_shapes(),
+        compiler_params=grow_params(20),
+    )(early, late, edge, valid, form, *consts)
 
 
 def correlate_edge(form, top, bottom, left, right, valid, consts):
@@ -515,32 +543,41 @@
     )(form, top, bottom, left, right, valid, *consts)
 
 
-def correlate_late(form, top, bottom, early, edge, valid, consts):
+def correlate_late(form, top, bottom, consts):
     return pl.pallas_call(
         late_kernel,
-        out_shape=(SMALL,) * 2,
-        in_specs=[VMEM_SPEC] * 13,
-        out_specs=(VMEM_SPEC,) * 2,
+        out_shape=SMALL,
+        in_specs=[VMEM_SPEC] * 10,
+        out_specs=VMEM_SPEC,
         scratch_shapes=frame_shapes(),
         compiler_params=grow_params(24),
-    )(form, top, bottom, early, edge, valid, *consts)
+    )(form, top, bottom, *consts)
 
 
 def relax(result, fields, above, beneath):
-    field = jax.ShapeDtypeStruct((2, 12, 16), jnp.float32)
-    return pl.pallas_call(
+    field = jax.ShapeDtypeStruct((12, 2, 16), jnp.float32)
+    flow, mesh = pl.pallas_call(
         relax_kernel,
         out_shape=(field, field),
         in_specs=[VMEM_SPEC] * 4,
-        out_specs=(VMEM_SPEC,) * 2,
         compiler_params=grow_params(8),
     )(result, fields, above, beneath)
+    return flow.transpose(1, 0, 2), mesh.transpose(1, 0, 2)
 
 
 def pack_kernel(*refs):
     sources, out, rows, held, arrived = refs[:6], refs[6], refs[7], refs[8:14], refs[14]
-    copies = [pltpu.make_async_copy(src, dst, arrived.at[n]) for n, (src, dst) in enumerate(zip(sources, held))]
-    for copy in copies:
+    copies = [pltpu.make_async_copy(sources[n], held[n], arrived.at[n]) for n in range(2, 6)]
+    pieces = []
+    for k in range(5):
+        lanes = pl.ds(8 * TILE_W * k, 8 * TILE_W)
+        pieces.append(
+            [
+                pltpu.make_async_copy(sources[n].at[:, lanes], held[n].at[:, lanes], arrived.at[6 + 2 * k + n])
+                for n in range(2)
+            ]
+        )
+    for copy in copies + sum(pieces, []):
         copy.start()
     for copy in copies:
         copy.wait()
@@ -585,6 +622,9 @@
         return jnp.concatenate([a_part, b_part], axis=0)
 
     for y in range(0, SLOT_H, 2):
+        if y % 8 == 0 and y < TILE_H:
+            for copy in pieces[y // 8]:
+                copy.wait()
         both = jnp.concatenate([send_row(y), send_row(y + 1)], axis=1)
         sent = dot(select, both)
         rows[pl.ds(y, 128, stride=SLOT_H), :] = sent[:, :128]
@@ -665,7 +705,7 @@
         scratch_shapes=[
             pltpu.VMEM((128 * SLOT_H, 128), jnp.float32),
             *[pltpu.VMEM(x.shape, x.dtype) for x in arrays],
-            pltpu.SemaphoreType.DMA((6,)),
+            pltpu.SemaphoreType.DMA((16,)),
         ],
         compiler_params=pltpu.CompilerParams(vmem_limit_bytes=60 << 20),
     )(*arrays)
@@ -709,10 +749,11 @@
     early = correlate_early(form, consts)
     left = shifted(column(high, top, bottom, TX - 1), "col", 1)
     right = shifted(column(low, top, bottom, 0), "col", -1)
+    late = correlate_late(form, top, bottom, consts)
     edge, to_right, to_left = correlate_edge(form, top, bottom, left, right, patch_valid, consts)
     from_left = shifted(to_right, "col", 1)
     from_right = shifted(to_left, "col", -1)
-    result, fields = correlate_late(form, top, bottom, early, edge, patch_valid, consts)
+    result, fields = correlate_tail(early, late, edge, patch_valid, form, consts)
     fields = fields + from_left + from_right
     above = shifted(fields[8:16], "row", 1)
     beneath = shifted(fields[0:8], "row", -1)

time: 111 us -> 111 us (level)
  Pallas kernels: 30.9 us -> 32.5 us
  local copies, waits for them, and re-layouts: 1.28 us -> 0.06 us
    pallas_call x1 -> x2, Pallas kernels: 4.43 us -> 7.39 us  [the longest x1 4.45 us: correlate_late(): pl.pallas_call(late_kernel, out_shape=SMALL, in_specs=[VMEM_SPEC] * 10, o...]
    pallas_call x1, Pallas kernels: 8.09 us -> 5.5 us  [correlate_early(): pl.pallas_call(early_kernel, out_shape=SMALL, in_specs=[VMEM_SPEC] * 8, o...]
    pallas_call x2 -> x0, local copies, waits for them, and re-layouts: 1.22 us -> none  [relax(): pl.pallas_call(relax_kernel, out_shape=(field, field), in_specs=[VMEM_SPE...]
  transfers between devices with their start and end apart: 8 -> 8, of which waited for: 5 -> 5; matrix products, arithmetic and copies ran while one was open for 0% -> 0% of each run, Pallas kernels for 11% -> 12%
where the time goes in v6:
time: 111 us
  blocking collectives  36.7 us (33%)
  Pallas kernels  32.5 us (29%)
  starting transfers between devices  23.9 us (22%)
  waiting for transfers between devices  16.6 us (15%)
    all_to_all x1, blocking collectives, per_device(): lax.all_to_all(packed, ('row', 'col'), split_axis=0, concat_axis=0, tiled...  36.7 us
    ppermute x8, starting transfers between devices, shifted(): return lax.ppermute(block, axis, pairs)  23.9 us
    ppermute x8, waiting for transfers between devices, shifted(): return lax.ppermute(block, axis, pairs)  16.6 us
    pallas_call x1, Pallas kernels, correlate_edge(): pl.pallas_call(edge_kernel, out_shape=(SMALL,) * 3, in_specs=[VMEM_SPEC]...  11.6 us
    pallas_call x1, Pallas kernels, correlate_early(): pl.pallas_call(early_kernel, out_shape=SMALL, in_specs=[VMEM_SPEC] * 8, o...  5.5 us
    pallas_call x1, Pallas kernels, pack(): pl.pallas_call(pack_kernel, out_shape=jax.ShapeDtypeStruct((128, SLOT_H,...  4.97 us
    pallas_call x1, Pallas kernels, correlate_late(): pl.pallas_call(late_kernel, out_shape=SMALL, in_specs=[VMEM_SPEC] * 10, o...  4.45 us
    pallas_call x1, Pallas kernels, correlate_tail(): pl.pallas_call(tail_kernel, out_shape=(SMALL,) * 2, in_specs=[VMEM_SPEC]...  2.94 us
  transfers between devices with their start and end apart: 8, of which 5 were waited for; matrix products, arithmetic and copies ran while one was open for 0% of the time, Pallas kernels for 12%

profile of v6, /device:TPU:34, one launch (start us, length us, event | category | flops | bytes accessed | tf_op | source)
XLA Modules:
  0.0 110.6 jit_solution(18275036898878813576)
XLA Ops:
  0.6 5.0 %shard_map.149 = bf16[128,56,128]{2,1,0:T(8,128)(2,1)} custom-call(bf16[96,3200]{1,0:T(8,128)(2,1)} %refs_0_.1, bf16[96,3200]{1,0:T(8,128)(2,1)} %refs_1_.3, s32[1,96]{1,0:T(1,128)} %bitcast.16, s32[1,96]{1,0:T(1,128)} %bitcast.17, s32[2,96]{1,0:T(2,128)} %bitcast.14, s32[2,96]{1,0:T(2,128)} %bitcast.15), custom_call_target="tpu_custom_call" | custom-call | tf_op jit(solution)/shard_map/pallas_call | solution.py:700
  5.6 36.7 %all_to_all.5.got = bf16[128,56,128]{2,1,0:T(8,128)(2,1)S(1)} all-to-all(bf16[128,56,128]{2,1,0:T(8,128)(2,1)} %shard_map.149), channel_id=1, replica_groups=mesh['row'=4,'col'=32] {'row','col'}, dimensions={0} | all-to-all | bytes 3670016 | tf_op jit(solution)/shard_map/all_to_all | solution.py:744
  42.3 0.0 copy-start
  42.3 0.0 copy-start.1
  42.3 0.0 copy-start.2
  42.3 0.0 copy-start.3
  42.3 0.0 copy-start.4
  42.3 0.0 copy-start.5
  42.3 0.0 copy-start.6
  42.3 0.0 copy-start.7
  42.3 2.1 %shard_map.150 = (bf16[8,2,488,128]{3,2,1,0:T(8,128)(2,1)S(1)}, bf16[8,2,64,128]{3,2,1,0:T(8,128)(2,1)S(1)}, bf16[8,2,64,128]{3,2,1,0:T(8,128)(2,1)S(1)}, bf16[2...) custom-call(bf16[128,56,128]{2,1,0:T(8,128)(2,1)S(1)} %all_to_all.5.got), custom_call_target="tpu_custom_call" | custom-call | tf_op jit(solution)/shard_map/pallas_call | solution.py:717
  44.4 1.9 %collective-permute-start = (bf16[8,2,64,128]{3,2,1,0:T(8,128)(2,1)S(1)}, bf16[8,2,64,128]{3,2,1,0:T(8,128)(2,1)S(1)}, u32[]{:S(2)}, u32[]{:S(2)}) collective-permute-start(bf16[8,2,64,128]{3,2,1,0:T(8,128)(2,1)S(1)} %get-tuple-element.15), channel_id=1, source_target_pairs={{0,32},{32,64},{64,96},{1,33},{33,65},{65,97},{2,34},{34,66},{66,9... | collective-permute-start | bytes 786440 | tf_op jit(solution)/shard_map/ppermute | solution.py:734
  46.3 3.9 %collective-permute-start.1 = (bf16[8,2,64,128]{3,2,1,0:T(8,128)(2,1)S(1)}, bf16[8,2,64,128]{3,2,1,0:T(8,128)(2,1)S(1)}, u32[]{:S(2)}, u32[]{:S(2)}) collective-permute-start(bf16[8,2,64,128]{3,2,1,0:T(8,128)(2,1)S(1)} %get-tuple-element.16), channel_id=1, source_target_pairs={{32,0},{64,32},{96,64},{33,1},{65,33},{97,65},{34,2},{66,34},{98,6... | collective-permute-start | bytes 786440 | tf_op jit(solution)/shard_map/ppermute | solution.py:734
  50.3 3.5 %collective-permute-done.top = bf16[8,2,64,128]{3,2,1,0:T(8,128)(2,1)S(1)} collective-permute-done((bf16[8,2,64,128]{3,2,1,0:T(8,128)(2,1)S(1)}, bf16[8,2,64,128]{3,2,1,0:T(8,128)(2,1)S(1)}, u32[]{:S(2)}, u32[]{:S(2)}) %collective-permute-start) | collective-permute-done | bytes 262176 | tf_op jit(solution)/shard_map/ppermute | solution.py:734
  53.7 1.9 %collective-permute-done.1.bottom = bf16[8,2,64,128]{3,2,1,0:T(8,128)(2,1)S(1)} collective-permute-done((bf16[8,2,64,128]{3,2,1,0:T(8,128)(2,1)S(1)}, bf16[8,2,64,128]{3,2,1,0:T(8,128)(2,1)S(1)}, u32[]{:S(2)}, u32[]{:S(2)}) %collective-permute-start.1) | collective-permute-done | bytes 262176 | tf_op jit(solution)/shard_map/ppermute | solution.py:734
  55.7 1.9 %collective-permute-start.3 = (bf16[2,608,128]{2,1,0:T(8,128)(2,1)S(1)}, bf16[2,608,128]{2,1,0:T(8,128)(2,1)S(1)}, u32[]{:S(2)}, u32[]{:S(2)}) collective-permute-start(bf16[2,608,128]{2,1,0:T(8,128)(2,1)S(1)} %pad_add_fusion), channel_id=1, source_target_pairs={{1,0},{2,1},{3,2},{4,3},{5,4},{6,5},{7,6},{8,7},{9,8},{10,9},{11,1... | collective-permute-start | bytes 933896 | tf_op jit(solution)/shard_map/ppermute | solution.py:734
  57.7 2.4 %collective-permute-start.2 = (bf16[2,608,128]{2,1,0:T(8,128)(2,1)S(1)}, bf16[2,608,128]{2,1,0:T(8,128)(2,1)S(1)}, u32[]{:S(2)}, u32[]{:S(2)}) collective-permute-start(bf16[2,608,128]{2,1,0:T(8,128)(2,1)S(1)} %pad_add_fusion.1), channel_id=1, source_target_pairs={{0,1},{1,2},{2,3},{3,4},{4,5},{5,6},{6,7},{7,8},{8,9},{9,10},{10,1... | collective-permute-start | bytes 933896 | tf_op jit(solution)/shard_map/ppermute | solution.py:734
  60.1 1.9 %collective-permute-done.3.right = bf16[2,608,128]{2,1,0:T(8,128)(2,1)S(1)} collective-permute-done((bf16[2,608,128]{2,1,0:T(8,128)(2,1)S(1)}, bf16[2,608,128]{2,1,0:T(8,128)(2,1)S(1)}, u32[]{:S(2)}, u32[]{:S(2)}) %collective-permute-start.3) | collective-permute-done | bytes 311328 | tf_op jit(solution)/shard_map/ppermute | solution.py:734
  62.0 6.0 %collective-permute-done.2.left = bf16[2,608,128]{2,1,0:T(8,128)(2,1)S(1)} collective-permute-done((bf16[2,608,128]{2,1,0:T(8,128)(2,1)S(1)}, bf16[2,608,128]{2,1,0:T(8,128)(2,1)S(1)}, u32[]{:S(2)}, u32[]{:S(2)}) %collective-permute-start.2) | collective-permute-done | bytes 311328 | tf_op jit(solution)/shard_map/ppermute | solution.py:734
  68.0 0.0 copy-done
  68.0 0.0 copy-done.1
  68.0 0.0 copy-done.2
  68.0 0.0 copy-done.3
  68.0 0.0 copy-done.4
  68.0 0.0 copy-done.5
  68.0 0.0 copy-done.6
  68.0 0.0 copy-done.7
  68.1 11.6 %shard_map.153 = (f32[16,128]{1,0:T(8,128)S(1)}, f32[16,128]{1,0:T(8,128)S(1)}, f32[16,128]{1,0:T(8,128)S(1)}) custom-call(bf16[8,2,488,128]{3,2,1,0:T(8,128)(2,1)S(1)} %get-tuple-element.14.refs_0_.form, bf16[8,2,64,128]{3,2,1,0:T(8,128)(2,1)S(1)} %collective-permute-done.top, bf16[8,2,64,128]{3,2,1,0:T(8,128)(2,1)S(1)} %collective-permute-done.1.bottom, ...), custom_call_target="tpu_custom_call" | custom-call | tf_op jit(solution)/shard_map/pallas_call | solution.py:536
  79.7 1.9 %collective-permute-start.4 = (f32[16,128]{1,0:T(8,128)S(1)}, f32[16,128]{1,0:T(8,128)S(1)}, u32[]{:S(2)}, u32[]{:S(2)}) collective-permute-start(f32[16,128]{1,0:T(8,128)S(1)} %get-tuple-element.22), channel_id=1, source_target_pairs={{0,1},{1,2},{2,3},{3,4},{4,5},{5,6},{6,7},{7,8},{8,9},{9,10},{10,1... | collective-permute-start | bytes 24584 | tf_op jit(solution)/shard_map/ppermute | solution.py:734
  81.6 5.9 %collective-permute-start.5 = (f32[16,128]{1,0:T(8,128)S(1)}, f32[16,128]{1,0:T(8,128)S(1)}, u32[]{:S(2)}, u32[]{:S(2)}) collective-permute-start(f32[16,128]{1,0:T(8,128)S(1)} %get-tuple-element.23), channel_id=1, source_target_pairs={{1,0},{2,1},{3,2},{4,3},{5,4},{6,5},{7,6},{8,7},{9,8},{10,9},{11,1... | collective-permute-start | bytes 24584 | tf_op jit(solution)/shard_map/ppermute | solution.py:734
  87.6 5.5 %shard_map.151.early = f32[16,128]{1,0:T(8,128)S(1)} custom-call(bf16[8,2,488,128]{3,2,1,0:T(8,128)(2,1)S(1)} %get-tuple-element.14.refs_0_.form, bf16[256,512]{1,0:T(8,128)(2,1)S(1)} %copy-done.1, bf16[320,208]{1,0:T(8,128)(2,1)S(1)} %copy-done.2, bf16[88,160]{1,0:T(8,128)(2,1)S(1)} %copy-done.5, bf16[256,256]{1,0:T(8,128)(2,1)S(1)} %copy-done.3, ...), custom_call_target="tpu_custom_call" | custom-call | tf_op jit(solution)/shard_map/pallas_call | solution.py:514
  93.1 4.5 %shard_map.152.late = f32[16,128]{1,0:T(8,128)S(1)} custom-call(bf16[8,2,488,128]{3,2,1,0:T(8,128)(2,1)S(1)} %get-tuple-element.14.refs_0_.form, bf16[8,2,64,128]{3,2,1,0:T(8,128)(2,1)S(1)} %collective-permute-done.top, bf16[8,2,64,128]{3,2,1,0:T(8,128)(2,1)S(1)} %collective-permute-done.1.bottom, bf16[256,512]{1,0:T(8,128)(2,1)S(1)} %copy-done.1, ...), custom_call_target="tpu_custom_call" | custom-call | tf_op jit(solution)/shard_map/pallas_call | solution.py:547
  97.5 2.9 %shard_map.154 = (f32[16,128]{1,0:T(8,128)S(1)}, f32[16,128]{1,0:T(8,128)S(1)}) custom-call(f32[16,128]{1,0:T(8,128)S(1)} %shard_map.151.early, f32[16,128]{1,0:T(8,128)S(1)} %shard_map.152.late, f32[16,128]{1,0:T(8,128)S(1)} %get-tuple-element.19.edge, s32[12,16]{1,0:T(8,128)S(1)} %copy-done.7, bf16[8,2,488,128]{3,2,1,0:T(8,128)(2,1)S(1)} %get-tuple-element.14.refs_0_.form, ...), custom_call_target="tpu_custom_call" | custom-call | tf_op jit(solution)/shard_map/pallas_call | solution.py:525
  100.5 0.0 collective-permute-done.4
  100.5 0.0 collective-permute-done.5
  100.5 3.6 %collective-permute-start.7 = (f32[8,128]{1,0:T(8,128)S(1)}, f32[8,128]{1,0:T(8,128)S(1)}, u32[]{:S(2)}, u32[]{:S(2)}) collective-permute-start(f32[8,128]{1,0:T(8,128)S(1)} %get-tuple-element.30), channel_id=1, source_target_pairs={{32,0},{64,32},{96,64},{33,1},{65,33},{97,65},{34,2},{66,34},{98,6... | collective-permute-start | bytes 12296 | tf_op jit(solution)/shard_map/ppermute | solution.py:734
  104.1 2.2 %collective-permute-start.6 = (f32[8,128]{1,0:T(8,128)S(1)}, f32[8,128]{1,0:T(8,128)S(1)}, u32[]{:S(2)}, u32[]{:S(2)}) collective-permute-start(f32[8,128]{1,0:T(8,128)S(1)} %get-tuple-element.31), channel_id=1, source_target_pairs={{0,32},{32,64},{64,96},{1,33},{33,65},{65,97},{2,34},{34,66},{66,9... | collective-permute-start | bytes 12296 | tf_op jit(solution)/shard_map/ppermute | solution.py:734
  106.4 0.0 collective-permute-done.7.beneath
  106.4 3.3 %collective-permute-done.6.above = f32[8,128]{1,0:T(8,128)S(1)} collective-permute-done((f32[8,128]{1,0:T(8,128)S(1)}, f32[8,128]{1,0:T(8,128)S(1)}, u32[]{:S(2)}, u32[]{:S(2)}) %collective-permute-start.6) | collective-permute-done | bytes 4128 | tf_op jit(solution)/shard_map/ppermute | solution.py:734
  109.7 0.9 shard_map.155
  (6 shorter events, 0.1 us)
Async XLA Ops:
  42.3 25.7 %copy-start = (bf16[1280,128]{1,0:T(8,128)(2,1)S(1)}, bf16[1280,128]{1,0:T(8,128)(2,1)}, u32[]{:S(2)}) copy-start(bf16[1280,128]{1,0:T(8,128)(2,1)} %constant.22.clone.refs_6_.select) | copy-start | bytes 983044
  42.3 25.7 %copy-start.1 = (bf16[256,512]{1,0:T(8,128)(2,1)S(1)}, bf16[256,512]{1,0:T(8,128)(2,1)}, u32[]{:S(2)}) copy-start(bf16[256,512]{1,0:T(8,128)(2,1)} %constant.17.clone.refs_1_.first) | copy-start | bytes 786436
  42.3 25.7 %copy-start.2 = (bf16[320,208]{1,0:T(8,128)(2,1)S(1)}, bf16[320,208]{1,0:T(8,128)(2,1)}, u32[]{:S(2)}) copy-start(bf16[320,208]{1,0:T(8,128)(2,1)} %constant.18.clone.refs_2_.second) | copy-start | bytes 399364
  42.3 25.7 %copy-start.3 = (bf16[256,256]{1,0:T(8,128)(2,1)S(1)}, bf16[256,256]{1,0:T(8,128)(2,1)}, u32[]{:S(2)}) copy-start(bf16[256,256]{1,0:T(8,128)(2,1)} %constant.20.clone.refs_4_.mix_cols) | copy-start | bytes 393220
  42.3 25.7 %copy-start.4 = (bf16[256,128]{1,0:T(8,128)(2,1)S(1)}, bf16[256,128]{1,0:T(8,128)(2,1)}, u32[]{:S(2)}) copy-start(bf16[256,128]{1,0:T(8,128)(2,1)} %constant.23.clone.refs_7_.window) | copy-start | bytes 196612
  42.3 25.7 %copy-start.5 = (bf16[88,160]{1,0:T(8,128)(2,1)S(1)}, bf16[88,160]{1,0:T(8,128)(2,1)}, u32[]{:S(2)}) copy-start(bf16[88,160]{1,0:T(8,128)(2,1)} %constant.19.clone.refs_3_.mix_rows) | copy-start | bytes 84484
  42.3 25.7 %copy-start.6 = (bf16[16,256]{1,0:T(8,128)(2,1)S(1)}, bf16[16,256]{1,0:T(8,128)(2,1)}, u32[]{:S(2)}) copy-start(bf16[16,256]{1,0:T(8,128)(2,1)} %constant.21.clone.refs_5_.sign_cols) | copy-start | bytes 24580
  42.3 25.7 %copy-start.7 = (s32[12,16]{1,0:T(8,128)S(1)}, s32[12,16]{1,0:T(8,128)}, u32[]{:S(2)}) copy-start(s32[12,16]{1,0:T(8,128)} %valid.3) | copy-start | bytes 2308
  44.4 9.4 %collective-permute-start = (bf16[8,2,64,128]{3,2,1,0:T(8,128)(2,1)S(1)}, bf16[8,2,64,128]{3,2,1,0:T(8,128)(2,1)S(1)}, u32[]{:S(2)}, u32[]{:S(2)}) collective-permute-start(bf16[8,2,64,128]{3,2,1,0:T(8,128)(2,1)S(1)} %get-tuple-element.15), channel_id=1, source_target_pairs={{0,32},{32,64},{64,96},{1,33},{33,65},{65,97},{2,34},{34,66},{66,9... | collective-permute-start | bytes 786440 | tf_op jit(solution)/shard_map/ppermute | solution.py:734
  46.3 9.4 %collective-permute-start.1 = (bf16[8,2,64,128]{3,2,1,0:T(8,128)(2,1)S(1)}, bf16[8,2,64,128]{3,2,1,0:T(8,128)(2,1)S(1)}, u32[]{:S(2)}, u32[]{:S(2)}) collective-permute-start(bf16[8,2,64,128]{3,2,1,0:T(8,128)(2,1)S(1)} %get-tuple-element.16), channel_id=1, source_target_pairs={{32,0},{64,32},{96,64},{33,1},{65,33},{97,65},{34,2},{66,34},{98,6... | collective-permute-start | bytes 786440 | tf_op jit(solution)/shard_map/ppermute | solution.py:734
  55.7 6.3 %collective-permute-start.3 = (bf16[2,608,128]{2,1,0:T(8,128)(2,1)S(1)}, bf16[2,608,128]{2,1,0:T(8,128)(2,1)S(1)}, u32[]{:S(2)}, u32[]{:S(2)}) collective-permute-start(bf16[2,608,128]{2,1,0:T(8,128)(2,1)S(1)} %pad_add_fusion), channel_id=1, source_target_pairs={{1,0},{2,1},{3,2},{4,3},{5,4},{6,5},{7,6},{8,7},{9,8},{10,9},{11,1... | collective-permute-start | bytes 933896 | tf_op jit(solution)/shard_map/ppermute | solution.py:734
  57.7 10.3 %collective-permute-start.2 = (bf16[2,608,128]{2,1,0:T(8,128)(2,1)S(1)}, bf16[2,608,128]{2,1,0:T(8,128)(2,1)S(1)}, u32[]{:S(2)}, u32[]{:S(2)}) collective-permute-start(bf16[2,608,128]{2,1,0:T(8,128)(2,1)S(1)} %pad_add_fusion.1), channel_id=1, source_target_pairs={{0,1},{1,2},{2,3},{3,4},{4,5},{5,6},{6,7},{7,8},{8,9},{9,10},{10,1... | collective-permute-start | bytes 933896 | tf_op jit(solution)/shard_map/ppermute | solution.py:734
  79.7 20.8 %collective-permute-start.4 = (f32[16,128]{1,0:T(8,128)S(1)}, f32[16,128]{1,0:T(8,128)S(1)}, u32[]{:S(2)}, u32[]{:S(2)}) collective-permute-start(f32[16,128]{1,0:T(8,128)S(1)} %get-tuple-element.22), channel_id=1, source_target_pairs={{0,1},{1,2},{2,3},{3,4},{4,5},{5,6},{6,7},{7,8},{8,9},{9,10},{10,1... | collective-permute-start | bytes 24584 | tf_op jit(solution)/shard_map/ppermute | solution.py:734
  81.6 18.8 %collective-permute-start.5 = (f32[16,128]{1,0:T(8,128)S(1)}, f32[16,128]{1,0:T(8,128)S(1)}, u32[]{:S(2)}, u32[]{:S(2)}) collective-permute-start(f32[16,128]{1,0:T(8,128)S(1)} %get-tuple-element.23), channel_id=1, source_target_pairs={{1,0},{2,1},{3,2},{4,3},{5,4},{6,5},{7,6},{8,7},{9,8},{10,9},{11,1... | collective-permute-start | bytes 24584 | tf_op jit(solution)/shard_map/ppermute | solution.py:734
  100.5 5.9 %collective-permute-start.7 = (f32[8,128]{1,0:T(8,128)S(1)}, f32[8,128]{1,0:T(8,128)S(1)}, u32[]{:S(2)}, u32[]{:S(2)}) collective-permute-start(f32[8,128]{1,0:T(8,128)S(1)} %get-tuple-element.30), channel_id=1, source_target_pairs={{32,0},{64,32},{96,64},{33,1},{65,33},{97,65},{34,2},{66,34},{98,6... | collective-permute-start | bytes 12296 | tf_op jit(solution)/shard_map/ppermute | solution.py:734
  104.1 5.5 %collective-permute-start.6 = (f32[8,128]{1,0:T(8,128)S(1)}, f32[8,128]{1,0:T(8,128)S(1)}, u32[]{:S(2)}, u32[]{:S(2)}) collective-permute-start(f32[8,128]{1,0:T(8,128)S(1)} %get-tuple-element.31), channel_id=1, source_target_pairs={{0,32},{32,64},{64,96},{1,33},{33,65},{65,97},{2,34},{34,66},{66,9... | collective-permute-start | bytes 12296 | tf_op jit(solution)/shard_map/ppermute | solution.py:734

commit v7 on v6

--- a/solution.py
+++ b/solution.py
@@ -94,13 +94,13 @@
 
 
 def dot_exact(a, b):
-    return lax.dot_general(
-        a,
-        b,
-        (((1,), (0,)), ((), ())),
-        preferred_element_type=jnp.float32,
-        precision=lax.Precision.HIGHEST,
-    )
+    parts = []
+    for _ in range(3):
+        parts.append(a.astype(jnp.bfloat16))
+        a = a - parts[-1].astype(jnp.float32)
+    rows = a.shape[0]
+    both = dot(jnp.concatenate(parts, axis=0), b)
+    return both[:rows] + (both[rows : 2 * rows] + both[2 * rows :])
 
 
 EDGE_GROUPS = (0, 4, 5)
@@ -302,11 +302,11 @@
 
 
 def finish(raw, raw_end, cells, select, window, groups):
-    window = window[...].astype(jnp.float32)
+    window = window[...]
     scale = (1.0 / (PATCH * PATCH)) / (
         window_means(cells, 0, window, groups) * window_means(cells, 1, window, groups)
     )
-    sums = dot_exact(raw[...].reshape(WIN * 16, 1280), select[...].astype(jnp.float32)).reshape(WIN, 16, 128)
+    sums = dot_exact(raw[...].reshape(WIN * 16, 1280), select[...]).reshape(WIN, 16, 128)
     pad = jnp.zeros((120, 128), jnp.float32)
     ends = [
         pltpu.roll(jnp.concatenate([raw_end[n], pad], axis=0).T[:16], 32, axis=1) for n in range(WIN)
@@ -567,17 +567,8 @@
 
 def pack_kernel(*refs):
     sources, out, rows, held, arrived = refs[:6], refs[6], refs[7], refs[8:14], refs[14]
-    copies = [pltpu.make_async_copy(sources[n], held[n], arrived.at[n]) for n in range(2, 6)]
-    pieces = []
-    for k in range(5):
-        lanes = pl.ds(8 * TILE_W * k, 8 * TILE_W)
-        pieces.append(
-            [
-                pltpu.make_async_copy(sources[n].at[:, lanes], held[n].at[:, lanes], arrived.at[6 + 2 * k + n])
-                for n in range(2)
-            ]
-        )
-    for copy in copies + sum(pieces, []):
+    copies = [pltpu.make_async_copy(src, dst, arrived.at[n]) for n, (src, dst) in enumerate(zip(sources, held))]
+    for copy in copies:
         copy.start()
     for copy in copies:
         copy.wait()
@@ -622,9 +613,6 @@
         return jnp.concatenate([a_part, b_part], axis=0)
 
     for y in range(0, SLOT_H, 2):
-        if y % 8 == 0 and y < TILE_H:
-            for copy in pieces[y // 8]:
-                copy.wait()
         both = jnp.concatenate([send_row(y), send_row(y + 1)], axis=1)
         sent = dot(select, both)
         rows[pl.ds(y, 128, stride=SLOT_H), :] = sent[:, :128]
@@ -705,7 +693,7 @@
         scratch_shapes=[
             pltpu.VMEM((128 * SLOT_H, 128), jnp.float32),
             *[pltpu.VMEM(x.shape, x.dtype) for x in arrays],
-            pltpu.SemaphoreType.DMA((16,)),
+            pltpu.SemaphoreType.DMA((6,)),
         ],
         compiler_params=pltpu.CompilerParams(vmem_limit_bytes=60 << 20),
     )(*arrays)

time: 111 us -> 109 us (0.982)
  Pallas kernels: 32.5 us -> 30.8 us
  transfers between devices with their start and end apart: 8 -> 8, of which waited for: 5 -> 5; matrix products, arithmetic and copies ran while one was open for 0% -> 0% of each run, Pallas kernels for 12% -> 11%
where the time goes in v7:
time: 109 us
  blocking collectives  36.7 us (34%)
  Pallas kernels  30.8 us (28%)
  starting transfers between devices  23.9 us (22%)
  waiting for transfers between devices  16.6 us (15%)
    all_to_all x1, blocking collectives, per_device(): lax.all_to_all(packed, ('row', 'col'), split_axis=0, concat_axis=0, tiled...  36.7 us
    ppermute x8, starting transfers between devices, shifted(): return lax.ppermute(block, axis, pairs)  23.9 us
    ppermute x8, waiting for transfers between devices, shifted(): return lax.ppermute(block, axis, pairs)  16.6 us
    pallas_call x1, Pallas kernels, correlate_edge(): pl.pallas_call(edge_kernel, out_shape=(SMALL,) * 3, in_specs=[VMEM_SPEC]...  11.4 us
    pallas_call x1, Pallas kernels, correlate_early(): pl.pallas_call(early_kernel, out_shape=SMALL, in_specs=[VMEM_SPEC] * 8, o...  5.27 us
    pallas_call x1, Pallas kernels, correlate_late(): pl.pallas_call(late_kernel, out_shape=SMALL, in_specs=[VMEM_SPEC] * 10, o...  4.29 us
    pallas_call x1, Pallas kernels, pack(): pl.pallas_call(pack_kernel, out_shape=jax.ShapeDtypeStruct((128, SLOT_H,...  4.11 us
    pallas_call x1, Pallas kernels, correlate_tail(): pl.pallas_call(tail_kernel, out_shape=(SMALL,) * 2, in_specs=[VMEM_SPEC]...  2.79 us
  transfers between devices with their start and end apart: 8, of which 5 were waited for; matrix products, arithmetic and copies ran while one was open for 0% of the time, Pallas kernels for 11%

profile of v7, /device:TPU:34, one launch (start us, length us, event | category | flops | bytes accessed | tf_op | source)
XLA Modules:
  0.0 108.9 jit_solution(2325309310851097020)
XLA Ops:
  0.6 4.1 %shard_map.149 = bf16[128,56,128]{2,1,0:T(8,128)(2,1)} custom-call(bf16[96,3200]{1,0:T(8,128)(2,1)} %refs_0_.1, bf16[96,3200]{1,0:T(8,128)(2,1)} %refs_1_.3, s32[1,96]{1,0:T(1,128)} %bitcast.16, s32[1,96]{1,0:T(1,128)} %bitcast.17, s32[2,96]{1,0:T(2,128)} %bitcast.14, s32[2,96]{1,0:T(2,128)} %bitcast.15), custom_call_target="tpu_custom_call" | custom-call | tf_op jit(solution)/shard_map/pallas_call | solution.py:688
  4.8 36.7 %all_to_all.5.got = bf16[128,56,128]{2,1,0:T(8,128)(2,1)S(1)} all-to-all(bf16[128,56,128]{2,1,0:T(8,128)(2,1)} %shard_map.149), channel_id=1, replica_groups=mesh['row'=4,'col'=32] {'row','col'}, dimensions={0} | all-to-all | bytes 3670016 | tf_op jit(solution)/shard_map/all_to_all | solution.py:732
  41.4 0.0 copy-start
  41.4 0.0 copy-start.1
  41.4 0.0 copy-start.2
  41.4 0.0 copy-start.3
  41.4 0.0 copy-start.4
  41.4 0.0 copy-start.5
  41.4 0.0 copy-start.6
  41.5 0.0 copy-start.7
  41.5 2.0 %shard_map.150 = (bf16[8,2,488,128]{3,2,1,0:T(8,128)(2,1)S(1)}, bf16[8,2,64,128]{3,2,1,0:T(8,128)(2,1)S(1)}, bf16[8,2,64,128]{3,2,1,0:T(8,128)(2,1)S(1)}, bf16[2...) custom-call(bf16[128,56,128]{2,1,0:T(8,128)(2,1)S(1)} %all_to_all.5.got), custom_call_target="tpu_custom_call" | custom-call | tf_op jit(solution)/shard_map/pallas_call | solution.py:705
  43.5 1.9 %collective-permute-start = (bf16[8,2,64,128]{3,2,1,0:T(8,128)(2,1)S(1)}, bf16[8,2,64,128]{3,2,1,0:T(8,128)(2,1)S(1)}, u32[]{:S(2)}, u32[]{:S(2)}) collective-permute-start(bf16[8,2,64,128]{3,2,1,0:T(8,128)(2,1)S(1)} %get-tuple-element.15), channel_id=1, source_target_pairs={{0,32},{32,64},{64,96},{1,33},{33,65},{65,97},{2,34},{34,66},{66,9... | collective-permute-start | bytes 786440 | tf_op jit(solution)/shard_map/ppermute | solution.py:722
  45.5 3.9 %collective-permute-start.1 = (bf16[8,2,64,128]{3,2,1,0:T(8,128)(2,1)S(1)}, bf16[8,2,64,128]{3,2,1,0:T(8,128)(2,1)S(1)}, u32[]{:S(2)}, u32[]{:S(2)}) collective-permute-start(bf16[8,2,64,128]{3,2,1,0:T(8,128)(2,1)S(1)} %get-tuple-element.16), channel_id=1, source_target_pairs={{32,0},{64,32},{96,64},{33,1},{65,33},{97,65},{34,2},{66,34},{98,6... | collective-permute-start | bytes 786440 | tf_op jit(solution)/shard_map/ppermute | solution.py:722
  49.4 3.5 %collective-permute-done.top = bf16[8,2,64,128]{3,2,1,0:T(8,128)(2,1)S(1)} collective-permute-done((bf16[8,2,64,128]{3,2,1,0:T(8,128)(2,1)S(1)}, bf16[8,2,64,128]{3,2,1,0:T(8,128)(2,1)S(1)}, u32[]{:S(2)}, u32[]{:S(2)}) %collective-permute-start) | collective-permute-done | bytes 262176 | tf_op jit(solution)/shard_map/ppermute | solution.py:722
  52.9 1.9 %collective-permute-done.1.bottom = bf16[8,2,64,128]{3,2,1,0:T(8,128)(2,1)S(1)} collective-permute-done((bf16[8,2,64,128]{3,2,1,0:T(8,128)(2,1)S(1)}, bf16[8,2,64,128]{3,2,1,0:T(8,128)(2,1)S(1)}, u32[]{:S(2)}, u32[]{:S(2)}) %collective-permute-start.1) | collective-permute-done | bytes 262176 | tf_op jit(solution)/shard_map/ppermute | solution.py:722
  54.9 1.9 %collective-permute-start.3 = (bf16[2,608,128]{2,1,0:T(8,128)(2,1)S(1)}, bf16[2,608,128]{2,1,0:T(8,128)(2,1)S(1)}, u32[]{:S(2)}, u32[]{:S(2)}) collective-permute-start(bf16[2,608,128]{2,1,0:T(8,128)(2,1)S(1)} %pad_add_fusion), channel_id=1, source_target_pairs={{1,0},{2,1},{3,2},{4,3},{5,4},{6,5},{7,6},{8,7},{9,8},{10,9},{11,1... | collective-permute-start | bytes 933896 | tf_op jit(solution)/shard_map/ppermute | solution.py:722
  56.8 2.4 %collective-permute-start.2 = (bf16[2,608,128]{2,1,0:T(8,128)(2,1)S(1)}, bf16[2,608,128]{2,1,0:T(8,128)(2,1)S(1)}, u32[]{:S(2)}, u32[]{:S(2)}) collective-permute-start(bf16[2,608,128]{2,1,0:T(8,128)(2,1)S(1)} %pad_add_fusion.1), channel_id=1, source_target_pairs={{0,1},{1,2},{2,3},{3,4},{4,5},{5,6},{6,7},{7,8},{8,9},{9,10},{10,1... | collective-permute-start | bytes 933896 | tf_op jit(solution)/shard_map/ppermute | solution.py:722
  59.2 1.9 %collective-permute-done.3.right = bf16[2,608,128]{2,1,0:T(8,128)(2,1)S(1)} collective-permute-done((bf16[2,608,128]{2,1,0:T(8,128)(2,1)S(1)}, bf16[2,608,128]{2,1,0:T(8,128)(2,1)S(1)}, u32[]{:S(2)}, u32[]{:S(2)}) %collective-permute-start.3) | collective-permute-done | bytes 311328 | tf_op jit(solution)/shard_map/ppermute | solution.py:722
  61.2 6.0 %collective-permute-done.2.left = bf16[2,608,128]{2,1,0:T(8,128)(2,1)S(1)} collective-permute-done((bf16[2,608,128]{2,1,0:T(8,128)(2,1)S(1)}, bf16[2,608,128]{2,1,0:T(8,128)(2,1)S(1)}, u32[]{:S(2)}, u32[]{:S(2)}) %collective-permute-start.2) | collective-permute-done | bytes 311328 | tf_op jit(solution)/shard_map/ppermute | solution.py:722
  67.2 0.0 copy-done
  67.2 0.0 copy-done.1
  67.2 0.0 copy-done.2
  67.2 0.0 copy-done.3
  67.2 0.0 copy-done.4
  67.2 0.0 copy-done.5
  67.2 0.0 copy-done.6
  67.2 0.0 copy-done.7
  67.2 11.4 %shard_map.153 = (f32[16,128]{1,0:T(8,128)S(1)}, f32[16,128]{1,0:T(8,128)S(1)}, f32[16,128]{1,0:T(8,128)S(1)}) custom-call(bf16[8,2,488,128]{3,2,1,0:T(8,128)(2,1)S(1)} %get-tuple-element.14.refs_0_.form, bf16[8,2,64,128]{3,2,1,0:T(8,128)(2,1)S(1)} %collective-permute-done.top, bf16[8,2,64,128]{3,2,1,0:T(8,128)(2,1)S(1)} %collective-permute-done.1.bottom, ...), custom_call_target="tpu_custom_call" | custom-call | tf_op jit(solution)/shard_map/pallas_call | solution.py:536
  78.6 1.9 %collective-permute-start.4 = (f32[16,128]{1,0:T(8,128)S(1)}, f32[16,128]{1,0:T(8,128)S(1)}, u32[]{:S(2)}, u32[]{:S(2)}) collective-permute-start(f32[16,128]{1,0:T(8,128)S(1)} %get-tuple-element.22), channel_id=1, source_target_pairs={{0,1},{1,2},{2,3},{3,4},{4,5},{5,6},{6,7},{7,8},{8,9},{9,10},{10,1... | collective-permute-start | bytes 24584 | tf_op jit(solution)/shard_map/ppermute | solution.py:722
  80.5 5.9 %collective-permute-start.5 = (f32[16,128]{1,0:T(8,128)S(1)}, f32[16,128]{1,0:T(8,128)S(1)}, u32[]{:S(2)}, u32[]{:S(2)}) collective-permute-start(f32[16,128]{1,0:T(8,128)S(1)} %get-tuple-element.23), channel_id=1, source_target_pairs={{1,0},{2,1},{3,2},{4,3},{5,4},{6,5},{7,6},{8,7},{9,8},{10,9},{11,1... | collective-permute-start | bytes 24584 | tf_op jit(solution)/shard_map/ppermute | solution.py:722
  86.4 5.3 %shard_map.151.early = f32[16,128]{1,0:T(8,128)S(1)} custom-call(bf16[8,2,488,128]{3,2,1,0:T(8,128)(2,1)S(1)} %get-tuple-element.14.refs_0_.form, bf16[256,512]{1,0:T(8,128)(2,1)S(1)} %copy-done.1, bf16[320,208]{1,0:T(8,128)(2,1)S(1)} %copy-done.2, bf16[88,160]{1,0:T(8,128)(2,1)S(1)} %copy-done.5, bf16[256,256]{1,0:T(8,128)(2,1)S(1)} %copy-done.3, ...), custom_call_target="tpu_custom_call" | custom-call | tf_op jit(solution)/shard_map/pallas_call | solution.py:514
  91.7 4.3 %shard_map.152.late = f32[16,128]{1,0:T(8,128)S(1)} custom-call(bf16[8,2,488,128]{3,2,1,0:T(8,128)(2,1)S(1)} %get-tuple-element.14.refs_0_.form, bf16[8,2,64,128]{3,2,1,0:T(8,128)(2,1)S(1)} %collective-permute-done.top, bf16[8,2,64,128]{3,2,1,0:T(8,128)(2,1)S(1)} %collective-permute-done.1.bottom, bf16[256,512]{1,0:T(8,128)(2,1)S(1)} %copy-done.1, ...), custom_call_target="tpu_custom_call" | custom-call | tf_op jit(solution)/shard_map/pallas_call | solution.py:547
  96.0 2.8 %shard_map.154 = (f32[16,128]{1,0:T(8,128)S(1)}, f32[16,128]{1,0:T(8,128)S(1)}) custom-call(f32[16,128]{1,0:T(8,128)S(1)} %shard_map.151.early, f32[16,128]{1,0:T(8,128)S(1)} %shard_map.152.late, f32[16,128]{1,0:T(8,128)S(1)} %get-tuple-element.19.edge, s32[12,16]{1,0:T(8,128)S(1)} %copy-done.7, bf16[8,2,488,128]{3,2,1,0:T(8,128)(2,1)S(1)} %get-tuple-element.14.refs_0_.form, ...), custom_call_target="tpu_custom_call" | custom-call | tf_op jit(solution)/shard_map/pallas_call | solution.py:525
  98.8 0.0 collective-permute-done.4
  98.8 0.0 collective-permute-done.5
  98.8 3.6 %collective-permute-start.7 = (f32[8,128]{1,0:T(8,128)S(1)}, f32[8,128]{1,0:T(8,128)S(1)}, u32[]{:S(2)}, u32[]{:S(2)}) collective-permute-start(f32[8,128]{1,0:T(8,128)S(1)} %get-tuple-element.30), channel_id=1, source_target_pairs={{32,0},{64,32},{96,64},{33,1},{65,33},{97,65},{34,2},{66,34},{98,6... | collective-permute-start | bytes 12296 | tf_op jit(solution)/shard_map/ppermute | solution.py:722
  102.5 2.2 %collective-permute-start.6 = (f32[8,128]{1,0:T(8,128)S(1)}, f32[8,128]{1,0:T(8,128)S(1)}, u32[]{:S(2)}, u32[]{:S(2)}) collective-permute-start(f32[8,128]{1,0:T(8,128)S(1)} %get-tuple-element.31), channel_id=1, source_target_pairs={{0,32},{32,64},{64,96},{1,33},{33,65},{65,97},{2,34},{34,66},{66,9... | collective-permute-start | bytes 12296 | tf_op jit(solution)/shard_map/ppermute | solution.py:722
  104.7 0.0 collective-permute-done.7.beneath
  104.7 3.3 %collective-permute-done.6.above = f32[8,128]{1,0:T(8,128)S(1)} collective-permute-done((f32[8,128]{1,0:T(8,128)S(1)}, f32[8,128]{1,0:T(8,128)S(1)}, u32[]{:S(2)}, u32[]{:S(2)}) %collective-permute-start.6) | collective-permute-done | bytes 4128 | tf_op jit(solution)/shard_map/ppermute | solution.py:722
  108.0 0.9 shard_map.155
  (6 shorter events, 0.1 us)
Async XLA Ops:
  41.4 25.7 %copy-start = (bf16[1280,128]{1,0:T(8,128)(2,1)S(1)}, bf16[1280,128]{1,0:T(8,128)(2,1)}, u32[]{:S(2)}) copy-start(bf16[1280,128]{1,0:T(8,128)(2,1)} %constant.22.clone.refs_6_.select) | copy-start | bytes 983044
  41.4 25.7 %copy-start.1 = (bf16[256,512]{1,0:T(8,128)(2,1)S(1)}, bf16[256,512]{1,0:T(8,128)(2,1)}, u32[]{:S(2)}) copy-start(bf16[256,512]{1,0:T(8,128)(2,1)} %constant.17.clone.refs_1_.first) | copy-start | bytes 786436
  41.4 25.7 %copy-start.2 = (bf16[320,208]{1,0:T(8,128)(2,1)S(1)}, bf16[320,208]{1,0:T(8,128)(2,1)}, u32[]{:S(2)}) copy-start(bf16[320,208]{1,0:T(8,128)(2,1)} %constant.18.clone.refs_2_.second) | copy-start | bytes 399364
  41.4 25.7 %copy-start.3 = (bf16[256,256]{1,0:T(8,128)(2,1)S(1)}, bf16[256,256]{1,0:T(8,128)(2,1)}, u32[]{:S(2)}) copy-start(bf16[256,256]{1,0:T(8,128)(2,1)} %constant.20.clone.refs_4_.mix_cols) | copy-start | bytes 393220
  41.4 25.8 %copy-start.4 = (bf16[256,128]{1,0:T(8,128)(2,1)S(1)}, bf16[256,128]{1,0:T(8,128)(2,1)}, u32[]{:S(2)}) copy-start(bf16[256,128]{1,0:T(8,128)(2,1)} %constant.23.clone.refs_7_.window) | copy-start | bytes 196612
  41.4 25.8 %copy-start.5 = (bf16[88,160]{1,0:T(8,128)(2,1)S(1)}, bf16[88,160]{1,0:T(8,128)(2,1)}, u32[]{:S(2)}) copy-start(bf16[88,160]{1,0:T(8,128)(2,1)} %constant.19.clone.refs_3_.mix_rows) | copy-start | bytes 84484
  41.4 25.7 %copy-start.6 = (bf16[16,256]{1,0:T(8,128)(2,1)S(1)}, bf16[16,256]{1,0:T(8,128)(2,1)}, u32[]{:S(2)}) copy-start(bf16[16,256]{1,0:T(8,128)(2,1)} %constant.21.clone.refs_5_.sign_cols) | copy-start | bytes 24580
  41.5 25.7 %copy-start.7 = (s32[12,16]{1,0:T(8,128)S(1)}, s32[12,16]{1,0:T(8,128)}, u32[]{:S(2)}) copy-start(s32[12,16]{1,0:T(8,128)} %valid.3) | copy-start | bytes 2308
  43.5 9.4 %collective-permute-start = (bf16[8,2,64,128]{3,2,1,0:T(8,128)(2,1)S(1)}, bf16[8,2,64,128]{3,2,1,0:T(8,128)(2,1)S(1)}, u32[]{:S(2)}, u32[]{:S(2)}) collective-permute-start(bf16[8,2,64,128]{3,2,1,0:T(8,128)(2,1)S(1)} %get-tuple-element.15), channel_id=1, source_target_pairs={{0,32},{32,64},{64,96},{1,33},{33,65},{65,97},{2,34},{34,66},{66,9... | collective-permute-start | bytes 786440 | tf_op jit(solution)/shard_map/ppermute | solution.py:722
  45.5 9.4 %collective-permute-start.1 = (bf16[8,2,64,128]{3,2,1,0:T(8,128)(2,1)S(1)}, bf16[8,2,64,128]{3,2,1,0:T(8,128)(2,1)S(1)}, u32[]{:S(2)}, u32[]{:S(2)}) collective-permute-start(bf16[8,2,64,128]{3,2,1,0:T(8,128)(2,1)S(1)} %get-tuple-element.16), channel_id=1, source_target_pairs={{32,0},{64,32},{96,64},{33,1},{65,33},{97,65},{34,2},{66,34},{98,6... | collective-permute-start | bytes 786440 | tf_op jit(solution)/shard_map/ppermute | solution.py:722
  54.9 6.3 %collective-permute-start.3 = (bf16[2,608,128]{2,1,0:T(8,128)(2,1)S(1)}, bf16[2,608,128]{2,1,0:T(8,128)(2,1)S(1)}, u32[]{:S(2)}, u32[]{:S(2)}) collective-permute-start(bf16[2,608,128]{2,1,0:T(8,128)(2,1)S(1)} %pad_add_fusion), channel_id=1, source_target_pairs={{1,0},{2,1},{3,2},{4,3},{5,4},{6,5},{7,6},{8,7},{9,8},{10,9},{11,1... | collective-permute-start | bytes 933896 | tf_op jit(solution)/shard_map/ppermute | solution.py:722
  56.8 10.3 %collective-permute-start.2 = (bf16[2,608,128]{2,1,0:T(8,128)(2,1)S(1)}, bf16[2,608,128]{2,1,0:T(8,128)(2,1)S(1)}, u32[]{:S(2)}, u32[]{:S(2)}) collective-permute-start(bf16[2,608,128]{2,1,0:T(8,128)(2,1)S(1)} %pad_add_fusion.1), channel_id=1, source_target_pairs={{0,1},{1,2},{2,3},{3,4},{4,5},{5,6},{6,7},{7,8},{8,9},{9,10},{10,1... | collective-permute-start | bytes 933896 | tf_op jit(solution)/shard_map/ppermute | solution.py:722
  78.6 20.2 %collective-permute-start.4 = (f32[16,128]{1,0:T(8,128)S(1)}, f32[16,128]{1,0:T(8,128)S(1)}, u32[]{:S(2)}, u32[]{:S(2)}) collective-permute-start(f32[16,128]{1,0:T(8,128)S(1)} %get-tuple-element.22), channel_id=1, source_target_pairs={{0,1},{1,2},{2,3},{3,4},{4,5},{5,6},{6,7},{7,8},{8,9},{9,10},{10,1... | collective-permute-start | bytes 24584 | tf_op jit(solution)/shard_map/ppermute | solution.py:722
  80.5 18.3 %collective-permute-start.5 = (f32[16,128]{1,0:T(8,128)S(1)}, f32[16,128]{1,0:T(8,128)S(1)}, u32[]{:S(2)}, u32[]{:S(2)}) collective-permute-start(f32[16,128]{1,0:T(8,128)S(1)} %get-tuple-element.23), channel_id=1, source_target_pairs={{1,0},{2,1},{3,2},{4,3},{5,4},{6,5},{7,6},{8,7},{9,8},{10,9},{11,1... | collective-permute-start | bytes 24584 | tf_op jit(solution)/shard_map/ppermute | solution.py:722
  98.8 5.9 %collective-permute-start.7 = (f32[8,128]{1,0:T(8,128)S(1)}, f32[8,128]{1,0:T(8,128)S(1)}, u32[]{:S(2)}, u32[]{:S(2)}) collective-permute-start(f32[8,128]{1,0:T(8,128)S(1)} %get-tuple-element.30), channel_id=1, source_target_pairs={{32,0},{64,32},{96,64},{33,1},{65,33},{97,65},{34,2},{66,34},{98,6... | collective-permute-start | bytes 12296 | tf_op jit(solution)/shard_map/ppermute | solution.py:722
  102.5 5.5 %collective-permute-start.6 = (f32[8,128]{1,0:T(8,128)S(1)}, f32[8,128]{1,0:T(8,128)S(1)}, u32[]{:S(2)}, u32[]{:S(2)}) collective-permute-start(f32[8,128]{1,0:T(8,128)S(1)} %get-tuple-element.31), channel_id=1, source_target_pairs={{0,32},{32,64},{64,96},{1,33},{33,65},{65,97},{2,34},{34,66},{66,9... | collective-permute-start | bytes 12296 | tf_op jit(solution)/shard_map/ppermute | solution.py:722

commit v8 on v7

--- a/solution.py
+++ b/solution.py
@@ -566,7 +566,8 @@
 
 
 def pack_kernel(*refs):
-    sources, out, rows, held, arrived = refs[:6], refs[6], refs[7], refs[8:14], refs[14]
+    sources, target, rows, held, arrived = refs[:6], refs[6], refs[7], refs[8:14], refs[14]
+    out, sent_out = refs[15:]
     copies = [pltpu.make_async_copy(src, dst, arrived.at[n]) for n, (src, dst) in enumerate(zip(sources, held))]
     for copy in copies:
         copy.start()
@@ -624,7 +625,14 @@
         out[pl.ds(8 * n, 8)] = block.astype(jnp.bfloat16)
         return carry
 
-    lax.fori_loop(0, 16, flush, 0)
+    sends = []
+    for part in range(4):
+        lax.fori_loop(4 * part, 4 * part + 4, flush, 0)
+        slots = pl.ds(32 * part, 32)
+        sends.append(pltpu.make_async_copy(out.at[slots], target.at[slots], sent_out.at[part]))
+        sends[-1].start()
+    for send in sends:
+        send.wait()
 
 
 def place_kernel(got, form, up, down, low, high, rows, plane_a, plane_b):
@@ -689,11 +697,13 @@
         pack_kernel,
         out_shape=jax.ShapeDtypeStruct((128, SLOT_H, 128), jnp.bfloat16),
         in_specs=[pl.BlockSpec(memory_space=pltpu.HBM)] * 6,
-        out_specs=VMEM_SPEC,
+        out_specs=pl.BlockSpec(memory_space=pltpu.HBM),
         scratch_shapes=[
             pltpu.VMEM((128 * SLOT_H, 128), jnp.float32),
             *[pltpu.VMEM(x.shape, x.dtype) for x in arrays],
             pltpu.SemaphoreType.DMA((6,)),
+            pltpu.VMEM((128, SLOT_H, 128), jnp.bfloat16),
+            pltpu.SemaphoreType.DMA((4,)),
         ],
         compiler_params=pltpu.CompilerParams(vmem_limit_bytes=60 << 20),
     )(*arrays)

time: 109 us -> 109 us (level)
  no operation moved by 1% of the time
where the time goes in v8:
time: 109 us
  blocking collectives  36.7 us (34%)
  Pallas kernels  30.7 us (28%)
  starting transfers between devices  23.9 us (22%)
  waiting for transfers between devices  16.6 us (15%)
    all_to_all x1, blocking collectives, per_device(): lax.all_to_all(packed, ('row', 'col'), split_axis=0, concat_axis=0, tiled...  36.7 us
    ppermute x8, starting transfers between devices, shifted(): return lax.ppermute(block, axis, pairs)  23.9 us
    ppermute x8, waiting for transfers between devices, shifted(): return lax.ppermute(block, axis, pairs)  16.6 us
    pallas_call x1, Pallas kernels, correlate_edge(): pl.pallas_call(edge_kernel, out_shape=(SMALL,) * 3, in_specs=[VMEM_SPEC]...  11.4 us
    pallas_call x1, Pallas kernels, correlate_early(): pl.pallas_call(early_kernel, out_shape=SMALL, in_specs=[VMEM_SPEC] * 8, o...  5.27 us
    pallas_call x1, Pallas kernels, correlate_late(): pl.pallas_call(late_kernel, out_shape=SMALL, in_specs=[VMEM_SPEC] * 10, o...  4.29 us
    pallas_call x1, Pallas kernels, pack(): pl.pallas_call(pack_kernel, out_shape=jax.ShapeDtypeStruct((128, SLOT_H,...  3.96 us
    pallas_call x1, Pallas kernels, correlate_tail(): pl.pallas_call(tail_kernel, out_shape=(SMALL,) * 2, in_specs=[VMEM_SPEC]...  2.79 us
  transfers between devices with their start and end apart: 8, of which 5 were waited for; matrix products, arithmetic and copies ran while one was open for 0% of the time, Pallas kernels for 11%

profile of v8, /device:TPU:34, one launch (start us, length us, event | category | flops | bytes accessed | tf_op | source)
XLA Modules:
  0.0 108.8 jit_solution(5361299613533056011)
XLA Ops:
  0.6 4.0 %shard_map.149 = bf16[128,56,128]{2,1,0:T(8,128)(2,1)} custom-call(bf16[96,3200]{1,0:T(8,128)(2,1)} %refs_0_.1, bf16[96,3200]{1,0:T(8,128)(2,1)} %refs_1_.3, s32[1,96]{1,0:T(1,128)} %bitcast.16, s32[1,96]{1,0:T(1,128)} %bitcast.17, s32[2,96]{1,0:T(2,128)} %bitcast.14, s32[2,96]{1,0:T(2,128)} %bitcast.15), custom_call_target="tpu_custom_call" | custom-call | tf_op jit(solution)/shard_map/pallas_call | solution.py:696
  4.6 36.7 %all_to_all.5.got = bf16[128,56,128]{2,1,0:T(8,128)(2,1)S(1)} all-to-all(bf16[128,56,128]{2,1,0:T(8,128)(2,1)} %shard_map.149), channel_id=1, replica_groups=mesh['row'=4,'col'=32] {'row','col'}, dimensions={0} | all-to-all | bytes 3670016 | tf_op jit(solution)/shard_map/all_to_all | solution.py:742
  41.3 0.0 copy-start
  41.3 0.0 copy-start.1
  41.3 0.0 copy-start.2
  41.3 0.0 copy-start.3
  41.3 0.0 copy-start.4
  41.3 0.0 copy-start.5
  41.3 0.0 copy-start.6
  41.3 0.0 copy-start.7
  41.3 2.1 %shard_map.150 = (bf16[8,2,488,128]{3,2,1,0:T(8,128)(2,1)S(1)}, bf16[8,2,64,128]{3,2,1,0:T(8,128)(2,1)S(1)}, bf16[8,2,64,128]{3,2,1,0:T(8,128)(2,1)S(1)}, bf16[2...) custom-call(bf16[128,56,128]{2,1,0:T(8,128)(2,1)S(1)} %all_to_all.5.got), custom_call_target="tpu_custom_call" | custom-call | tf_op jit(solution)/shard_map/pallas_call | solution.py:715
  43.4 1.9 %collective-permute-start = (bf16[8,2,64,128]{3,2,1,0:T(8,128)(2,1)S(1)}, bf16[8,2,64,128]{3,2,1,0:T(8,128)(2,1)S(1)}, u32[]{:S(2)}, u32[]{:S(2)}) collective-permute-start(bf16[8,2,64,128]{3,2,1,0:T(8,128)(2,1)S(1)} %get-tuple-element.15), channel_id=1, source_target_pairs={{0,32},{32,64},{64,96},{1,33},{33,65},{65,97},{2,34},{34,66},{66,9... | collective-permute-start | bytes 786440 | tf_op jit(solution)/shard_map/ppermute | solution.py:732
  45.3 3.9 %collective-permute-start.1 = (bf16[8,2,64,128]{3,2,1,0:T(8,128)(2,1)S(1)}, bf16[8,2,64,128]{3,2,1,0:T(8,128)(2,1)S(1)}, u32[]{:S(2)}, u32[]{:S(2)}) collective-permute-start(bf16[8,2,64,128]{3,2,1,0:T(8,128)(2,1)S(1)} %get-tuple-element.16), channel_id=1, source_target_pairs={{32,0},{64,32},{96,64},{33,1},{65,33},{97,65},{34,2},{66,34},{98,6... | collective-permute-start | bytes 786440 | tf_op jit(solution)/shard_map/ppermute | solution.py:732
  49.3 3.5 %collective-permute-done.top = bf16[8,2,64,128]{3,2,1,0:T(8,128)(2,1)S(1)} collective-permute-done((bf16[8,2,64,128]{3,2,1,0:T(8,128)(2,1)S(1)}, bf16[8,2,64,128]{3,2,1,0:T(8,128)(2,1)S(1)}, u32[]{:S(2)}, u32[]{:S(2)}) %collective-permute-start) | collective-permute-done | bytes 262176 | tf_op jit(solution)/shard_map/ppermute | solution.py:732
  52.7 1.9 %collective-permute-done.1.bottom = bf16[8,2,64,128]{3,2,1,0:T(8,128)(2,1)S(1)} collective-permute-done((bf16[8,2,64,128]{3,2,1,0:T(8,128)(2,1)S(1)}, bf16[8,2,64,128]{3,2,1,0:T(8,128)(2,1)S(1)}, u32[]{:S(2)}, u32[]{:S(2)}) %collective-permute-start.1) | collective-permute-done | bytes 262176 | tf_op jit(solution)/shard_map/ppermute | solution.py:732
  54.7 1.9 %collective-permute-start.3 = (bf16[2,608,128]{2,1,0:T(8,128)(2,1)S(1)}, bf16[2,608,128]{2,1,0:T(8,128)(2,1)S(1)}, u32[]{:S(2)}, u32[]{:S(2)}) collective-permute-start(bf16[2,608,128]{2,1,0:T(8,128)(2,1)S(1)} %pad_add_fusion), channel_id=1, source_target_pairs={{1,0},{2,1},{3,2},{4,3},{5,4},{6,5},{7,6},{8,7},{9,8},{10,9},{11,1... | collective-permute-start | bytes 933896 | tf_op jit(solution)/shard_map/ppermute | solution.py:732
  56.7 2.4 %collective-permute-start.2 = (bf16[2,608,128]{2,1,0:T(8,128)(2,1)S(1)}, bf16[2,608,128]{2,1,0:T(8,128)(2,1)S(1)}, u32[]{:S(2)}, u32[]{:S(2)}) collective-permute-start(bf16[2,608,128]{2,1,0:T(8,128)(2,1)S(1)} %pad_add_fusion.1), channel_id=1, source_target_pairs={{0,1},{1,2},{2,3},{3,4},{4,5},{5,6},{6,7},{7,8},{8,9},{9,10},{10,1... | collective-permute-start | bytes 933896 | tf_op jit(solution)/shard_map/ppermute | solution.py:732
  59.1 1.9 %collective-permute-done.3.right = bf16[2,608,128]{2,1,0:T(8,128)(2,1)S(1)} collective-permute-done((bf16[2,608,128]{2,1,0:T(8,128)(2,1)S(1)}, bf16[2,608,128]{2,1,0:T(8,128)(2,1)S(1)}, u32[]{:S(2)}, u32[]{:S(2)}) %collective-permute-start.3) | collective-permute-done | bytes 311328 | tf_op jit(solution)/shard_map/ppermute | solution.py:732
  61.0 6.0 %collective-permute-done.2.left = bf16[2,608,128]{2,1,0:T(8,128)(2,1)S(1)} collective-permute-done((bf16[2,608,128]{2,1,0:T(8,128)(2,1)S(1)}, bf16[2,608,128]{2,1,0:T(8,128)(2,1)S(1)}, u32[]{:S(2)}, u32[]{:S(2)}) %collective-permute-start.2) | collective-permute-done | bytes 311328 | tf_op jit(solution)/shard_map/ppermute | solution.py:732
  67.0 0.0 copy-done
  67.0 0.0 copy-done.1
  67.0 0.0 copy-done.2
  67.0 0.0 copy-done.3
  67.0 0.0 copy-done.4
  67.0 0.0 copy-done.5
  67.0 0.0 copy-done.6
  67.0 0.0 copy-done.7
  67.1 11.4 %shard_map.153 = (f32[16,128]{1,0:T(8,128)S(1)}, f32[16,128]{1,0:T(8,128)S(1)}, f32[16,128]{1,0:T(8,128)S(1)}) custom-call(bf16[8,2,488,128]{3,2,1,0:T(8,128)(2,1)S(1)} %get-tuple-element.14.refs_0_.form, bf16[8,2,64,128]{3,2,1,0:T(8,128)(2,1)S(1)} %collective-permute-done.top, bf16[8,2,64,128]{3,2,1,0:T(8,128)(2,1)S(1)} %collective-permute-done.1.bottom, ...), custom_call_target="tpu_custom_call" | custom-call | tf_op jit(solution)/shard_map/pallas_call | solution.py:536
  78.4 1.9 %collective-permute-start.4 = (f32[16,128]{1,0:T(8,128)S(1)}, f32[16,128]{1,0:T(8,128)S(1)}, u32[]{:S(2)}, u32[]{:S(2)}) collective-permute-start(f32[16,128]{1,0:T(8,128)S(1)} %get-tuple-element.22), channel_id=1, source_target_pairs={{0,1},{1,2},{2,3},{3,4},{4,5},{5,6},{6,7},{7,8},{8,9},{9,10},{10,1... | collective-permute-start | bytes 24584 | tf_op jit(solution)/shard_map/ppermute | solution.py:732
  80.3 5.9 %collective-permute-start.5 = (f32[16,128]{1,0:T(8,128)S(1)}, f32[16,128]{1,0:T(8,128)S(1)}, u32[]{:S(2)}, u32[]{:S(2)}) collective-permute-start(f32[16,128]{1,0:T(8,128)S(1)} %get-tuple-element.23), channel_id=1, source_target_pairs={{1,0},{2,1},{3,2},{4,3},{5,4},{6,5},{7,6},{8,7},{9,8},{10,9},{11,1... | collective-permute-start | bytes 24584 | tf_op jit(solution)/shard_map/ppermute | solution.py:732
  86.3 5.3 %shard_map.151.early = f32[16,128]{1,0:T(8,128)S(1)} custom-call(bf16[8,2,488,128]{3,2,1,0:T(8,128)(2,1)S(1)} %get-tuple-element.14.refs_0_.form, bf16[256,512]{1,0:T(8,128)(2,1)S(1)} %copy-done.1, bf16[320,208]{1,0:T(8,128)(2,1)S(1)} %copy-done.2, bf16[88,160]{1,0:T(8,128)(2,1)S(1)} %copy-done.5, bf16[256,256]{1,0:T(8,128)(2,1)S(1)} %copy-done.3, ...), custom_call_target="tpu_custom_call" | custom-call | tf_op jit(solution)/shard_map/pallas_call | solution.py:514
  91.5 4.3 %shard_map.152.late = f32[16,128]{1,0:T(8,128)S(1)} custom-call(bf16[8,2,488,128]{3,2,1,0:T(8,128)(2,1)S(1)} %get-tuple-element.14.refs_0_.form, bf16[8,2,64,128]{3,2,1,0:T(8,128)(2,1)S(1)} %collective-permute-done.top, bf16[8,2,64,128]{3,2,1,0:T(8,128)(2,1)S(1)} %collective-permute-done.1.bottom, bf16[256,512]{1,0:T(8,128)(2,1)S(1)} %copy-done.1, ...), custom_call_target="tpu_custom_call" | custom-call | tf_op jit(solution)/shard_map/pallas_call | solution.py:547
  95.8 2.8 %shard_map.154 = (f32[16,128]{1,0:T(8,128)S(1)}, f32[16,128]{1,0:T(8,128)S(1)}) custom-call(f32[16,128]{1,0:T(8,128)S(1)} %shard_map.151.early, f32[16,128]{1,0:T(8,128)S(1)} %shard_map.152.late, f32[16,128]{1,0:T(8,128)S(1)} %get-tuple-element.19.edge, s32[12,16]{1,0:T(8,128)S(1)} %copy-done.7, bf16[8,2,488,128]{3,2,1,0:T(8,128)(2,1)S(1)} %get-tuple-element.14.refs_0_.form, ...), custom_call_target="tpu_custom_call" | custom-call | tf_op jit(solution)/shard_map/pallas_call | solution.py:525
  98.6 0.0 collective-permute-done.4
  98.6 0.0 collective-permute-done.5
  98.7 3.6 %collective-permute-start.7 = (f32[8,128]{1,0:T(8,128)S(1)}, f32[8,128]{1,0:T(8,128)S(1)}, u32[]{:S(2)}, u32[]{:S(2)}) collective-permute-start(f32[8,128]{1,0:T(8,128)S(1)} %get-tuple-element.30), channel_id=1, source_target_pairs={{32,0},{64,32},{96,64},{33,1},{65,33},{97,65},{34,2},{66,34},{98,6... | collective-permute-start | bytes 12296 | tf_op jit(solution)/shard_map/ppermute | solution.py:732
  102.3 2.2 %collective-permute-start.6 = (f32[8,128]{1,0:T(8,128)S(1)}, f32[8,128]{1,0:T(8,128)S(1)}, u32[]{:S(2)}, u32[]{:S(2)}) collective-permute-start(f32[8,128]{1,0:T(8,128)S(1)} %get-tuple-element.31), channel_id=1, source_target_pairs={{0,32},{32,64},{64,96},{1,33},{33,65},{65,97},{2,34},{34,66},{66,9... | collective-permute-start | bytes 12296 | tf_op jit(solution)/shard_map/ppermute | solution.py:732
  104.5 0.0 collective-permute-done.7.beneath
  104.5 3.3 %collective-permute-done.6.above = f32[8,128]{1,0:T(8,128)S(1)} collective-permute-done((f32[8,128]{1,0:T(8,128)S(1)}, f32[8,128]{1,0:T(8,128)S(1)}, u32[]{:S(2)}, u32[]{:S(2)}) %collective-permute-start.6) | collective-permute-done | bytes 4128 | tf_op jit(solution)/shard_map/ppermute | solution.py:732
  107.8 0.9 shard_map.155
  (6 shorter events, 0.1 us)
Async XLA Ops:
  41.3 25.7 %copy-start = (bf16[1280,128]{1,0:T(8,128)(2,1)S(1)}, bf16[1280,128]{1,0:T(8,128)(2,1)}, u32[]{:S(2)}) copy-start(bf16[1280,128]{1,0:T(8,128)(2,1)} %constant.22.clone.refs_6_.select) | copy-start | bytes 983044
  41.3 25.7 %copy-start.1 = (bf16[256,512]{1,0:T(8,128)(2,1)S(1)}, bf16[256,512]{1,0:T(8,128)(2,1)}, u32[]{:S(2)}) copy-start(bf16[256,512]{1,0:T(8,128)(2,1)} %constant.17.clone.refs_1_.first) | copy-start | bytes 786436
  41.3 25.7 %copy-start.2 = (bf16[320,208]{1,0:T(8,128)(2,1)S(1)}, bf16[320,208]{1,0:T(8,128)(2,1)}, u32[]{:S(2)}) copy-start(bf16[320,208]{1,0:T(8,128)(2,1)} %constant.18.clone.refs_2_.second) | copy-start | bytes 399364
  41.3 25.7 %copy-start.3 = (bf16[256,256]{1,0:T(8,128)(2,1)S(1)}, bf16[256,256]{1,0:T(8,128)(2,1)}, u32[]{:S(2)}) copy-start(bf16[256,256]{1,0:T(8,128)(2,1)} %constant.20.clone.refs_4_.mix_cols) | copy-start | bytes 393220
  41.3 25.7 %copy-start.4 = (bf16[256,128]{1,0:T(8,128)(2,1)S(1)}, bf16[256,128]{1,0:T(8,128)(2,1)}, u32[]{:S(2)}) copy-start(bf16[256,128]{1,0:T(8,128)(2,1)} %constant.23.clone.refs_7_.window) | copy-start | bytes 196612
  41.3 25.7 %copy-start.5 = (bf16[88,160]{1,0:T(8,128)(2,1)S(1)}, bf16[88,160]{1,0:T(8,128)(2,1)}, u32[]{:S(2)}) copy-start(bf16[88,160]{1,0:T(8,128)(2,1)} %constant.19.clone.refs_3_.mix_rows) | copy-start | bytes 84484
  41.3 25.7 %copy-start.6 = (bf16[16,256]{1,0:T(8,128)(2,1)S(1)}, bf16[16,256]{1,0:T(8,128)(2,1)}, u32[]{:S(2)}) copy-start(bf16[16,256]{1,0:T(8,128)(2,1)} %constant.21.clone.refs_5_.sign_cols) | copy-start | bytes 24580
  41.3 25.7 %copy-start.7 = (s32[12,16]{1,0:T(8,128)S(1)}, s32[12,16]{1,0:T(8,128)}, u32[]{:S(2)}) copy-start(s32[12,16]{1,0:T(8,128)} %valid.3) | copy-start | bytes 2308
  43.4 9.3 %collective-permute-start = (bf16[8,2,64,128]{3,2,1,0:T(8,128)(2,1)S(1)}, bf16[8,2,64,128]{3,2,1,0:T(8,128)(2,1)S(1)}, u32[]{:S(2)}, u32[]{:S(2)}) collective-permute-start(bf16[8,2,64,128]{3,2,1,0:T(8,128)(2,1)S(1)} %get-tuple-element.15), channel_id=1, source_target_pairs={{0,32},{32,64},{64,96},{1,33},{33,65},{65,97},{2,34},{34,66},{66,9... | collective-permute-start | bytes 786440 | tf_op jit(solution)/shard_map/ppermute | solution.py:732
  45.3 9.3 %collective-permute-start.1 = (bf16[8,2,64,128]{3,2,1,0:T(8,128)(2,1)S(1)}, bf16[8,2,64,128]{3,2,1,0:T(8,128)(2,1)S(1)}, u32[]{:S(2)}, u32[]{:S(2)}) collective-permute-start(bf16[8,2,64,128]{3,2,1,0:T(8,128)(2,1)S(1)} %get-tuple-element.16), channel_id=1, source_target_pairs={{32,0},{64,32},{96,64},{33,1},{65,33},{97,65},{34,2},{66,34},{98,6... | collective-permute-start | bytes 786440 | tf_op jit(solution)/shard_map/ppermute | solution.py:732
  54.7 6.3 %collective-permute-start.3 = (bf16[2,608,128]{2,1,0:T(8,128)(2,1)S(1)}, bf16[2,608,128]{2,1,0:T(8,128)(2,1)S(1)}, u32[]{:S(2)}, u32[]{:S(2)}) collective-permute-start(bf16[2,608,128]{2,1,0:T(8,128)(2,1)S(1)} %pad_add_fusion), channel_id=1, source_target_pairs={{1,0},{2,1},{3,2},{4,3},{5,4},{6,5},{7,6},{8,7},{9,8},{10,9},{11,1... | collective-permute-start | bytes 933896 | tf_op jit(solution)/shard_map/ppermute | solution.py:732
  56.7 10.3 %collective-permute-start.2 = (bf16[2,608,128]{2,1,0:T(8,128)(2,1)S(1)}, bf16[2,608,128]{2,1,0:T(8,128)(2,1)S(1)}, u32[]{:S(2)}, u32[]{:S(2)}) collective-permute-start(bf16[2,608,128]{2,1,0:T(8,128)(2,1)S(1)} %pad_add_fusion.1), channel_id=1, source_target_pairs={{0,1},{1,2},{2,3},{3,4},{4,5},{5,6},{6,7},{7,8},{8,9},{9,10},{10,1... | collective-permute-start | bytes 933896 | tf_op jit(solution)/shard_map/ppermute | solution.py:732
  78.4 20.2 %collective-permute-start.4 = (f32[16,128]{1,0:T(8,128)S(1)}, f32[16,128]{1,0:T(8,128)S(1)}, u32[]{:S(2)}, u32[]{:S(2)}) collective-permute-start(f32[16,128]{1,0:T(8,128)S(1)} %get-tuple-element.22), channel_id=1, source_target_pairs={{0,1},{1,2},{2,3},{3,4},{4,5},{5,6},{6,7},{7,8},{8,9},{9,10},{10,1... | collective-permute-start | bytes 24584 | tf_op jit(solution)/shard_map/ppermute | solution.py:732
  80.3 18.3 %collective-permute-start.5 = (f32[16,128]{1,0:T(8,128)S(1)}, f32[16,128]{1,0:T(8,128)S(1)}, u32[]{:S(2)}, u32[]{:S(2)}) collective-permute-start(f32[16,128]{1,0:T(8,128)S(1)} %get-tuple-element.23), channel_id=1, source_target_pairs={{1,0},{2,1},{3,2},{4,3},{5,4},{6,5},{7,6},{8,7},{9,8},{10,9},{11,1... | collective-permute-start | bytes 24584 | tf_op jit(solution)/shard_map/ppermute | solution.py:732
  98.7 5.9 %collective-permute-start.7 = (f32[8,128]{1,0:T(8,128)S(1)}, f32[8,128]{1,0:T(8,128)S(1)}, u32[]{:S(2)}, u32[]{:S(2)}) collective-permute-start(f32[8,128]{1,0:T(8,128)S(1)} %get-tuple-element.30), channel_id=1, source_target_pairs={{32,0},{64,32},{96,64},{33,1},{65,33},{97,65},{34,2},{66,34},{98,6... | collective-permute-start | bytes 12296 | tf_op jit(solution)/shard_map/ppermute | solution.py:732
  102.3 5.5 %collective-permute-start.6 = (f32[8,128]{1,0:T(8,128)S(1)}, f32[8,128]{1,0:T(8,128)S(1)}, u32[]{:S(2)}, u32[]{:S(2)}) collective-permute-start(f32[8,128]{1,0:T(8,128)S(1)} %get-tuple-element.31), channel_id=1, source_target_pairs={{0,32},{32,64},{64,96},{1,33},{33,65},{65,97},{2,34},{34,66},{66,9... | collective-permute-start | bytes 12296 | tf_op jit(solution)/shard_map/ppermute | solution.py:732
